TPU v7x, 32 devices: a whole 2x2x4 slice. The times are simulated.
32 devices in a mesh: fsdp: 4 (over x, core), ctx: 8 (over z, y).
Axes of the slice: x: 2, y: 2, z: 4, core: 2. Of those that a mesh axis runs over, the one named last changes fastest.
Arguments:
- tokens: bfloat16 [4, 2048, 1024], P('fsdp', 'ctx'), may hold values from -6 to 6
- out_grad: bfloat16 [4, 2048, 1024], P('fsdp', 'ctx'), may hold values from -6 to 6
- slot_block: int32 [4, 16], P('fsdp'), may hold values from 0 to 15, as said below
- w_attend: bfloat16 [1024, 3072], P('fsdp'), may hold values from -0.1875 to 0.1875
- w_mixing: bfloat16 [1024, 1024], P('fsdp'), may hold values from -1 to 1
- w_expand: bfloat16 [1024, 4096], P('fsdp'), may hold values from -0.1875 to 0.1875
- w_shrink: bfloat16 [4096, 1024], P('fsdp'), may hold values from -0.09375 to 0.09375
- w_norms: bfloat16 [4, 1024], P(None, 'fsdp'), may hold values from -1.2 to 1.4
- first_attend: float32 [1024, 3072], P('fsdp'), may hold values from -24 to 24
- first_mixing: float32 [1024, 1024], P('fsdp'), may hold values from -24 to 24
- first_expand: float32 [1024, 4096], P('fsdp'), may hold values from -24 to 24
- first_shrink: float32 [4096, 1024], P('fsdp'), may hold values from -24 to 24
- first_norms: float32 [4, 1024], P(None, 'fsdp'), may hold values from -24 to 24
- second_attend: float32 [1024, 3072], P('fsdp'), may hold values from 0.5 to 8
- second_mixing: float32 [1024, 1024], P('fsdp'), may hold values from 0.5 to 8
- second_expand: float32 [1024, 4096], P('fsdp'), may hold values from 0.5 to 8
- second_shrink: float32 [4096, 1024], P('fsdp'), may hold values from 0.5 to 8
- second_norms: float32 [4, 1024], P(None, 'fsdp'), may hold values from 0.5 to 8
Outputs:
- layer_out: bfloat16 [4, 2048, 1024], P('fsdp', 'ctx')
- tokens_grad: float32 [4, 2048, 1024], P('fsdp', 'ctx')
- grad_attend: float32 [1024, 3072], P('fsdp')
- update_attend: float32 [1024, 3072], P('fsdp')
- first_new_attend: float32 [1024, 3072], P('fsdp')
- second_new_attend: float32 [1024, 3072], P('fsdp')
- grad_mixing: float32 [1024, 1024], P('fsdp')
- update_mixing: float32 [1024, 1024], P('fsdp')
- first_new_mixing: float32 [1024, 1024], P('fsdp')
- second_new_mixing: float32 [1024, 1024], P('fsdp')
- grad_expand: float32 [1024, 4096], P('fsdp')
- update_expand: float32 [1024, 4096], P('fsdp')
- first_new_expand: float32 [1024, 4096], P('fsdp')
- second_new_expand: float32 [1024, 4096], P('fsdp')
- grad_shrink: float32 [4096, 1024], P('fsdp')
- update_shrink: float32 [4096, 1024], P('fsdp')
- first_new_shrink: float32 [4096, 1024], P('fsdp')
- second_new_shrink: float32 [4096, 1024], P('fsdp')
- grad_norms: float32 [4, 1024], P(None, 'fsdp')
- update_norms: float32 [4, 1024], P(None, 'fsdp')
- first_new_norms: float32 [4, 1024], P(None, 'fsdp')
- second_new_norms: float32 [4, 1024], P(None, 'fsdp')
Inputs may be any that keep to these rules, and one draw needn't show every extreme that they name: `slot_block`: in each row every block number appears once, and slots 2i and 2i+1 hold two blocks whose numbers add up to 15.
All inputs are finite; a program needn't handle non-finite values.
Results may differ from a plain program's by a relative error of at most 0.025.
Values may be sent and summed in bfloat16 or wider, within the bound.
A program may use at most 256 MiB of HBM per device.

v0:
```python
import math

import jax
import jax.numpy as jnp
from jax import lax
from jax.sharding import PartitionSpec as P

HD = 64
HGROUP = 2
STEP_COUNT = 10


EPS_NORM = 1e-05
NEG = -1e30
BETA_ONE = 0.9
BETA_TWO = 0.999
LEARN = 0.02
DECAY = 0.1
EPS_ADAM = 1e-08
CUBIC = 0.044715
ROOT_TWO_PI = math.sqrt(2.0 / math.pi)


def layer_norm(values, gain, shift):
    center = values - jnp.mean(values, axis=-1, keepdims=True)
    spread = jnp.mean(center * center, axis=-1, keepdims=True)
    return center * lax.rsqrt(spread + EPS_NORM) * gain + shift


def gelu(values):
    cube = values * values * values
    return 0.5 * values * (1.0 + jnp.tanh(ROOT_TWO_PI * (values + CUBIC * cube)))


def positions(slots, block):
    offsets = jnp.arange(block, dtype=jnp.int32)
    placed = slots[:, :, None] * block + offsets[None, None, :]
    return placed.reshape(slots.shape[0], slots.shape[1] * block)


def adam_step(weight, grad, first, second):
    first_new = BETA_ONE * first + (1.0 - BETA_ONE) * grad
    second_new = BETA_TWO * second + (1.0 - BETA_TWO) * grad * grad
    mean_hat = first_new / (1.0 - BETA_ONE**STEP_COUNT)
    square_hat = second_new / (1.0 - BETA_TWO**STEP_COUNT)
    update = -LEARN * (
        mean_hat / (jnp.sqrt(square_hat) + EPS_ADAM) + DECAY * weight.astype(jnp.float32)
    )
    return (update, first_new, second_new)


def shards(
    tokens,
    out_grad,
    slot_block,
    w_attend,
    w_mixing,
    w_expand,
    w_shrink,
    w_norms,
    first_attend,
    first_mixing,
    first_expand,
    first_shrink,
    first_norms,
    second_attend,
    second_mixing,
    second_expand,
    second_shrink,
    second_norms,
):
    whole_attend, whole_mixing, whole_expand, whole_shrink, whole_norms = (
        lax.all_gather(w_attend, "fsdp", axis=0, tiled=True),
        lax.all_gather(w_mixing, "fsdp", axis=0, tiled=True),
        lax.all_gather(w_expand, "fsdp", axis=0, tiled=True),
        lax.all_gather(w_shrink, "fsdp", axis=0, tiled=True),
        lax.all_gather(w_norms, "fsdp", axis=1, tiled=True),
    )
    seqs, local, width = tokens.shape
    block = local // 2
    length = slot_block.shape[1] * block
    total_rows = seqs * local
    heads = width // HD
    group_width = HGROUP * HD
    scale = 1.0 / math.sqrt(HD)
    norm_values = whole_norms.astype(jnp.float32)
    owned = lax.dynamic_slice_in_dim(slot_block, 2 * lax.axis_index("ctx"), 2, 1)
    query_place = positions(owned, block)
    key_place = positions(slot_block, block)
    allowed = key_place[:, None, None, :] <= query_place[:, None, :, None]
    start = tokens.reshape(total_rows, width).astype(jnp.float32)
    normed, norm_back = jax.vjp(layer_norm, start, norm_values[0], norm_values[1])
    normed_low = normed.astype(jnp.bfloat16)
    joint = jnp.dot(normed_low, whole_attend, preferred_element_type=jnp.float32).astype(
        jnp.bfloat16
    )
    query = joint[:, :width].reshape(seqs, local, width)
    keys_own = joint[:, width : 2 * width].reshape(seqs, local, width)
    values_own = joint[:, 2 * width :].reshape(seqs, local, width)
    keys, values = (
        lax.all_gather(keys_own, "ctx", axis=1, tiled=True),
        lax.all_gather(values_own, "ctx", axis=1, tiled=True),
    )

    def group_scores(index):
        offset = index * group_width
        query_group = lax.dynamic_slice_in_dim(query, offset, group_width, 2).reshape(
            seqs, local, HGROUP, HD
        )
        key_group = lax.dynamic_slice_in_dim(keys, offset, group_width, 2).reshape(
            seqs, length, HGROUP, HD
        )
        value_group = lax.dynamic_slice_in_dim(values, offset, group_width, 2).reshape(
            seqs, length, HGROUP, HD
        )
        raw = (
            jnp.einsum(
                "sqhd,skhd->shqk", query_group, key_group, preferred_element_type=jnp.float32
            )
            * scale
        )
        return (jnp.where(allowed, raw, NEG), query_group, key_group, value_group)

    def forward_group(index, state):
        mixed_buffer, totals_buffer = state
        masked, query_group, key_group, value_group = group_scores(index)
        top = jnp.max(masked, axis=-1, keepdims=True)
        total = top + jnp.log(jnp.sum(jnp.exp(masked - top), axis=-1, keepdims=True))
        probs = jnp.exp(masked - total).astype(jnp.bfloat16)
        result = jnp.einsum(
            "shqk,skhd->sqhd", probs, value_group, preferred_element_type=jnp.float32
        )
        result = result.reshape(seqs, local, group_width).astype(jnp.bfloat16)
        mixed_buffer = lax.dynamic_update_slice_in_dim(mixed_buffer, result, index * group_width, 2)
        totals_buffer = lax.dynamic_update_slice_in_dim(
            totals_buffer, total[..., 0], index * HGROUP, 1
        )
        return (mixed_buffer, totals_buffer)

    mixed, totals = lax.fori_loop(
        0,
        heads // HGROUP,
        forward_group,
        (
            jnp.zeros((seqs, local, width), jnp.bfloat16),
            jnp.zeros((seqs, heads, local), jnp.float32),
        ),
    )
    mixed_rows = mixed.reshape(total_rows, width)
    middle = start + jnp.dot(mixed_rows, whole_mixing, preferred_element_type=jnp.float32)
    normed_two, norm_two_back = jax.vjp(layer_norm, middle, norm_values[2], norm_values[3])
    normed_two_low = normed_two.astype(jnp.bfloat16)
    expanded = jnp.dot(normed_two_low, whole_expand, preferred_element_type=jnp.float32)
    activated, gelu_back = jax.vjp(gelu, expanded)
    activated_low = activated.astype(jnp.bfloat16)
    result_rows = middle + jnp.dot(activated_low, whole_shrink, preferred_element_type=jnp.float32)
    layer_out = result_rows.reshape(seqs, local, width).astype(jnp.bfloat16)
    incoming = out_grad.reshape(total_rows, width)
    grad_shrink = jnp.dot(activated_low.T, incoming, preferred_element_type=jnp.float32)
    grad_activated = jnp.dot(incoming, whole_shrink.T, preferred_element_type=jnp.float32).astype(
        jnp.bfloat16
    )
    grad_expanded = gelu_back(grad_activated.astype(jnp.float32))[0].astype(jnp.bfloat16)
    grad_expand = jnp.dot(normed_two_low.T, grad_expanded, preferred_element_type=jnp.float32)
    grad_normed_two = jnp.dot(grad_expanded, whole_expand.T, preferred_element_type=jnp.float32)
    grad_middle_norm, grad_gain_two, grad_shift_two = norm_two_back(grad_normed_two)
    grad_middle = incoming.astype(jnp.float32) + grad_middle_norm
    grad_branch = grad_middle.astype(jnp.bfloat16)
    grad_mixing = jnp.dot(mixed_rows.T, grad_branch, preferred_element_type=jnp.float32)
    grad_mixed = jnp.dot(grad_branch, whole_mixing.T, preferred_element_type=jnp.float32)
    grad_mixed = grad_mixed.astype(jnp.bfloat16).reshape(seqs, local, width)

    def backward_group(index, state):
        grad_query, grad_keys, grad_values = state
        offset = index * group_width
        masked, query_group, key_group, value_group = group_scores(index)
        total = lax.dynamic_slice_in_dim(totals, index * HGROUP, HGROUP, 1)
        probs = jnp.exp(masked - total[..., None])
        grad_group = lax.dynamic_slice_in_dim(grad_mixed, offset, group_width, 2).reshape(
            seqs, local, HGROUP, HD
        )
        grad_probs = jnp.einsum(
            "sqhd,skhd->shqk", grad_group, value_group, preferred_element_type=jnp.float32
        )
        grad_scores = probs * (grad_probs - jnp.sum(probs * grad_probs, axis=-1, keepdims=True))
        grad_scores = grad_scores.astype(jnp.bfloat16)
        part_query = (
            jnp.einsum(
                "shqk,skhd->sqhd", grad_scores, key_group, preferred_element_type=jnp.float32
            )
            * scale
        )
        part_keys = (
            jnp.einsum(
                "shqk,sqhd->skhd", grad_scores, query_group, preferred_element_type=jnp.float32
            )
            * scale
        )
        part_values = jnp.einsum(
            "shqk,sqhd->skhd",
            probs.astype(jnp.bfloat16),
            grad_group,
            preferred_element_type=jnp.float32,
        )
        grad_query = lax.dynamic_update_slice_in_dim(
            grad_query, part_query.reshape(seqs, local, group_width), offset, 2
        )
        grad_keys = lax.dynamic_update_slice_in_dim(
            grad_keys, part_keys.reshape(seqs, length, group_width), offset, 2
        )
        grad_values = lax.dynamic_update_slice_in_dim(
            grad_values, part_values.reshape(seqs, length, group_width), offset, 2
        )
        return (grad_query, grad_keys, grad_values)

    grad_query, grad_keys_all, grad_values_all = lax.fori_loop(
        0,
        heads // HGROUP,
        backward_group,
        (
            jnp.zeros((seqs, local, width), jnp.float32),
            jnp.zeros((seqs, length, width), jnp.float32),
            jnp.zeros((seqs, length, width), jnp.float32),
        ),
    )
    grad_keys, grad_values = (
        lax.psum_scatter(
            grad_keys_all.astype(jnp.bfloat16), "ctx", scatter_dimension=1, tiled=True
        ).astype(jnp.float32),
        lax.psum_scatter(
            grad_values_all.astype(jnp.bfloat16), "ctx", scatter_dimension=1, tiled=True
        ).astype(jnp.float32),
    )
    grad_joint = jnp.concatenate(
        [
            grad_query.astype(jnp.bfloat16),
            grad_keys.astype(jnp.bfloat16),
            grad_values.astype(jnp.bfloat16),
        ],
        axis=2,
    ).reshape(total_rows, 3 * width)
    grad_attend = jnp.dot(normed_low.T, grad_joint, preferred_element_type=jnp.float32)
    grad_normed = jnp.dot(grad_joint, whole_attend.T, preferred_element_type=jnp.float32)
    grad_start_norm, grad_gain_one, grad_shift_one = norm_back(grad_normed)
    tokens_grad = (grad_middle + grad_start_norm).reshape(seqs, local, width)
    grad_norms = jnp.stack([grad_gain_one, grad_shift_one, grad_gain_two, grad_shift_two])
    owned_attend, owned_mixing, owned_expand, owned_shrink, owned_norms = (
        lax.psum_scatter(
            grad_attend.astype(jnp.bfloat16), "fsdp", scatter_dimension=0, tiled=True
        ).astype(jnp.float32),
        lax.psum_scatter(
            grad_mixing.astype(jnp.bfloat16), "fsdp", scatter_dimension=0, tiled=True
        ).astype(jnp.float32),
        lax.psum_scatter(
            grad_expand.astype(jnp.bfloat16), "fsdp", scatter_dimension=0, tiled=True
        ).astype(jnp.float32),
        lax.psum_scatter(
            grad_shrink.astype(jnp.bfloat16), "fsdp", scatter_dimension=0, tiled=True
        ).astype(jnp.float32),
        lax.psum_scatter(
            grad_norms.astype(jnp.bfloat16), "fsdp", scatter_dimension=1, tiled=True
        ).astype(jnp.float32),
    )
    sum_attend, sum_mixing, sum_expand, sum_shrink, sum_norms = (
        lax.psum(owned_attend.astype(jnp.bfloat16), "ctx").astype(jnp.float32),
        lax.psum(owned_mixing.astype(jnp.bfloat16), "ctx").astype(jnp.float32),
        lax.psum(owned_expand.astype(jnp.bfloat16), "ctx").astype(jnp.float32),
        lax.psum(owned_shrink.astype(jnp.bfloat16), "ctx").astype(jnp.float32),
        lax.psum(owned_norms.astype(jnp.bfloat16), "ctx").astype(jnp.float32),
    )
    update_attend, first_new_attend, second_new_attend = adam_step(
        w_attend, sum_attend, first_attend, second_attend
    )
    update_mixing, first_new_mixing, second_new_mixing = adam_step(
        w_mixing, sum_mixing, first_mixing, second_mixing
    )
    update_expand, first_new_expand, second_new_expand = adam_step(
        w_expand, sum_expand, first_expand, second_expand
    )
    update_shrink, first_new_shrink, second_new_shrink = adam_step(
        w_shrink, sum_shrink, first_shrink, second_shrink
    )
    update_norms, first_new_norms, second_new_norms = adam_step(
        w_norms, sum_norms, first_norms, second_norms
    )
    return (
        layer_out,
        tokens_grad,
        sum_attend,
        update_attend,
        first_new_attend,
        second_new_attend,
        sum_mixing,
        update_mixing,
        first_new_mixing,
        second_new_mixing,
        sum_expand,
        update_expand,
        first_new_expand,
        second_new_expand,
        sum_shrink,
        update_shrink,
        first_new_shrink,
        second_new_shrink,
        sum_norms,
        update_norms,
        first_new_norms,
        second_new_norms,
    )


def solution(mesh):
    return jax.shard_map(
        shards,
        mesh=mesh,
        in_specs=(
            P("fsdp", "ctx", None),
            P("fsdp", "ctx", None),
            P("fsdp", None),
            P("fsdp", None),
            P("fsdp", None),
            P("fsdp", None),
            P("fsdp", None),
            P(None, "fsdp"),
            P("fsdp", None),
            P("fsdp", None),
            P("fsdp", None),
            P("fsdp", None),
            P(None, "fsdp"),
            P("fsdp", None),
            P("fsdp", None),
            P("fsdp", None),
            P("fsdp", None),
            P(None, "fsdp"),
        ),
        out_specs=(
            P("fsdp", "ctx", None),
            P("fsdp", "ctx", None),
            P("fsdp", None),
            P("fsdp", None),
            P("fsdp", None),
            P("fsdp", None),
            P("fsdp", None),
            P("fsdp", None),
            P("fsdp", None),
            P("fsdp", None),
            P("fsdp", None),
            P("fsdp", None),
            P("fsdp", None),
            P("fsdp", None),
            P("fsdp", None),
            P("fsdp", None),
            P("fsdp", None),
            P("fsdp", None),
            P(None, "fsdp"),
            P(None, "fsdp"),
            P(None, "fsdp"),
            P(None, "fsdp"),
        ),
        check_vma=False,
    )
```

profile of v0, /device:TPU:0, one launch (start us, length us, event | category | flops | bytes accessed | tf_op | source)
XLA Modules:
  0.0 1200.0 jit_solution(6608566212357250092)
XLA Ops:
  8.0 6.3 all_gather.21
  16.8 41.9 %all-gather.9.cloned.1.call-done = bf16[1024,3072]{1,0:T(8,128)(2,1)} async-done(((bf16[256,3072]{1,0:T(8,128)(2,1)}), bf16[1024,3072]{1,0:T(8,128)(2,1)}) %all-gather.9.cloned.1.call-update) | async-done | bytes 6291472 | tf_op jit(solution)/shard_map/all_gather | solution.py:73
  58.7 4.9 convolution_convert_fusion.4
  67.8 70.6 %all-gather.17.cloned.1.call-done = bf16[2048,1024]{1,0:T(8,128)(2,1)} async-done(((bf16[256,1024]{1,0:T(8,128)(2,1)}), bf16[2048,1024]{1,0:T(8,128)(2,1)}) %all-gather.17.cloned.1.call-update) | async-done | bytes 4194320 | tf_op jit(solution)/shard_map/all_gather | solution.py:102
  138.4 6.4 copy.47
  144.8 68.0 %all-gather.19.cloned.1.call-done = bf16[2048,1024]{1,0:T(8,128)(2,1)} async-done(((bf16[256,1024]{1,0:T(8,128)(2,1)}), bf16[2048,1024]{1,0:T(8,128)(2,1)}) %all-gather.19.cloned.1.call-update) | async-done | bytes 4194320 | tf_op jit(solution)/shard_map/all_gather | solution.py:101
  212.8 6.4 copy.49
  219.2 74.3 %while.34 = (s32[]{:T(128)}, bf16[1,256,1024]{1,2,0:T(8,128)(2,1)S(1)}, f32[1,16,256]{2,1,0:T(8,128)S(1)}, bf16[1,2048,1024]{1,2,0:T(8,128)(2,1)}, bf16[1,256,10...) while((s32[]{:T(128)}, ...), condition=%wide.region_5.6_spmd.clone, body=%wide.region_2.5_spmd.clone.sunk | while | flops 276332032 | bytes 33973524 | solution.py:140
  221.0 3.0 fusion.120
  224.1 3.1 exponential_reduce_fusion.2
  230.2 3.0 fusion.120
  233.2 3.1 exponential_reduce_fusion.2
  239.2 3.0 fusion.120
  242.3 3.6 exponential_reduce_fusion.2
  258.8 3.0 fusion.120
  270.9 3.1 exponential_reduce_fusion.2
  277.0 3.0 fusion.120
  286.2 3.0 fusion.120
  297.1 7.9 fusion.64
  305.0 49.5 %all-gather.15.cloned.1.call-done = bf16[4096,1024]{1,0:T(8,128)(2,1)} async-done(((bf16[1024,1024]{1,0:T(8,128)(2,1)}), bf16[4096,1024]{1,0:T(8,128)(2,1)}) %all-gather.15.cloned.1.call-update) | async-done | bytes 8388624 | tf_op jit(solution)/shard_map/all_gather | solution.py:76
  354.6 8.5 fusion.17
  374.8 120.1 %while.35 = (s32[]{:T(128)}, bf16[1,256,1024]{1,2,0:T(8,128)(2,1)}, bf16[1,2048,1024]{1,2,0:T(8,128)(2,1)}, bf16[1,2048,1024]{1,2,0:T(8,128)(2,1)}, bf16[1,2048,...) while((s32[]{:T(128)}, bf16[1,256,1024]{1,2,0:T(8,128)(2,1)}, ...), condition=%wide.region_12.13_spmd.clone, body=%wide.region_10.0_spmd.clone.sunk | while | flops 681639424 | bytes 56970552 | solution.py:216
  381.9 4.0 multiply_reduce_fusion.5
  396.9 4.0 multiply_reduce_fusion.5
  411.9 4.0 multiply_reduce_fusion.5
  426.9 4.0 multiply_reduce_fusion.5
  441.9 4.0 multiply_reduce_fusion.5
  457.0 4.0 multiply_reduce_fusion.5
  472.0 4.0 multiply_reduce_fusion.5
  487.0 4.0 multiply_reduce_fusion.5
  495.9 3.1 convolution_convert_fusion.5
  499.3 7.3 convolution_convert_fusion.1
  507.7 8.5 convolution_convert_fusion
  516.2 67.3 %reduce-scatter.12.cloned.1.call-done = bf16[1,256,1024]{1,2,0:T(8,128)(2,1)} async-done(((bf16[1,2048,1024]{1,2,0:T(8,128)(2,1)}), bf16[1,256,1024]{1,2,0:T(8,128)(2,1)}) %reduce-scatter.12.cloned.1.call-update) | async-done | bytes 524304 | tf_op jit(solution)/shard_map/reduce_scatter | solution.py:230
  583.6 92.9 %reduce-scatter.10.cloned.1.call-done = bf16[1,256,1024]{1,2,0:T(8,128)(2,1)} async-done(((bf16[1,2048,1024]{1,2,0:T(8,128)(2,1)}), bf16[1,256,1024]{1,2,0:T(8,128)(2,1)}) %reduce-scatter.10.cloned.1.call-update) | async-done | bytes 524304 | tf_op jit(solution)/shard_map/reduce_scatter | solution.py:227
  676.4 6.0 convolution_convert_fusion.2
  682.6 5.4 fusion.35
  690.8 19.9 %reduce-scatter.16.cloned.1.call-done = bf16[256,1024]{1,0:T(8,128)(2,1)} async-done(((bf16[1024,1024]{1,0:T(8,128)(2,1)}), bf16[256,1024]{1,0:T(8,128)(2,1)}) %reduce-scatter.16.cloned.1.call-update) | async-done | bytes 524304 | tf_op jit(solution)/shard_map/reduce_scatter | solution.py:251
  710.7 74.4 %reduce-scatter.18.cloned.1.call-done = bf16[256,4096]{1,0:T(8,128)(2,1)} async-done(((bf16[1024,4096]{1,0:T(8,128)(2,1)}), bf16[256,4096]{1,0:T(8,128)(2,1)}) %reduce-scatter.18.cloned.1.call-update) | async-done | bytes 2097168 | tf_op jit(solution)/shard_map/reduce_scatter | solution.py:254
  785.1 74.4 %reduce-scatter.20.cloned.1.call-done = bf16[1024,1024]{1,0:T(8,128)(2,1)} async-done(((bf16[4096,1024]{1,0:T(8,128)(2,1)}), bf16[1024,1024]{1,0:T(8,128)(2,1)}) %reduce-scatter.20.cloned.1.call-update) | async-done | bytes 2097168 | tf_op jit(solution)/shard_map/reduce_scatter | solution.py:257
  859.5 60.9 %reduce-scatter.14.cloned.1.call-done = bf16[256,3072]{1,0:T(8,128)(2,1)} async-done(((bf16[1024,3072]{1,0:T(8,128)(2,1)}), bf16[256,3072]{1,0:T(8,128)(2,1)}) %reduce-scatter.14.cloned.1.call-update) | async-done | bytes 1572880 | tf_op jit(solution)/shard_map/reduce_scatter | solution.py:248
  920.5 8.3 fusion.28
  930.3 13.3 %reduce-scatter.22.cloned.1.call-done = bf16[256,4]{1,0:T(8,128)(2,1)} async-done(((bf16[1024,4]{1,0:T(8,128)(2,1)}), bf16[256,4]{1,0:T(8,128)(2,1)}) %reduce-scatter.22.cloned.1.call-update) | async-done | bytes 2064
  944.5 21.9 %psum.39 = bf16[4,256]{1,0:T(4,128)(2,1)S(1)} all-reduce(bf16[4,256]{1,0:T(4,128)(2,1)S(1)} %copy.55), channel_id=1, replica_groups=mesh['fsdp'=4,'ctx'=8] {'ctx'}, use_global_device_ids=true, to_apply=%region_30.31 | all-reduce | flops 1024 | bytes 4096 | tf_op jit(solution)/shard_map/psum | solution.py:269
  967.0 196.3 %all-reduce.3.cloned.1.call-done = (bf16[256,3072]{1,0:T(8,128)(2,1)}, bf16[256,1024]{1,0:T(8,128)(2,1)}, bf16[256,4096]{1,0:T(8,128)(2,1)}, bf16[1024,1024]{1,0:T(8,128)(2,1)}) async-done(((bf16[256,3072]{1,0:T(8,128)(2,1)}, bf16[256,1024]{1,0:T(8,128)(2,1)}, bf16[256,4096]{1,0:T(8,128)(2,1)}, bf16[1024,1024]{1,0:T(8,128)(2,1)}), (bf16[256,3072]{1,0:T(8,128)(2,1)}, bf16[256,1024]{1,0:T(8,128)(2,1)}, ...) | async-done | bytes 6291472 | tf_op jit(solution)/shard_map/psum | solution.py:265
  1163.3 8.7 add_multiply_fusion.2
  1176.4 9.8 add_multiply_fusion.1
  1186.2 6.8 add_multiply_fusion
  (333 shorter events, 165.3 us)
Async XLA Ops:
  7.2 51.5 %all-gather.9.cloned.1.call-start = ((), (), s32[]{:S(2)}) async-start(), calls=%async_computation.7 | async-start | bytes 7864320 | tf_op jit(solution)/shard_map/all_gather | solution.py:73
  7.9 130.4 %all-gather.17.cloned.1.call-start = ((), (), s32[]{:S(2)}) async-start(), calls=%async_computation.17 | async-start | bytes 4718592 | tf_op jit(solution)/shard_map/all_gather | solution.py:102
  16.8 46.8 %copy-start.27 = (f32[256]{0:T(256)}, f32[256]{0:T(256)S(1)}, u32[]{:S(2)}) copy-start(f32[256]{0:T(256)S(1)} %fusion.34) | copy-start | bytes 3076
  63.6 3.7 copy-start.33
  64.7 148.0 %all-gather.19.cloned.1.call-start = ((), (), s32[]{:S(2)}) async-start(), calls=%async_computation.18 | async-start | bytes 4718592 | tf_op jit(solution)/shard_map/all_gather | solution.py:101
  65.5 228.1 %all-gather.11.cloned.1.call-start = ((), (), s32[]{:S(2)}) async-start(), calls=%async_computation.8 | async-start | bytes 2621440 | tf_op jit(solution)/shard_map/all_gather | solution.py:74
  66.1 231.0 %all-gather.13.cloned.1.call-start = ((), (), s32[]{:S(2)}) async-start(), calls=%async_computation.9 | async-start | bytes 10485760 | tf_op jit(solution)/shard_map/all_gather | solution.py:75
  66.6 287.9 %all-gather.15.cloned.1.call-start = ((), (), s32[]{:S(2)}) async-start(), calls=%async_computation.10 | async-start | bytes 10485760 | tf_op jit(solution)/shard_map/all_gather | solution.py:76
  67.2 516.3 %reduce-scatter.12.cloned.1.call-start = ((), (), s32[]{:S(2)}) async-start(), calls=%async_computation.12 | async-start | bytes 4718592 | tf_op jit(solution)/shard_map/reduce_scatter | solution.py:230
  219.2 75.1 %copy-start.2 = (bf16[1,256,1024]{2,1,0:T(8,128)(2,1)S(1)}, bf16[1,256,1024]{2,1,0:T(8,128)(2,1)}, u32[]{:S(2)}) copy-start(bf16[1,256,1024]{2,1,0:T(8,128)(2,1)} %param.22) | copy-start | bytes 1572868
  242.3 4.7 copy-start
  293.6 11.5 copy-start.6
  297.1 57.5 %copy-start.19 = (bf16[1,256,1024]{2,1,0:T(8,128)(2,1)S(1)}, bf16[1,256,1024]{2,1,0:T(8,128)(2,1)}, u32[]{:S(2)}) copy-start(bf16[1,256,1024]{2,1,0:T(8,128)(2,1)} %param.23) | copy-start | bytes 1572868
  354.6 8.5 copy-start.32
  367.3 7.4 copy-start.22
  381.9 4.0 copy-start.1
  396.9 4.0 copy-start.1
  411.9 4.0 copy-start.1
  426.9 4.0 copy-start.1
  441.9 4.0 copy-start.1
  456.9 4.0 copy-start.1
  472.0 4.0 copy-start.1
  487.0 4.0 copy-start.1
  494.9 181.5 %reduce-scatter.10.cloned.1.call-start = ((), (), s32[]{:S(2)}) async-start(), calls=%async_computation.11 | async-start | bytes 4718592 | tf_op jit(solution)/shard_map/reduce_scatter | solution.py:227
  495.7 215.1 %reduce-scatter.16.cloned.1.call-start = ((), (), s32[]{:S(2)}) async-start(), calls=%async_computation.14 | async-start | bytes 2621440 | tf_op jit(solution)/shard_map/reduce_scatter | solution.py:251
  499.0 286.1 %reduce-scatter.18.cloned.1.call-start = ((), (), s32[]{:S(2)}) async-start(), calls=%async_computation.15 | async-start | bytes 10485760 | tf_op jit(solution)/shard_map/reduce_scatter | solution.py:254
  506.6 352.8 %reduce-scatter.20.cloned.1.call-start = ((), (), s32[]{:S(2)}) async-start(), calls=%async_computation.16 | async-start | bytes 10485760 | tf_op jit(solution)/shard_map/reduce_scatter | solution.py:257
  516.2 160.3 %copy-start.26 = (bf16[1,256,1024]{1,2,0:T(8,128)(2,1)S(1)}, bf16[1,256,1024]{1,2,0:T(8,128)(2,1)}, u32[]{:S(2)}) copy-start(bf16[1,256,1024]{1,2,0:T(8,128)(2,1)} %get-tuple-element.320) | copy-start | bytes 1572868
  516.2 404.2 %reduce-scatter.14.cloned.1.call-start = ((), (), s32[]{:S(2)}) async-start(), calls=%async_computation.13 | async-start | bytes 7864320 | tf_op jit(solution)/shard_map/reduce_scatter | solution.py:248
  682.5 261.1 %reduce-scatter.22.cloned.1.call-start = ((), (), s32[]{:S(2)}) async-start(), calls=%async_computation.19 | async-start | bytes 327680
  682.5 5.5 copy-start.28
  690.5 472.8 %all-reduce.3.cloned.1.call-start = ((), (), s32[]{:S(2)}) async-start(), calls=%async_computation.20 | async-start | bytes 12582912 | tf_op jit(solution)/shard_map/psum | solution.py:265
  920.4 8.3 copy-start.13
  920.5 8.3 copy-start.21
  928.7 37.6 %copy-start.29 = (bf16[4,256]{1,0:T(4,128)(2,1)S(1)}, bf16[4,256]{1,0:T(4,128)(2,1)}, u32[]{:S(2)}) copy-start(bf16[4,256]{1,0:T(4,128)(2,1)} %param.29) | copy-start | bytes 6148
  928.7 37.6 %copy-start.30 = (f32[4,256]{1,0:T(4,128)S(1)}, f32[4,256]{1,0:T(4,128)}, u32[]{:S(2)}) copy-start(f32[4,256]{1,0:T(4,128)} %param.34) | copy-start | bytes 12292
  928.7 37.6 %copy-start.31 = (f32[4,256]{1,0:T(4,128)S(1)}, f32[4,256]{1,0:T(4,128)}, u32[]{:S(2)}) copy-start(f32[4,256]{1,0:T(4,128)} %param.39) | copy-start | bytes 12292
  928.8 234.5 %copy-start.5 = (bf16[256,3072]{1,0:T(8,128)(2,1)S(1)}, bf16[256,3072]{1,0:T(8,128)(2,1)}, u32[]{:S(2)}) copy-start(bf16[256,3072]{1,0:T(8,128)(2,1)} %param.25) | copy-start | bytes 4718596
  1163.3 8.7 copy-start.16
  1163.3 8.7 copy-start.23
  1163.3 8.7 copy-start.24
  1163.3 8.7 copy-start.25
  1163.3 11.2 copy-start.9
  1172.0 4.4 copy-start.8
  1176.4 9.9 copy-start.4
  1176.4 9.9 copy-start.10
  1176.4 9.9 copy-start.11
  1176.4 9.9 copy-start.15
  (14 other events, 35.1 us)
Sparse Core Ops, SparseCore 0:
  9.6 49.0 all-gather.8
  64.9 73.4 all-gather.16
  141.1 71.6 all-gather.18
  214.2 20.8 all-gather.10
  236.5 58.3 all-gather.12
  296.3 58.2 all-gather.14
  495.0 88.4 reduce-scatter.11
  588.2 88.1 reduce-scatter.9
  679.5 31.1 reduce-scatter.15
  713.3 71.7 reduce-scatter.17
  787.7 71.7 reduce-scatter.19
  862.0 58.3 reduce-scatter.13
  923.4 20.0 reduce-scatter.21
  948.5 214.7 all-reduce.2
where the time goes:
time: 1210 us; the launch traced here: 1200 us
  waiting for transfers between devices  833 us (69%)
  matrix products  166 us (14%)
  local copies, waits for them, and re-layouts  87.7 us (7%)
  other arithmetic  68.2 us (6%)
  blocking collectives  28.2 us (2%)
  between operations  14.8 us (1%)
    psum x1, waiting for transfers between devices, shards(): lax.psum(owned_attend.astype(jnp.bfloat16), 'ctx').astype(jnp.float32)  196 us
    reduce_scatter x1, waiting for transfers between devices, shards(): lax.psum_scatter(grad_keys_all.astype(jnp.bfloat16), 'ctx', scatter_dimen...  92.9 us
    reduce_scatter x1, waiting for transfers between devices, shards(): lax.psum_scatter(grad_expand.astype(jnp.bfloat16), 'fsdp', scatter_dimens...  74.4 us
    reduce_scatter x1, waiting for transfers between devices, shards(): lax.psum_scatter(grad_shrink.astype(jnp.bfloat16), 'fsdp', scatter_dimens...  74.4 us
    all_gather x1, waiting for transfers between devices, shards(): lax.all_gather(values_own, 'ctx', axis=1, tiled=True)  70.6 us
    all_gather x1, waiting for transfers between devices, shards(): lax.all_gather(keys_own, 'ctx', axis=1, tiled=True)  68 us
    reduce_scatter x1, waiting for transfers between devices, shards(): lax.psum_scatter(grad_values_all.astype(jnp.bfloat16), 'ctx', scatter_dim...  67.3 us
    reduce_scatter x1, waiting for transfers between devices, shards(): lax.psum_scatter(grad_attend.astype(jnp.bfloat16), 'fsdp', scatter_dimens...  60.9 us
  transfers between devices with their start and end apart: 14, of which 12 were waited for; matrix products, arithmetic and copies ran while one was open for 12% of the time, Pallas kernels for 0%

commit v1 on v0

v1 whole, which is shorter than its diff:
```python
import functools
import math

import jax
import jax.numpy as jnp
from jax import lax
from jax.experimental import pallas as pl
from jax.experimental.pallas import tpu as pltpu
from jax.sharding import PartitionSpec as P

HD = 64
STEP_COUNT = 10
EPS_NORM = 1e-05
NEG = -1e30
BETA_ONE = 0.9
BETA_TWO = 0.999
LEARN = 0.02
DECAY = 0.1
EPS_ADAM = 1e-08
CUBIC = 0.044715
ROOT_TWO_PI = math.sqrt(2.0 / math.pi)
LOG2E = math.log2(math.e)
TILE = 256
MESH = pl.DeviceIdType.MESH
F32 = jnp.float32
BF16 = jnp.bfloat16


def dot(left, right):
    return jnp.dot(left, right, preferred_element_type=F32)


def norm_parts(values):
    center = values - jnp.mean(values, axis=-1, keepdims=True)
    spread = jnp.mean(center * center, axis=-1, keepdims=True)
    inverse = lax.rsqrt(spread + EPS_NORM)
    return center * inverse, inverse


def norm_back(err, gain, normal, inverse):
    scaled = err * gain
    first = jnp.mean(scaled, axis=-1, keepdims=True)
    second = jnp.mean(scaled * normal, axis=-1, keepdims=True)
    return inverse * (scaled - first - normal * second)


def gelu_and_slope(values):
    square = values * values
    inner = ROOT_TWO_PI * values * (1.0 + CUBIC * square)
    tanh = jnp.tanh(inner)
    half = 0.5 * (1.0 + tanh)
    slope = half + 0.5 * values * (1.0 - tanh * tanh) * ROOT_TWO_PI * (
        1.0 + 3.0 * CUBIC * square
    )
    return values * half, slope


def adam_step(weight, grad, first, second):
    first_new = BETA_ONE * first + (1.0 - BETA_ONE) * grad
    second_new = BETA_TWO * second + (1.0 - BETA_TWO) * grad * grad
    mean_hat = first_new / (1.0 - BETA_ONE**STEP_COUNT)
    square_hat = second_new / (1.0 - BETA_TWO**STEP_COUNT)
    update = -LEARN * (
        mean_hat / (jnp.sqrt(square_hat) + EPS_ADAM) + DECAY * weight.astype(F32)
    )
    return (update, first_new, second_new)


def comm_call(kernel, out_shape, scratch, ident, operands, any_space=True):
    space = pl.ANY if any_space else pltpu.VMEM
    outs = jax.tree.map(lambda _: pl.BlockSpec(memory_space=space), out_shape)
    return pl.pallas_call(
        kernel,
        out_shape=out_shape,
        in_specs=[pl.BlockSpec(memory_space=space)] * len(operands),
        out_specs=outs,
        scratch_shapes=scratch,
        compiler_params=pltpu.CompilerParams(collective_id=ident, has_side_effects=True),
    )(*operands)


def remote(src, dst, send, recv, device):
    return pltpu.make_async_remote_copy(
        src_ref=src,
        dst_ref=dst,
        send_sem=send,
        recv_sem=recv,
        device_id=device,
        device_id_type=MESH,
    )


def fsdp_partners():
    f, c = lax.axis_index("fsdp"), lax.axis_index("ctx")
    x, k = f // 2, f % 2
    return f, c, x, k, x * 2 + 1 - k, (1 - x) * 2 + k


def greet(devices):
    barrier = pltpu.get_barrier_semaphore()
    for device in devices:
        pl.semaphore_signal(barrier, inc=1, device_id=device, device_id_type=MESH)
    pl.semaphore_wait(barrier, len(devices))


GATHER_CHUNKS = 4


def fsdp_gather_kernel(x_ref, o_ref, local_sem, send_sem, recv_sem):
    f, c, x, k, mate, across = fsdp_partners()
    mate_across = (1 - x) * 2 + 1 - k
    greet([(mate, c), (across, c)])
    rows = x_ref.shape[0]
    step = rows // GATHER_CHUNKS
    copies = []
    for t in range(GATHER_CHUNKS):
        part = pl.ds(t * step, step)
        copy = remote(
            x_ref.at[part],
            o_ref.at[f, part],
            send_sem.at[1, t],
            recv_sem.at[1, t],
            (across, c),
        )
        copy.start()
        copies.append(copy)
    near = remote(x_ref, o_ref.at[f], send_sem.at[0, 0], recv_sem.at[0, 0], (mate, c))
    near.start()
    local = pltpu.make_async_copy(x_ref, o_ref.at[f], local_sem)
    local.start()
    forwards = []
    for t in range(GATHER_CHUNKS):
        part = pl.ds(t * step, step)
        copies[t].wait_recv()
        forward = remote(
            o_ref.at[across, part],
            o_ref.at[across, part],
            send_sem.at[2, t],
            recv_sem.at[2, t],
            (mate, c),
        )
        forward.start()
        forwards.append(forward)
    local.wait()
    near.wait()
    for t in range(GATHER_CHUNKS):
        copies[t].wait_send()
        forwards[t].wait()


def fsdp_gather(values, ident, sizes):
    if sizes != (4, 8):
        return lax.all_gather(values, "fsdp", axis=0, tiled=False)
    return comm_call(
        fsdp_gather_kernel,
        jax.ShapeDtypeStruct((4,) + values.shape, values.dtype),
        [
            pltpu.SemaphoreType.DMA,
            pltpu.SemaphoreType.DMA((3, GATHER_CHUNKS)),
            pltpu.SemaphoreType.DMA((3, GATHER_CHUNKS)),
        ],
        ident,
        (values,),
    )


SCATTER_CHUNKS = 4


def fsdp_scatter_kernel(x_ref, o_ref, near_buf, far_out, far_in, send_sem, recv_sem):
    f, c, x, k, mate, across = fsdp_partners()
    greet([(mate, c), (across, c)])
    rows = x_ref.shape[1]
    step = rows // SCATTER_CHUNKS
    away = 1 - x
    near_far = []
    for t in range(SCATTER_CHUNKS):
        part = pl.ds(t * step, step)
        copy = remote(
            x_ref.at[away * 2 + 1 - k, part],
            near_buf.at[0, part],
            send_sem.at[0, t],
            recv_sem.at[0, t],
            (mate, c),
        )
        copy.start()
        near_far.append(copy)
    near_own = remote(
        x_ref.at[mate], near_buf.at[1], send_sem.at[2, 0], recv_sem.at[2, 0], (mate, c)
    )
    near_own.start()
    far = []
    for t in range(SCATTER_CHUNKS):
        part = pl.ds(t * step, step)
        near_far[t].wait_recv()
        far_out[part] = (
            x_ref[away * 2 + k, part].astype(F32) + near_buf[0, part].astype(F32)
        ).astype(BF16)
        copy = remote(
            far_out.at[part],
            far_in.at[part],
            send_sem.at[1, t],
            recv_sem.at[1, t],
            (across, c),
        )
        copy.start()
        far.append(copy)
    near_own.wait_recv()
    for t in range(SCATTER_CHUNKS):
        part = pl.ds(t * step, step)
        far[t].wait_recv()
        o_ref[part] = (
            x_ref[f, part].astype(F32)
            + near_buf[1, part].astype(F32)
            + far_in[part].astype(F32)
        )
    near_own.wait_send()
    for t in range(SCATTER_CHUNKS):
        near_far[t].wait_send()
        far[t].wait_send()


def fsdp_scatter(values, ident, sizes):
    if sizes != (4, 8):
        return lax.psum_scatter(
            values.astype(BF16), "fsdp", scatter_dimension=0, tiled=False
        ).astype(F32)
    rows, width = values.shape[1:]
    return comm_call(
        fsdp_scatter_kernel,
        jax.ShapeDtypeStruct((rows, width), F32),
        [
            pltpu.VMEM((2, rows, width), BF16),
            pltpu.VMEM((rows, width), BF16),
            pltpu.VMEM((rows, width), BF16),
            pltpu.SemaphoreType.DMA((3, SCATTER_CHUNKS)),
            pltpu.SemaphoreType.DMA((3, SCATTER_CHUNKS)),
        ],
        ident,
        (values,),
        any_space=False,
    )


def ctx_exchange_kernel(n, x_ref, o_ref, local_sem, send_sem, recv_sem):
    f, c = lax.axis_index("fsdp"), lax.axis_index("ctx")
    greet([(f, (c + j) % n) for j in range(1, n)])
    copies = []
    for j in range(n - 1, 0, -1):
        there = (c + j) % n
        copy = remote(
            x_ref.at[there], o_ref.at[c], send_sem.at[j], recv_sem.at[j], (f, there)
        )
        copy.start()
        copies.append(copy)
    local = pltpu.make_async_copy(x_ref.at[c], o_ref.at[c], local_sem)
    local.start()
    local.wait()
    for copy in copies:
        copy.wait()


def ctx_exchange(values, ident, sizes):
    if sizes != (4, 8):
        return lax.all_to_all(values, "ctx", split_axis=0, concat_axis=0, tiled=True)
    n = sizes[1]
    return comm_call(
        functools.partial(ctx_exchange_kernel, n),
        jax.ShapeDtypeStruct(values.shape, values.dtype),
        [
            pltpu.SemaphoreType.DMA,
            pltpu.SemaphoreType.DMA((n,)),
            pltpu.SemaphoreType.DMA((n,)),
        ],
        ident,
        (values,),
    )


def ctx_gather_kernel(cut, x_ref, o_ref, local_sem, send_sem, recv_sem):
    f, c = lax.axis_index("fsdp"), lax.axis_index("ctx")
    z, y = c // 2, c % 2
    depth = lax.axis_size("ctx") // 2
    rows = x_ref.shape[0]
    parts = (pl.ds(0, cut), pl.ds(cut, rows - cut))
    mate = z * 2 + 1 - y
    barrier = pltpu.get_barrier_semaphore()

    def signal(device):
        pl.semaphore_signal(barrier, inc=1, device_id=device, device_id_type=MESH)

    signal((f, mate))
    pl.when(z > 0)(lambda: signal((f, c - 2)))
    pl.when(z < depth - 1)(lambda: signal((f, c + 2)))
    pl.semaphore_wait(barrier, 1 + (z + depth - 1) // depth + (2 * depth - 2 - z) // depth)

    def copy(zz, yy, part, way, own=False):
        block = zz * 2 + yy
        src = x_ref.at[parts[part]] if own else o_ref.at[block, parts[part]]
        there = (c - 2, c + 2, mate)[way]
        return remote(
            src,
            o_ref.at[block, parts[part]],
            send_sem.at[block, part, way],
            recv_sem.at[block, part],
            (f, there),
        )

    local = pltpu.make_async_copy(x_ref, o_ref.at[c], local_sem)
    local.start()
    for part in (0, 1):
        pl.when(z < depth - 1)(lambda: copy(z, y, part, 1, True).start())
        pl.when(z > 0)(lambda: copy(z, y, part, 0, True).start())
    for part in (1, 0):
        copy(z, y, part, 2, True).start()
    local.wait()

    def arrive(zz, yy, part, way):
        copy(zz, yy, part, way).wait_recv()
        if way == 1:
            pl.when(z < depth - 1)(lambda: copy(zz, yy, part, 1).start())
        else:
            pl.when(z > 0)(lambda: copy(zz, yy, part, 0).start())
        if part == 0:
            copy(zz, yy, part, 2).start()

    def from_mate_second():
        copy(z, 1 - y, 1, 2).wait_recv()
        pl.when(z < depth - 1)(lambda: copy(z, 1 - y, 1, 1).start())
        pl.when(z > 0)(lambda: copy(z, 1 - y, 1, 0).start())

    def along(step, yy, part):
        pl.when(z - step >= 0)(lambda: arrive(z - step, yy, part, 1))
        pl.when(z + step < depth)(lambda: arrive(z + step, yy, part, 0))

    for step in range(1, depth):
        along(step, y, 0)
        along(step, y, 1)
        if step == 1:
            from_mate_second()
        along(step, 1 - y, 1)
    copy(z, 1 - y, 0, 2).wait_recv()
    for step in range(1, depth):
        pl.when(z - step >= 0)(lambda: copy(z - step, 1 - y, 0, 2).wait_recv())
        pl.when(z + step < depth)(lambda: copy(z + step, 1 - y, 0, 2).wait_recv())
    for step in range(depth):
        for yy, part in ((y, 0), (y, 1), (1 - y, 1)):

            def sent_right():
                copy(z - step, yy, part, 1).wait_send()

            def sent_left():
                copy(z + step, yy, part, 0).wait_send()

            pl.when((z - step >= 0) & (z < depth - 1))(sent_right)
            pl.when((z + step < depth) & (z > 0))(sent_left)
    copy(z, y, 0, 2).wait_send()
    copy(z, y, 1, 2).wait_send()
    for step in range(1, depth):
        pl.when(z - step >= 0)(lambda: copy(z - step, y, 0, 2).wait_send())
        pl.when(z + step < depth)(lambda: copy(z + step, y, 0, 2).wait_send())


def ctx_gather(values, ident, sizes):
    if sizes != (4, 8):
        return lax.all_gather(values, "ctx", axis=0, tiled=False)
    n = sizes[1]
    rows = values.shape[0]
    cut = rows * 5 // 8
    return comm_call(
        functools.partial(ctx_gather_kernel, cut),
        jax.ShapeDtypeStruct((n,) + values.shape, values.dtype),
        [
            pltpu.SemaphoreType.DMA,
            pltpu.SemaphoreType.DMA((n, 2, 3)),
            pltpu.SemaphoreType.DMA((n, 2)),
        ],
        ident,
        (values,),
    )


def head_rows(h):
    return slice(h * HD, (h + 1) * HD)


def attend_forward_kernel(
    heads, slot_ref, place_ref, qkv_ref, mixed_ref, out_t_ref, total_ref,
    q_pos, k_pos, v_pos, q_t, v_t, scores, o_pos,
):
    length, lanes = q_pos.shape
    blocks = slot_ref.shape[0]
    size = length // blocks
    tiles = length // TILE
    factor = LOG2E / math.sqrt(HD)
    for p in range(blocks):
        rows = qkv_ref[pl.ds(slot_ref[p] * size, size), :]
        here = slice(p * size, (p + 1) * size)
        q_pos[here, :] = rows[:, :lanes]
        k_pos[here, :] = rows[:, lanes : 2 * lanes]
        v_pos[here, :] = rows[:, 2 * lanes :]
    for t in range(tiles):
        here = slice(t * TILE, (t + 1) * TILE)
        q_t[:, here] = q_pos[here, :].T
        v_t[:, here] = v_pos[here, :].T
    head_of_row = lax.broadcasted_iota(jnp.int32, (lanes, TILE), 0) // HD
    allowed = lax.broadcasted_iota(jnp.int32, (TILE, TILE), 0) <= lax.broadcasted_iota(
        jnp.int32, (TILE, TILE), 1
    )

    def fold_max(values):
        return jnp.max(values.reshape(TILE // 8, 8, TILE), axis=0)

    def fold_sum(values):
        return jnp.sum(values.reshape(TILE // 8, 8, TILE), axis=0)

    @pl.loop(0, tiles)
    def _(i):
        here = pl.ds(pl.multiple_of(i * TILE, TILE), TILE)
        q_tile = q_t[:, here]
        q_heads = [
            jnp.where(head_of_row == h, q_tile, jnp.zeros_like(q_tile)) for h in range(heads)
        ]

        def first(j, tops):
            there = pl.ds(pl.multiple_of(j * TILE, TILE), TILE)
            keys = k_pos[there, :]
            result = []
            for h in range(heads):
                raw = dot(keys, q_heads[h])
                scores[h, there, :] = raw
                result.append(jnp.maximum(tops[h], fold_max(raw)))
            return tuple(result)

        tops = lax.fori_loop(
            0, i, first, tuple(jnp.full((8, TILE), NEG, F32) for _ in range(heads))
        )
        keys = k_pos[here, :]
        row_tops = []
        for h in range(heads):
            raw = jnp.where(allowed, dot(keys, q_heads[h]), NEG)
            scores[h, here, :] = raw
            row_tops.append(
                jnp.max(jnp.maximum(tops[h], fold_max(raw)), axis=0, keepdims=True) * factor
            )

        def second(j, state):
            there = pl.ds(pl.multiple_of(j * TILE, TILE), TILE)
            result = []
            for h in range(heads):
                sums, acc = state[h]
                probs = jnp.exp2(scores[h, there, :] * factor - row_tops[h])
                acc = acc + dot(v_t[head_rows(h), there], probs.astype(BF16))
                result.append((sums + fold_sum(probs), acc))
            return tuple(result)

        state = lax.fori_loop(
            0,
            i + 1,
            second,
            tuple(
                (jnp.zeros((8, TILE), F32), jnp.zeros((HD, TILE), F32)) for _ in range(heads)
            ),
        )
        outs = []
        for h in range(heads):
            sums, acc = state[h]
            row_sum = jnp.sum(sums, axis=0, keepdims=True)
            out = acc * (1.0 / row_sum)
            out_t_ref[head_rows(h), here] = out
            total_ref[pl.ds(h, 1), here] = row_tops[h] + jnp.log2(row_sum)
            outs.append(out)
        out = jnp.concatenate(outs, axis=0) if heads > 1 else outs[0]
        o_pos[here, :] = out.T.astype(BF16)

    for s in range(blocks):
        mixed_ref[s * size : (s + 1) * size, :] = o_pos[
            pl.ds(place_ref[s] * size, size), :
        ]


def attend_forward(slot_of, place_of, qkv, heads):
    length = qkv.shape[0]
    lanes = heads * HD
    vmem = pl.BlockSpec(memory_space=pltpu.VMEM)
    smem = pl.BlockSpec(memory_space=pltpu.SMEM)
    return pl.pallas_call(
        functools.partial(attend_forward_kernel, heads),
        out_shape=(
            jax.ShapeDtypeStruct((length, lanes), BF16),
            jax.ShapeDtypeStruct((lanes, length), F32),
            jax.ShapeDtypeStruct((8, length), F32),
        ),
        in_specs=[smem, smem, vmem],
        out_specs=(vmem, vmem, vmem),
        scratch_shapes=[pltpu.VMEM((length, lanes), BF16)] * 3
        + [pltpu.VMEM((lanes, length), BF16)] * 2
        + [pltpu.VMEM((heads, length, TILE), F32), pltpu.VMEM((length, lanes), BF16)],
        cost_estimate=pl.CostEstimate(
            flops=4 * length * length * lanes,
            bytes_accessed=10 * length * lanes,
            transcendentals=heads * length * length // 2,
        ),
    )(slot_of, place_of, qkv)


def attend_backward_kernel(
    heads, slot_ref, place_ref, qkv_ref, grad_ref, out_t_ref, total_ref, result_ref,
    q_pos, k_pos, v_pos, g_pos, k_heads, v_heads, q_t, k_t, g_t, delta,
    dq_t, dk_acc, dv_acc, d_pos,
):
    length, lanes = q_pos.shape
    blocks = slot_ref.shape[0]
    size = length // blocks
    tiles = length // TILE
    scale = 1.0 / math.sqrt(HD)
    factor = LOG2E * scale
    for p in range(blocks):
        rows = qkv_ref[pl.ds(slot_ref[p] * size, size), :]
        here = slice(p * size, (p + 1) * size)
        q_pos[here, :] = rows[:, :lanes]
        k_pos[here, :] = rows[:, lanes : 2 * lanes]
        v_pos[here, :] = rows[:, 2 * lanes :]
        g_pos[here, :] = grad_ref[pl.ds(slot_ref[p] * size, size), :]
    head_of_lane = lax.broadcasted_iota(jnp.int32, (TILE, lanes), 1) // HD
    allowed = lax.broadcasted_iota(jnp.int32, (TILE, TILE), 0) <= lax.broadcasted_iota(
        jnp.int32, (TILE, TILE), 1
    )
    for t in range(tiles):
        here = slice(t * TILE, (t + 1) * TILE)
        q_t[:, here] = q_pos[here, :].T
        k_t[:, here] = k_pos[here, :].T
        g_tile = g_pos[here, :].T
        g_t[:, here] = g_tile
        product = g_tile.astype(F32) * out_t_ref[:, here]
        for h in range(heads):
            delta[h : h + 1, here] = jnp.sum(product[head_rows(h)], axis=0, keepdims=True)
            keys, values = k_pos[here, :], v_pos[here, :]
            k_heads[h, here, :] = jnp.where(head_of_lane == h, keys, jnp.zeros_like(keys))
            v_heads[h, here, :] = jnp.where(head_of_lane == h, values, jnp.zeros_like(values))
    dq_t[...] = jnp.zeros_like(dq_t)

    def pair(j, i, masked):
        there = pl.ds(pl.multiple_of(j * TILE, TILE), TILE)
        here = pl.ds(pl.multiple_of(i * TILE, TILE), TILE)
        for h in range(heads):
            raw = dot(k_heads[h, there, :], q_t[:, here])
            probs = jnp.exp2(raw * factor - total_ref[pl.ds(h, 1), here])
            if masked:
                probs = jnp.where(allowed, probs, 0.0)
            d_probs = dot(v_heads[h, there, :], g_t[:, here])
            d_scores = (probs * (d_probs - delta[pl.ds(h, 1), here])).astype(BF16)
            dv = dot(probs.astype(BF16), g_pos[here, :])
            dk = dot(d_scores, q_pos[here, :])
            if masked:
                dv_acc[h], dk_acc[h] = dv, dk
            else:
                dv_acc[h] += dv
                dk_acc[h] += dk
            dq_t[head_rows(h), here] += dot(k_t[head_rows(h), there], d_scores)

    @pl.loop(0, tiles)
    def _(j):
        pair(j, j, True)

        @pl.loop(j + 1, tiles)
        def _(i):
            pair(j, i, False)

        there = pl.ds(pl.multiple_of(j * TILE, TILE), TILE)
        for index, acc, weight in ((1, dk_acc, scale), (2, dv_acc, 1.0)):
            value = acc[0]
            for h in range(1, heads):
                value = jnp.where(head_of_lane == h, acc[h], value)
            d_pos[there, index * lanes : (index + 1) * lanes] = (value * weight).astype(BF16)

    for t in range(tiles):
        here = slice(t * TILE, (t + 1) * TILE)
        d_pos[here, :lanes] = (dq_t[:, here].T * scale).astype(BF16)
    for s in range(blocks):
        result_ref[s * size : (s + 1) * size, :] = d_pos[pl.ds(place_ref[s] * size, size), :]


def attend_backward(slot_of, place_of, qkv, grad, out_t, total, heads):
    length = qkv.shape[0]
    lanes = heads * HD
    vmem = pl.BlockSpec(memory_space=pltpu.VMEM)
    smem = pl.BlockSpec(memory_space=pltpu.SMEM)
    rows = pltpu.VMEM((length, lanes), BF16)
    columns = pltpu.VMEM((lanes, length), BF16)
    by_head = pltpu.VMEM((heads, length, lanes), BF16)
    return pl.pallas_call(
        functools.partial(attend_backward_kernel, heads),
        out_shape=jax.ShapeDtypeStruct((length, 3 * lanes), BF16),
        in_specs=[smem, smem, vmem, vmem, vmem, vmem],
        out_specs=vmem,
        scratch_shapes=[rows] * 4
        + [by_head] * 2
        + [columns] * 3
        + [
            pltpu.VMEM((8, length), F32),
            pltpu.VMEM((lanes, length), F32),
            pltpu.VMEM((heads, TILE, lanes), F32),
            pltpu.VMEM((heads, TILE, lanes), F32),
            pltpu.VMEM((length, 3 * lanes), BF16),
        ],
        cost_estimate=pl.CostEstimate(
            flops=10 * length * length * lanes,
            bytes_accessed=20 * length * lanes,
            transcendentals=heads * length * length // 2,
        ),
    )(slot_of, place_of, qkv, grad, out_t, total)


def shards(
    sizes,
    tokens,
    out_grad,
    slot_block,
    w_attend,
    w_mixing,
    w_expand,
    w_shrink,
    w_norms,
    first_attend,
    first_mixing,
    first_expand,
    first_shrink,
    first_norms,
    second_attend,
    second_mixing,
    second_expand,
    second_shrink,
    second_norms,
):
    fsdp, ctx = sizes
    f, c = lax.axis_index("fsdp"), lax.axis_index("ctx")
    rows, width = tokens.shape[1:]
    heads = width // HD // ctx
    lanes = heads * HD
    length = rows * ctx
    own = width // fsdp
    hidden = w_shrink.shape[0]

    place_of = slot_block[0]
    slot_of = jnp.sum(
        jnp.where(
            place_of[None, :] == jnp.arange(2 * ctx, dtype=jnp.int32)[:, None],
            jnp.arange(2 * ctx, dtype=jnp.int32)[None, :],
            0,
        ),
        axis=1,
    )

    start = tokens[0]
    incoming = out_grad[0]
    attend_grouped = (
        w_attend.reshape(own, 3, ctx, lanes).transpose(0, 2, 1, 3).reshape(own, ctx, 3 * lanes)
    )
    attend_here = lax.dynamic_index_in_dim(attend_grouped, c, 1, keepdims=False)
    norms = lax.all_gather(w_norms, "fsdp", axis=1, tiled=True).astype(F32)
    whole_tokens = ctx_gather(start, 0, sizes).reshape(length, width)
    whole_here = fsdp_gather(attend_here, 1, sizes).reshape(width, 3 * lanes)
    whole_attend = lax.all_gather(
        attend_grouped.reshape(own, 3 * width), "fsdp", axis=0, tiled=True
    )
    whole_mixing = lax.all_gather(w_mixing, "fsdp", axis=0, tiled=True)
    expand_columns = lax.all_to_all(
        w_expand.reshape(own, fsdp, hidden).transpose(1, 0, 2),
        "fsdp",
        split_axis=0,
        concat_axis=0,
        tiled=True,
    ).reshape(width, hidden)
    grads_in = lax.all_gather(incoming, "fsdp", axis=0, tiled=True)

    normed_all = (norm_parts(whole_tokens.astype(F32))[0] * norms[0] + norms[1]).astype(BF16)
    qkv = dot(normed_all, whole_here).astype(BF16)
    mixed_heads, out_t, total = attend_forward(slot_of, place_of, qkv, heads)
    mixed = ctx_exchange(mixed_heads.reshape(ctx, rows, lanes), 2, sizes)
    mixed = mixed.transpose(1, 0, 2).reshape(rows, width)

    middle = start.astype(F32) + dot(mixed, whole_mixing)
    normal_two, inverse_two = norm_parts(middle)
    normed_two = (normal_two * norms[2] + norms[3]).astype(BF16)
    normed_two_all = fsdp_gather(normed_two, 3, sizes).reshape(fsdp * rows, width)
    expanded = dot(normed_two_all, expand_columns)
    grad_activated = (
        lax.dot_general(
            grads_in, w_shrink, (((1,), (1,)), ((), ())), preferred_element_type=F32
        )
        .astype(BF16)
        .astype(F32)
    )
    activated, slope = gelu_and_slope(expanded)
    activated = activated.astype(BF16)
    grad_expanded = (grad_activated * slope).astype(BF16)
    part_normed_two = lax.dot_general(
        grad_expanded, expand_columns, (((1,), (1,)), ((), ())), preferred_element_type=F32
    ).astype(BF16)
    part_out = dot(activated, w_shrink).astype(BF16)
    grad_normed_two = fsdp_scatter(part_normed_two.reshape(fsdp, rows, width), 4, sizes)
    layer_out = (
        middle + fsdp_scatter(part_out.reshape(fsdp, rows, width), 5, sizes)
    ).astype(BF16)
    grad_shrink = lax.dot_general(
        activated, grads_in, (((0,), (0,)), ((), ())), preferred_element_type=F32
    ).astype(BF16)
    grad_expand = lax.dot_general(
        normed_two_all, grad_expanded, (((0,), (0,)), ((), ())), preferred_element_type=F32
    ).astype(BF16)

    grad_middle = incoming.astype(F32) + norm_back(
        grad_normed_two, norms[2], normal_two, inverse_two
    )
    grad_branch = grad_middle.astype(BF16)
    grad_mixing = lax.dot_general(
        mixed, grad_branch, (((0,), (0,)), ((), ())), preferred_element_type=F32
    ).astype(BF16)
    grad_mixed = lax.dot_general(
        grad_branch, whole_mixing, (((1,), (1,)), ((), ())), preferred_element_type=F32
    ).astype(BF16)
    grad_heads = ctx_exchange(
        grad_mixed.reshape(rows, ctx, lanes).transpose(1, 0, 2), 2, sizes
    ).reshape(length, lanes)
    d_qkv = attend_backward(slot_of, place_of, qkv, grad_heads, out_t, total, heads)
    grad_joint = (
        ctx_exchange(d_qkv.reshape(ctx, rows, 3 * lanes), 6, sizes)
        .transpose(1, 0, 2)
        .reshape(rows, 3 * width)
    )
    grad_normed = lax.dot_general(
        grad_joint, whole_attend, (((1,), (1,)), ((), ())), preferred_element_type=F32
    )
    normal_one, inverse_one = norm_parts(start.astype(F32))
    tokens_grad = (
        grad_middle + norm_back(grad_normed, norms[0], normal_one, inverse_one)
    )[None]
    grad_norms = jnp.stack(
        [
            jnp.sum(grad_normed * normal_one, axis=0),
            jnp.sum(grad_normed, axis=0),
            jnp.sum(grad_normed_two * normal_two, axis=0),
            jnp.sum(grad_normed_two, axis=0),
        ]
    )
    sum_norms = lax.dynamic_slice_in_dim(
        lax.psum(grad_norms, ("fsdp", "ctx")), f * own, own, 1
    )

    part_attend = lax.dot_general(
        normed_all, d_qkv, (((0,), (0,)), ((), ())), preferred_element_type=F32
    ).astype(BF16)
    own_attend = fsdp_scatter(part_attend.reshape(fsdp, own, 3 * lanes), 7, sizes).astype(BF16)
    sum_attend = (
        lax.all_gather(own_attend, "ctx", axis=0, tiled=False)
        .reshape(ctx, own, 3, lanes)
        .transpose(1, 2, 0, 3)
        .reshape(own, 3 * width)
        .astype(F32)
    )

    own_mixing = lax.psum_scatter(grad_mixing, "fsdp", scatter_dimension=0, tiled=True)
    piece = own // ctx
    shrink_piece = hidden // ctx
    stacked = jnp.concatenate(
        [
            grad_shrink.reshape(ctx, shrink_piece, width),
            grad_expand.reshape(fsdp, ctx, piece, hidden)
            .transpose(1, 0, 2, 3)
            .reshape(ctx, fsdp * piece * hidden // width, width),
            own_mixing.reshape(ctx, piece, width),
        ],
        axis=1,
    )
    stacked = lax.psum_scatter(stacked, "ctx", scatter_dimension=0, tiled=False)
    expand_rows = fsdp * piece * hidden // width
    expand_piece = lax.all_to_all(
        stacked[shrink_piece : shrink_piece + expand_rows].reshape(fsdp, piece, hidden),
        "fsdp",
        split_axis=0,
        concat_axis=0,
        tiled=True,
    )
    expand_piece = expand_piece.transpose(1, 0, 2).reshape(expand_rows, width)
    stacked = jnp.concatenate(
        [stacked[:shrink_piece], expand_piece, stacked[shrink_piece + expand_rows :]], axis=0
    )
    stacked = lax.all_gather(stacked, "ctx", axis=0, tiled=False)
    sum_shrink = stacked[:, :shrink_piece].reshape(hidden, width).astype(F32)
    sum_expand = (
        stacked[:, shrink_piece : shrink_piece + expand_rows]
        .reshape(own, fsdp * hidden)
        .astype(F32)
    )
    sum_mixing = stacked[:, shrink_piece + expand_rows :].reshape(own, width).astype(F32)

    result = [layer_out[None], tokens_grad]
    for weight, grad, first, second in (
        (w_attend, sum_attend, first_attend, second_attend),
        (w_mixing, sum_mixing, first_mixing, second_mixing),
        (w_expand, sum_expand, first_expand, second_expand),
        (w_shrink, sum_shrink, first_shrink, second_shrink),
        (w_norms, sum_norms, first_norms, second_norms),
    ):
        result.append(grad)
        result.extend(adam_step(weight, grad, first, second))
    return tuple(result)


def solution(mesh):
    rows = P("fsdp", None)
    columns = P(None, "fsdp")
    tokens = P("fsdp", "ctx", None)
    return jax.shard_map(
        functools.partial(shards, (mesh.shape["fsdp"], mesh.shape["ctx"])),
        mesh=mesh,
        in_specs=(tokens, tokens, rows)
        + (rows, rows, rows, rows, columns) * 3,
        out_specs=(tokens, tokens) + (rows,) * 16 + (columns,) * 4,
        check_vma=False,
    )
```

time: 1210 us -> 621 us (0.51)
  waiting for transfers between devices: 833 us -> 98.1 us
  Pallas kernels: 0 us -> 279 us
  matrix products: 166 us -> 49.4 us
  local copies, waits for them, and re-layouts: 87.7 us -> 59.3 us
  blocking collectives: 28.2 us -> 46.2 us
    reduce_scatter x6 -> x2, waiting for transfers between devices: 390 us -> 40.1 us  [the longest x1 23.2 us: shards(): stacked = lax.psum_scatter(stacked, 'ctx', scatter_dimension=0, tiled=False)]
    pallas_call x0 -> x11, Pallas kernels: none -> 279 us  [the longest x9 232 us: comm_call(): pl.pallas_call(kernel, out_shape=out_shape, in_specs=[pl.BlockSpec(memory...]
    psum x1 -> x0, waiting for transfers between devices: 196 us -> none  [shards(): lax.psum(owned_attend.astype(jnp.bfloat16), 'ctx').astype(jnp.float32)]
    all_gather x6 -> x5, waiting for transfers between devices: 230 us -> 51.4 us  [the longest x1 35.7 us: shards(): stacked = lax.all_gather(stacked, 'ctx', axis=0, tiled=False)]
    dot_general x68 -> x12, matrix products: 166 us -> 49.4 us  [the longest x4 14.6 us: dot(): return jnp.dot(left, right, preferred_element_type=F32)]
    dynamic_slice x56 -> x1, local copies, waits for them, and re-layouts: 42.2 us -> 0.41 us  [shards(): attend_here = lax.dynamic_index_in_dim(attend_grouped, c, 1, keepdims=False)]
    reduce_sum x13 -> x7, other arithmetic: 28.7 us -> 7.78 us  [the longest x2 3.1 us: norm_parts(): center = values - jnp.mean(values, axis=-1, keepdims=True)]
    psum x1, blocking collectives: 21.9 us -> 41.1 us  [shards(): lax.psum(grad_norms, ('fsdp', 'ctx'))]
  transfers between devices with their start and end apart: 14 -> 9, of which waited for: 12 -> 5; matrix products, arithmetic and copies ran while one was open for 12% -> 18% of each run, Pallas kernels for 0% -> 42%
where the time goes in v1:
time: 621 us; the launch traced here: 614 us
  Pallas kernels  279 us (45%)
  waiting for transfers between devices  98.1 us (16%)
  local copies, waits for them, and re-layouts  59.3 us (10%)
  other arithmetic  59.1 us (10%)
  matrix products  49.4 us (8%)
  blocking collectives  46.2 us (7%)
  between operations  14.9 us (2%)
  starting transfers between devices  8.19 us (1%)
    pallas_call x9, Pallas kernels, comm_call(): pl.pallas_call(kernel, out_shape=out_shape, in_specs=[pl.BlockSpec(memory...  232 us
    psum x1, blocking collectives, shards(): lax.psum(grad_norms, ('fsdp', 'ctx'))  41.1 us
    all_gather x1, waiting for transfers between devices, shards(): stacked = lax.all_gather(stacked, 'ctx', axis=0, tiled=False)  35.7 us
    unnamed x73, local copies, waits for them, and re-layouts  33.9 us
    pallas_call x1, Pallas kernels, attend_backward(): pl.pallas_call(functools.partial(attend_backward_kernel, heads), out_shap...  26.5 us
    mul x5, other arithmetic, adam_step(): -LEARN  26.1 us
    reduce_scatter x1, waiting for transfers between devices, shards(): stacked = lax.psum_scatter(stacked, 'ctx', scatter_dimension=0, tiled=False)  23.2 us
    pallas_call x1, Pallas kernels, attend_forward(): pl.pallas_call(functools.partial(attend_forward_kernel, heads), out_shape...  20.2 us
  transfers between devices with their start and end apart: 9, of which 5 were waited for; matrix products, arithmetic and copies ran while one was open for 18% of the time, Pallas kernels for 42%

profile of v1, /device:TPU:0, one launch (start us, length us, event | category | flops | bytes accessed | tf_op | source)
XLA Modules:
  0.0 614.2 jit_solution(15662279117068325910)
XLA Ops:
  7.9 4.2 copy.71
  12.1 4.5 all-to-all-start
  17.8 61.4 %shard_map.345 = bf16[8,256,1024]{2,1,0:T(8,128)(2,1)} custom-call(bf16[256,1024]{1,0:T(8,128)(2,1)} %bitcast.131), custom_call_target="tpu_custom_call" | custom-call | tf_op jit(solution)/shard_map/pallas_call | solution.py:72
  79.2 3.0 convert_reduce_fusion
  85.2 8.3 %shard_map.346 = bf16[4,256,384]{2,1,0:T(8,128)(2,1)} custom-call(bf16[256,384]{1,0:T(8,128)(2,1)} %bitcast.161), custom_call_target="tpu_custom_call" | custom-call | tf_op jit(solution)/shard_map/pallas_call | solution.py:72
  93.5 5.2 all_gather.24
  99.3 3.4 add_convert_fusion
  102.7 3.6 convolution_convert_fusion.qkv_ref
  106.3 20.2 %shard_map.347 = (bf16[2048,128]{1,0:T(8,128)(2,1)}, f32[128,2048]{1,0:T(8,128)}, f32[8,2048]{1,0:T(8,128)}) custom-call(s32[16]{0:T(128)} %select_reduce_fusion.slot_ref, s32[16]{0:T(128)} %bitcast.181, bf16[2048,384]{1,0:T(8,128)(2,1)} %convolution_convert_fusion.qkv_ref), custom_call_target="tpu_custom_call" | custom-call | flops 2147483648 | bytes 2621440 | tf_op jit(solution)/shard_map/pallas_call | solution.py:487
  126.5 16.5 %shard_map.348 = bf16[8,256,128]{2,1,0:T(8,128)(2,1)} custom-call(bf16[8,256,128]{2,1,0:T(8,128)(2,1)} %bitcast.164), custom_call_target="tpu_custom_call" | custom-call | tf_op jit(solution)/shard_map/pallas_call | solution.py:72
  144.2 4.1 copy.72
  152.1 18.2 %shard_map.349 = bf16[4,256,1024]{2,1,0:T(8,128)(2,1)} custom-call(bf16[256,1024]{1,0:T(8,128)(2,1)} %add_convert_fusion.2.x_ref), custom_call_target="tpu_custom_call" | custom-call | tf_op jit(solution)/shard_map/pallas_call | solution.py:72
  170.3 4.7 fusion.43
  175.1 4.0 convolution_convert_fusion.4
  179.0 17.8 %shard_map.350 = f32[256,1024]{1,0:T(8,128)} custom-call(bf16[4,256,1024]{2,1,0:T(8,128)(2,1)} %bitcast.149), custom_call_target="tpu_custom_call" | custom-call | tf_op jit(solution)/shard_map/pallas_call | solution.py:72
  196.8 7.7 %multiply_convert_fusion = bf16[1024,1024]{1,0:T(8,128)(2,1)S(1)} fusion(f32[1024,1024]{1,0:T(8,128)} %copy-done.27, bf16[1024,1024]{1,0:T(8,128)(2,1)} %param.24, bf16[1,1024,1024]{2,1,0:T(8,128)(2,1)} %all-gather.13.cloned.1.call-done), kind=kOutput, calls=%fused_computation.18 | convolution fusion | flops 2168455168 | bytes 10485760 | tf_op jit(solution)/shard_map/dot_general | solution.py:689
  204.6 3.7 convolution_convert_fusion.3
  208.3 18.3 %shard_map.351 = f32[256,1024]{1,0:T(8,128)} custom-call(bf16[4,256,1024]{2,1,0:T(8,128)(2,1)} %bitcast.148), custom_call_target="tpu_custom_call" | custom-call | tf_op jit(solution)/shard_map/pallas_call | solution.py:72
  228.8 2.8 convert_add_fusion.1
  233.8 4.9 convolution_convert_fusion.2
  241.1 4.1 fusion.13
  245.1 16.9 %reduce-scatter.3.cloned.1.call-done = bf16[256,1024]{1,0:T(8,128)(2,1)} async-done(((bf16[1024,1024]{1,0:T(8,128)(2,1)}), bf16[256,1024]{1,0:T(8,128)(2,1)}) %reduce-scatter.3.cloned.1.call-update) | async-done | bytes 524304 | tf_op jit(solution)/shard_map/reduce_scatter | solution.py:763
  262.0 4.1 pad_maximum_fusion
  266.2 4.7 fusion.3
  272.9 31.1 %shard_map.352 = bf16[8,256,128]{2,1,0:T(8,128)(2,1)} custom-call(bf16[8,256,128]{2,1,0:T(8,128)(2,1)} %bitcast.155), custom_call_target="tpu_custom_call" | custom-call | tf_op jit(solution)/shard_map/pallas_call | solution.py:72
  304.0 26.5 %shard_map.353 = bf16[2048,384]{1,0:T(8,128)(2,1)} custom-call(s32[16]{0:T(128)} %select_reduce_fusion.slot_ref, s32[16]{0:T(128)} %bitcast.182, bf16[2048,384]{1,0:T(8,128)(2,1)} %convolution_convert_fusion.qkv_ref, bf16[2048,128]{1,0:T(8,128)(2,1)} %bitcast.163, f32[128,2048]{1,0:T(8,128)} %get-tuple-element.26.out_t_ref, ...), custom_call_target="tpu_custom_call" | custom-call | flops 5368709120 | bytes 5242880 | tf_op jit(solution)/shard_map/pallas_call | solution.py:592
  330.6 6.1 convolution_convert_fusion.5
  336.6 9.5 %shard_map.355 = f32[256,384]{1,0:T(8,128)} custom-call(bf16[4,256,384]{2,1,0:T(8,128)(2,1)} %bitcast.159), custom_call_target="tpu_custom_call" | custom-call | tf_op jit(solution)/shard_map/pallas_call | solution.py:72
  349.7 23.2 %reduce-scatter.5.cloned.1.call-done = bf16[1,288,1024]{2,1,0:T(8,128)(2,1)} async-done(((bf16[8,288,1024]{2,1,0:T(8,128)(2,1)}), bf16[1,288,1024]{2,1,0:T(8,128)(2,1)}) %reduce-scatter.5.cloned.1.call-update) | async-done | bytes 589840 | tf_op jit(solution)/shard_map/reduce_scatter | solution.py:776
  374.7 3.4 all-to-all-start.1
  379.0 5.1 all-to-all-done.1
  387.1 3.5 copy.79
  390.6 3.5 copy.80
  394.6 51.1 %shard_map.354 = bf16[8,256,384]{2,1,0:T(8,128)(2,1)} custom-call(bf16[8,256,384]{2,1,0:T(8,128)(2,1)} %bitcast.157), custom_call_target="tpu_custom_call" | custom-call | tf_op jit(solution)/shard_map/pallas_call | solution.py:72
  445.7 2.6 copy.75
  454.6 5.3 add_multiply_fusion.3
  459.9 3.5 copy.85
  463.5 3.5 copy.86
  467.0 3.5 copy.87
  472.9 15.6 %all-gather.11.cloned.1.call-done = bf16[1024,3072]{0,1:T(8,128)(2,1)} async-done(((bf16[256,3072]{0,1:T(8,128)(2,1)}), bf16[1024,3072]{0,1:T(8,128)(2,1)}) %all-gather.11.cloned.1.call-update) | async-done | bytes 6291472 | tf_op jit(solution)/shard_map/all_gather | solution.py:664
  488.5 5.5 fusion.26
  494.1 41.1 %psum.7 = f32[4,1024]{1,0:T(4,128)S(1)} all-reduce(f32[4,1024]{1,0:T(4,128)S(1)} %pad_maximum_fusion.2), channel_id=1, replica_groups=mesh['fsdp'=4,'ctx'=8] {'fsdp','ctx'}, use_global_device_ids=true, to_apply=%region_17.18 | all-reduce | flops 4096 | bytes 32768 | tf_op jit(solution)/shard_map/psum | solution.py:748
  537.2 35.7 %all-gather.17.cloned.1.call-done = bf16[2304,1024]{1,0:T(8,128)(2,1)} async-done(((bf16[288,1024]{1,0:T(8,128)(2,1)}), bf16[2304,1024]{1,0:T(8,128)(2,1)}) %all-gather.17.cloned.1.call-update) | async-done | bytes 4718608 | tf_op jit(solution)/shard_map/all_gather | solution.py:789
  574.0 5.1 fusion.40
  579.2 5.7 reshape.246
  584.8 4.1 add_multiply_fusion.4
  589.4 9.3 %add_multiply_fusion.1 = (f32[256,4096]{1,0:T(8,128)}, f32[256,4096]{1,0:T(8,128)}, f32[256,4096]{1,0:T(8,128)}) fusion(bf16[256,4096]{1,0:T(8,128)(2,1)S(1)} %copy-done.9, f32[256,4096]{1,0:T(8,128)S(1)} %copy-done.5, f32[256,4096]{1,0:T(8,128)} %param.28, f32[256,4096]{1,0:T(8,128)} %param.33), kind=kLoop, calls=%fused_computation.16 | loop fusion | flops 15728640 | bytes 27262976 | tf_op jit(solution)/shard_map/mul | solution.py:63
  600.2 6.9 %add_multiply_fusion = (f32[1024,1024]{1,0:T(8,128)}, f32[1024,1024]{1,0:T(8,128)}, f32[1024,1024]{1,0:T(8,128)}, f32[1024,1024]{1,0:T(8,128)}) fusion(bf16[1024,1024]{1,0:T(8,128)(2,1)S(1)} %copy-done.18, f32[1024,1024]{1,0:T(8,128)S(1)} %copy-done.15, f32[1024,1024]{1,0:T(8,128)S(1)} %copy-done.16, bf16[8,128,1024]{2,1,0:T(8,128)(2,1)S(1)} %get-tuple-element.98), kind=kLoop, calls=%fused_computation.14 | loop fusion | flops 16777216 | bytes 29360128 | tf_op jit(solution)/shard_map/mul | solution.py:63
  (123 shorter events, 42.6 us)
Async XLA Ops:
  7.2 141.2 %all-gather.9.cloned.1.call-start = ((), (), s32[]{:S(2)}) async-start(), calls=%async_computation.4 | async-start | bytes 2621440 | tf_op jit(solution)/shard_map/all_gather | solution.py:667
  7.9 9.5 %copy-start.12 = (bf16[256,3072]{1,0:T(8,128)(2,1)S(1)}, bf16[256,3072]{1,0:T(8,128)(2,1)}, u32[]{:S(2)}) copy-start(bf16[256,3072]{1,0:T(8,128)(2,1)} %param.21) | copy-start | bytes 4718596
  12.1 132.1 %all-to-all-start = ((bf16[4,256,1024]{1,2,0:T(8,128)(2,1)}), bf16[4,256,1024]{1,2,0:T(8,128)(2,1)}, u32[]{:S(2)}, u32[]{:S(2)}) async-start(bf16[4,256,1024]{1,2,0:T(8,128)(2,1)} %bitcast.15), calls=%async_computation | async-start | bytes 4194304 | tf_op jit(solution)/shard_map/all_to_all | solution.py:668
  16.6 180.2 %all-gather.13.cloned.1.call-start = ((), (), s32[]{:S(2)}) async-start(), calls=%async_computation.8 | async-start | bytes 2621440 | tf_op jit(solution)/shard_map/all_gather | solution.py:675
  17.4 244.6 %reduce-scatter.3.cloned.1.call-start = ((), (), s32[]{:S(2)}) async-start(), calls=%async_computation.6 | async-start | bytes 2621440 | tf_op jit(solution)/shard_map/reduce_scatter | solution.py:763
  17.8 66.3 %copy-start.10 = (bf16[32,8,24,128]{3,2,1,0:T(8,128)(2,1)}, bf16[32,8,24,128]{3,2,1,0:T(8,128)(2,1)S(1)}, u32[]{:S(2)}) copy-start(bf16[32,8,24,128]{3,2,1,0:T(8,128)(2,1)S(1)} %copy.89) | copy-start | bytes 4718596
  79.2 3.5 copy-start
  82.1 11.4 %copy-start.22 = (bf16[4,256]{1,0:T(4,128)(2,1)S(1)}, bf16[4,256]{1,0:T(4,128)(2,1)}, u32[]{:S(2)}) copy-start(bf16[4,256]{1,0:T(4,128)(2,1)} %param.25) | copy-start | bytes 6148
  82.2 16.5 %copy-start.26 = (s32[1,16]{1,0:T(1,128)S(1)}, s32[1,16]{1,0:T(1,128)}, u32[]{:S(2)}) copy-start(s32[1,16]{1,0:T(1,128)} %param.20) | copy-start | bytes 196
  99.3 3.4 copy-start.21
  126.5 21.9 %copy-start.1 = (bf16[1,256,1024]{2,1,0:T(8,128)(2,1)S(1)}, bf16[1,256,1024]{2,1,0:T(8,128)(2,1)}, u32[]{:S(2)}) copy-start(bf16[1,256,1024]{2,1,0:T(8,128)(2,1)} %param.18) | copy-start | bytes 1572868
  170.3 4.7 copy-start.17
  175.0 4.0 copy-start.27
  196.8 7.8 %copy-start.20 = (bf16[4,256,1024]{2,1,0:T(8,128)(2,1)S(1)}, bf16[4,256,1024]{2,1,0:T(8,128)(2,1)}, u32[]{:S(2)}) copy-start(bf16[4,256,1024]{2,1,0:T(8,128)(2,1)} %copy.72) | copy-start | bytes 6291460
  204.6 3.7 copy-start.29
  231.6 39.3 %copy-start.3 = (f32[256,1024]{1,0:T(8,128)}, f32[256,1024]{1,0:T(8,128)S(1)}, u32[]{:S(2)}) copy-start(f32[256,1024]{1,0:T(8,128)S(1)} %get-tuple-element.100) | copy-start | bytes 3145732
  233.7 139.3 %reduce-scatter.5.cloned.1.call-start = ((), (), s32[]{:S(2)}) async-start(), calls=%async_computation.7 | async-start | bytes 5308416 | tf_op jit(solution)/shard_map/reduce_scatter | solution.py:776
  233.8 6.4 %copy-start.28 = (f32[1024,1024]{1,0:T(8,128)S(1)}, f32[1024,1024]{1,0:T(8,128)}, u32[]{:S(2)}) copy-start(f32[1024,1024]{1,0:T(8,128)} %copy-done.27) | copy-start | bytes 12582916
  238.7 2.4 copy-start.25
  266.1 182.1 %all-gather.15.cloned.1.call-start = ((), (), s32[]{:S(2)}) async-start(), calls=%async_computation.9 | async-start | bytes 1769472 | tf_op jit(solution)/shard_map/all_gather | solution.py:756
  266.2 4.8 copy-start.8
  330.6 17.3 %copy-start.11 = (bf16[32,8,24,128]{3,2,1,0:T(8,128)(2,1)S(1)}, bf16[32,8,24,128]{3,2,1,0:T(8,128)(2,1)}, u32[]{:S(2)}) copy-start(bf16[32,8,24,128]{3,2,1,0:T(8,128)(2,1)} %copy-done.10) | copy-start | bytes 4718596
  347.8 140.7 %all-gather.11.cloned.1.call-start = ((), (), s32[]{:S(2)}) async-start(), calls=%async_computation.5 | async-start | bytes 7864320 | tf_op jit(solution)/shard_map/all_gather | solution.py:664
  349.7 35.6 %copy-start.13 = (bf16[256,3072]{1,0:T(8,128)(2,1)S(1)}, bf16[256,3072]{1,0:T(8,128)(2,1)}, u32[]{:S(2)}) copy-start(bf16[256,3072]{1,0:T(8,128)(2,1)} %param.21) | copy-start | bytes 4718596
  374.7 9.4 %all-to-all-start.1 = ((bf16[4,32,1024]{2,1,0:T(8,128)(2,1)}), bf16[4,32,1024]{2,1,0:T(8,128)(2,1)S(1)}, u32[]{:S(2)}, u32[]{:S(2)}) async-start(bf16[4,32,1024]{2,1,0:T(8,128)(2,1)} %bitcast.40), calls=%async_computation.3 | async-start | bytes 524288 | tf_op jit(solution)/shard_map/all_to_all | solution.py:778
  378.1 194.8 %all-gather.17.cloned.1.call-start = ((), (), s32[]{:S(2)}) async-start(), calls=%async_computation.10 | async-start | bytes 5308416 | tf_op jit(solution)/shard_map/all_gather | solution.py:789
  450.2 2.5 copy-start.14
  451.6 2.0 copy-start.6
  451.6 3.0 copy-start.7
  488.5 46.7 %copy-start.23 = (f32[4,256]{1,0:T(4,128)S(1)}, f32[4,256]{1,0:T(4,128)}, u32[]{:S(2)}) copy-start(f32[4,256]{1,0:T(4,128)} %param.30) | copy-start | bytes 12292
  488.5 46.7 %copy-start.24 = (f32[4,256]{1,0:T(4,128)S(1)}, f32[4,256]{1,0:T(4,128)}, u32[]{:S(2)}) copy-start(f32[4,256]{1,0:T(4,128)} %param.35) | copy-start | bytes 12292
  488.5 47.3 %copy-start.2 = (bf16[1,256,1024]{2,1,0:T(8,128)(2,1)S(1)}, bf16[1,256,1024]{2,1,0:T(8,128)(2,1)}, u32[]{:S(2)}) copy-start(bf16[1,256,1024]{2,1,0:T(8,128)(2,1)} %param.18) | copy-start | bytes 1572868
  488.5 47.3 %copy-start.4 = (f32[256,1024]{1,0:T(8,128)S(1)}, f32[256,1024]{1,0:T(8,128)}, u32[]{:S(2)}) copy-start(f32[256,1024]{1,0:T(8,128)} %copy-done.3) | copy-start | bytes 3145732
  579.2 5.7 copy-start.19
  584.8 4.1 copy-start.5
  584.8 4.6 copy-start.9
  589.4 9.3 %copy-start.15 = (f32[1024,1024]{1,0:T(8,128)S(1)}, f32[1024,1024]{1,0:T(8,128)}, u32[]{:S(2)}) copy-start(f32[1024,1024]{1,0:T(8,128)} %param.29) | copy-start | bytes 12582916
  589.4 10.0 %copy-start.16 = (f32[1024,1024]{1,0:T(8,128)S(1)}, f32[1024,1024]{1,0:T(8,128)}, u32[]{:S(2)}) copy-start(f32[1024,1024]{1,0:T(8,128)} %param.34) | copy-start | bytes 12582916
  589.4 10.8 %copy-start.18 = (bf16[1024,1024]{1,0:T(8,128)(2,1)S(1)}, bf16[1024,1024]{1,0:T(8,128)(2,1)}, u32[]{:S(2)}) copy-start(bf16[1024,1024]{1,0:T(8,128)(2,1)} %param.24) | copy-start | bytes 6291460
Sparse Core Ops, SparseCore 0:
  9.6 36.4 all-gather.8
  47.7 22.5 all-gather.12
  233.8 28.1 reduce-scatter.2
  266.2 106.6 reduce-scatter.4
  375.8 65.2 all-gather.14
  443.1 45.3 all-gather.10
  491.5 81.3 all-gather.16

commit v2 on v1

v2 whole, which is shorter than its diff:
```python
import functools
import math

import jax
import jax.numpy as jnp
from jax import lax
from jax.experimental import pallas as pl
from jax.experimental.pallas import tpu as pltpu
from jax.sharding import PartitionSpec as P

HD = 64
STEP_COUNT = 10
EPS_NORM = 1e-05
NEG = -1e30
BETA_ONE = 0.9
BETA_TWO = 0.999
LEARN = 0.02
DECAY = 0.1
EPS_ADAM = 1e-08
CUBIC = 0.044715
ROOT_TWO_PI = math.sqrt(2.0 / math.pi)
LOG2E = math.log2(math.e)
TILE = 256
MESH = pl.DeviceIdType.MESH
F32 = jnp.float32
BF16 = jnp.bfloat16


def dot(left, right):
    return jnp.dot(left, right, preferred_element_type=F32)


def norm_parts(values):
    center = values - jnp.mean(values, axis=-1, keepdims=True)
    spread = jnp.mean(center * center, axis=-1, keepdims=True)
    inverse = lax.rsqrt(spread + EPS_NORM)
    return center * inverse, inverse


def norm_back(err, gain, normal, inverse):
    scaled = err * gain
    first = jnp.mean(scaled, axis=-1, keepdims=True)
    second = jnp.mean(scaled * normal, axis=-1, keepdims=True)
    return inverse * (scaled - first - normal * second)


def gelu_and_slope(values):
    square = values * values
    inner = ROOT_TWO_PI * values * (1.0 + CUBIC * square)
    tanh = jnp.tanh(inner)
    half = 0.5 * (1.0 + tanh)
    slope = half + 0.5 * values * (1.0 - tanh * tanh) * ROOT_TWO_PI * (
        1.0 + 3.0 * CUBIC * square
    )
    return values * half, slope


def adam_step(weight, grad, first, second):
    first_new = BETA_ONE * first + (1.0 - BETA_ONE) * grad
    second_new = BETA_TWO * second + (1.0 - BETA_TWO) * grad * grad
    mean_hat = first_new / (1.0 - BETA_ONE**STEP_COUNT)
    square_hat = second_new / (1.0 - BETA_TWO**STEP_COUNT)
    update = -LEARN * (
        mean_hat / (jnp.sqrt(square_hat) + EPS_ADAM) + DECAY * weight.astype(F32)
    )
    return (update, first_new, second_new)


def comm_call(kernel, out_shape, scratch, ident, operands, any_space=True):
    space = pl.ANY if any_space else pltpu.VMEM
    outs = jax.tree.map(lambda _: pl.BlockSpec(memory_space=space), out_shape)
    return pl.pallas_call(
        kernel,
        out_shape=out_shape,
        in_specs=[pl.BlockSpec(memory_space=space)] * len(operands),
        out_specs=outs,
        scratch_shapes=scratch,
        compiler_params=pltpu.CompilerParams(collective_id=ident, has_side_effects=True),
    )(*operands)


def remote(src, dst, send, recv, device):
    return pltpu.make_async_remote_copy(
        src_ref=src,
        dst_ref=dst,
        send_sem=send,
        recv_sem=recv,
        device_id=device,
        device_id_type=MESH,
    )


def fsdp_partners():
    f, c = lax.axis_index("fsdp"), lax.axis_index("ctx")
    x, k = f // 2, f % 2
    return f, c, x, k, x * 2 + 1 - k, (1 - x) * 2 + k


def greet(devices):
    barrier = pltpu.get_barrier_semaphore()
    for device in devices:
        pl.semaphore_signal(barrier, inc=1, device_id=device, device_id_type=MESH)
    pl.semaphore_wait(barrier, len(devices))


CHUNKS = 4


class Pieces:
    def __init__(self, send_sems, recv_sems):
        self.send_sems, self.recv_sems, self.used = send_sems, recv_sems, 0

    def copy(self, src, dst, device):
        n = self.used
        self.used += 1
        return remote(src, dst, self.send_sems.at[n], self.recv_sems.at[n], device)


def row_parts(rows, count):
    step = rows // count
    return [pl.ds(t * step, step) for t in range(count)]


class FsdpGather:
    def __init__(self, pieces, x_ref, o_ref, local_sem, chunks=CHUNKS):
        f, c, x, k, mate, across = fsdp_partners()
        self.parts = row_parts(x_ref.shape[0], chunks)
        self.local = pltpu.make_async_copy(x_ref, o_ref.at[f], local_sem)
        self.far = [
            pieces.copy(x_ref.at[p], o_ref.at[f, p], (across, c)) for p in self.parts
        ]
        self.near = pieces.copy(x_ref, o_ref.at[f], (mate, c))
        self.passed = [
            pieces.copy(o_ref.at[across, p], o_ref.at[across, p], (mate, c))
            for p in self.parts
        ]

    def start(self):
        for copy in self.far:
            copy.start()
        self.near.start()
        self.local.start()

    def forward(self):
        for copy, onward in zip(self.far, self.passed):
            copy.wait_recv()
            onward.start()

    def finish(self):
        self.local.wait()
        self.near.wait()
        for copy, onward in zip(self.far, self.passed):
            copy.wait_send()
            onward.wait()


class FsdpScatter:
    def __init__(self, pieces, x_ref, near_buf, far_out, far_in, chunks=CHUNKS):
        f, c, x, k, mate, across = fsdp_partners()
        self.parts = row_parts(x_ref.shape[1], chunks)
        self.x_ref, self.near_buf, self.far_out, self.far_in = x_ref, near_buf, far_out, far_in
        self.f, self.across = f, across
        away_mate = (1 - x) * 2 + 1 - k
        self.near_far = [
            pieces.copy(x_ref.at[away_mate, p], near_buf.at[0, p], (mate, c))
            for p in self.parts
        ]
        self.near_own = pieces.copy(x_ref.at[mate], near_buf.at[1], (mate, c))
        self.far = [pieces.copy(far_out.at[p], far_in.at[p], (across, c)) for p in self.parts]

    def start(self):
        for copy in self.near_far:
            copy.start()
        self.near_own.start()

    def forward(self):
        for p, near, far in zip(self.parts, self.near_far, self.far):
            near.wait_recv()
            self.far_out[p] = (
                self.x_ref[self.across, p].astype(F32) + self.near_buf[0, p].astype(F32)
            ).astype(BF16)
            far.start()

    def finish(self, store):
        self.near_own.wait_recv()
        for p, far in zip(self.parts, self.far):
            far.wait_recv()
            store(
                p,
                self.x_ref[self.f, p].astype(F32)
                + self.near_buf[1, p].astype(F32)
                + self.far_in[p].astype(F32),
            )
        self.near_own.wait_send()
        for near, far in zip(self.near_far, self.far):
            near.wait_send()
            far.wait_send()


class CtxGather:
    def __init__(self, x_ref, o_ref, cut, local_sem, send_sem, recv_sem):
        f, c = lax.axis_index("fsdp"), lax.axis_index("ctx")
        self.f, self.c, self.z, self.y = f, c, c // 2, c % 2
        self.depth = o_ref.shape[0] // 2
        self.mate = self.z * 2 + 1 - self.y
        self.parts = (pl.ds(0, cut), pl.ds(cut, x_ref.shape[0] - cut))
        self.x_ref, self.o_ref, self.send_sem, self.recv_sem = x_ref, o_ref, send_sem, recv_sem
        self.local = pltpu.make_async_copy(x_ref, o_ref.at[c], local_sem)

    @staticmethod
    def semaphores(n):
        return [
            pltpu.SemaphoreType.DMA,
            pltpu.SemaphoreType.DMA((n, 2, 3)),
            pltpu.SemaphoreType.DMA((n, 2)),
        ]

    def copy(self, zz, yy, part, way, own=False):
        block = zz * 2 + yy
        src = self.x_ref.at[self.parts[part]] if own else self.o_ref.at[block, self.parts[part]]
        there = (self.c - 2, self.c + 2, self.mate)[way]
        return remote(
            src,
            self.o_ref.at[block, self.parts[part]],
            self.send_sem.at[block, part, way],
            self.recv_sem.at[block, part],
            (self.f, there),
        )

    def start(self):
        z, y = self.z, self.y
        self.local.start()
        for part in (0, 1):
            pl.when(z < self.depth - 1)(lambda: self.copy(z, y, part, 1, True).start())
            pl.when(z > 0)(lambda: self.copy(z, y, part, 0, True).start())
        for part in (1, 0):
            self.copy(z, y, part, 2, True).start()

    def arrive(self, zz, yy, part, way):
        self.copy(zz, yy, part, way).wait_recv()
        if way == 1:
            pl.when(self.z < self.depth - 1)(lambda: self.copy(zz, yy, part, 1).start())
        else:
            pl.when(self.z > 0)(lambda: self.copy(zz, yy, part, 0).start())
        if part == 0:
            self.copy(zz, yy, part, 2).start()

    def along(self, step, yy, part):
        z = self.z
        pl.when(z - step >= 0)(lambda: self.arrive(z - step, yy, part, 1))
        pl.when(z + step < self.depth)(lambda: self.arrive(z + step, yy, part, 0))

    def forward(self):
        z, y = self.z, self.y
        self.local.wait()
        for step in range(1, self.depth):
            self.along(step, y, 0)
            self.along(step, y, 1)
            if step == 1:
                self.copy(z, 1 - y, 1, 2).wait_recv()
                pl.when(z < self.depth - 1)(lambda: self.copy(z, 1 - y, 1, 1).start())
                pl.when(z > 0)(lambda: self.copy(z, 1 - y, 1, 0).start())
            self.along(step, 1 - y, 1)

    def finish(self):
        z, y, depth = self.z, self.y, self.depth
        self.copy(z, 1 - y, 0, 2).wait_recv()
        for step in range(1, depth):
            pl.when(z - step >= 0)(lambda: self.copy(z - step, 1 - y, 0, 2).wait_recv())
            pl.when(z + step < depth)(lambda: self.copy(z + step, 1 - y, 0, 2).wait_recv())
        for step in range(depth):
            for yy, part in ((y, 0), (y, 1), (1 - y, 1)):

                def sent_right():
                    self.copy(z - step, yy, part, 1).wait_send()

                def sent_left():
                    self.copy(z + step, yy, part, 0).wait_send()

                pl.when((z - step >= 0) & (z < depth - 1))(sent_right)
                pl.when((z + step < depth) & (z > 0))(sent_left)
        self.copy(z, y, 0, 2).wait_send()
        self.copy(z, y, 1, 2).wait_send()
        for step in range(1, depth):
            pl.when(z - step >= 0)(lambda: self.copy(z - step, y, 0, 2).wait_send())
            pl.when(z + step < depth)(lambda: self.copy(z + step, y, 0, 2).wait_send())


def greet_lines(others, depth):
    f, c = lax.axis_index("fsdp"), lax.axis_index("ctx")
    z = c // 2
    barrier = pltpu.get_barrier_semaphore()

    def signal(device):
        pl.semaphore_signal(barrier, inc=1, device_id=device, device_id_type=MESH)

    for device in others:
        signal(device)
    pl.when(z > 0)(lambda: signal((f, c - 2)))
    pl.when(z < depth - 1)(lambda: signal((f, c + 2)))
    pl.semaphore_wait(
        barrier, len(others) + (z + depth - 1) // depth + (2 * depth - 2 - z) // depth
    )


def gather_cut(rows):
    return rows * 13 // 16 // 8 * 8


def start_kernel(
    tokens_ref, attend_ref, norms_ref, expand_ref,
    tokens_out, attend_out, norms_out, expand_out,
    local_sems, send_sems, recv_sems, ctx_local, ctx_send, ctx_recv,
):
    f, c, x, k, mate, across = fsdp_partners()
    n = tokens_out.shape[0]
    others = [(f + j) % 4 for j in (1, 2, 3)]
    greet_lines([(o, c) for o in others] + [(f, c // 2 * 2 + 1 - c % 2)], n // 2)
    pieces = Pieces(send_sems, recv_sems)
    tokens = CtxGather(
        tokens_ref, tokens_out, gather_cut(tokens_ref.shape[0]), ctx_local, ctx_send, ctx_recv
    )
    tokens.start()
    attend = FsdpGather(pieces, attend_ref, attend_out, local_sems.at[0], 2)
    attend.start()
    own, hidden = expand_ref.shape[0], expand_out.shape[1]
    copies = [pieces.copy(norms_ref, norms_out.at[f], (o, c)) for o in others]
    for o in others:
        copies.append(
            pieces.copy(
                expand_ref.at[:, pl.ds(pl.multiple_of(o * hidden, 128), hidden)],
                expand_out.at[pl.ds(pl.multiple_of(f * own, 16), own)],
                (o, c),
            )
        )
    for copy in copies:
        copy.start()
    stay = [
        pltpu.make_async_copy(norms_ref, norms_out.at[f], local_sems.at[1]),
        pltpu.make_async_copy(
            expand_ref.at[:, pl.ds(pl.multiple_of(f * hidden, 128), hidden)],
            expand_out.at[pl.ds(pl.multiple_of(f * own, 16), own)],
            local_sems.at[2],
        ),
    ]
    for copy in stay:
        copy.start()
    attend.forward()
    tokens.forward()
    attend.finish()
    for copy in copies + stay:
        copy.wait()
    tokens.finish()


def start_exchange(tokens, attend_here, norms, w_expand, hidden, sizes):
    fsdp, ctx = sizes
    if sizes != (4, 8):
        own = w_expand.shape[0]
        columns = lax.all_to_all(
            w_expand.reshape(own, fsdp, hidden).transpose(1, 0, 2),
            "fsdp",
            split_axis=0,
            concat_axis=0,
            tiled=True,
        )
        return (
            lax.all_gather(tokens, "ctx", axis=0, tiled=False),
            lax.all_gather(attend_here, "fsdp", axis=0, tiled=False),
            lax.all_gather(norms, "fsdp", axis=0, tiled=False),
            columns.reshape(fsdp * own, hidden),
        )
    return comm_call(
        start_kernel,
        (
            jax.ShapeDtypeStruct((ctx,) + tokens.shape, BF16),
            jax.ShapeDtypeStruct((fsdp,) + attend_here.shape, BF16),
            jax.ShapeDtypeStruct((fsdp,) + norms.shape, F32),
            jax.ShapeDtypeStruct((fsdp * w_expand.shape[0], hidden), BF16),
        ),
        [
            pltpu.SemaphoreType.DMA((3,)),
            pltpu.SemaphoreType.DMA((11,)),
            pltpu.SemaphoreType.DMA((11,)),
        ]
        + CtxGather.semaphores(ctx),
        0,
        (tokens, attend_here, norms, w_expand),
    )


def fsdp_gather_kernel(x_ref, o_ref, local_sem, send_sems, recv_sems):
    f, c, x, k, mate, across = fsdp_partners()
    greet([(mate, c), (across, c)])
    gather = FsdpGather(Pieces(send_sems, recv_sems), x_ref, o_ref, local_sem)
    gather.start()
    gather.forward()
    gather.finish()


def fsdp_gather(values, ident, sizes):
    if sizes != (4, 8):
        return lax.all_gather(values, "fsdp", axis=0, tiled=False)
    return comm_call(
        fsdp_gather_kernel,
        jax.ShapeDtypeStruct((4,) + values.shape, values.dtype),
        [
            pltpu.SemaphoreType.DMA,
            pltpu.SemaphoreType.DMA((2 * CHUNKS + 1,)),
            pltpu.SemaphoreType.DMA((2 * CHUNKS + 1,)),
        ],
        ident,
        (values,),
    )


def scatter_buffers(rows, width):
    return [
        pltpu.VMEM((2, rows, width), BF16),
        pltpu.VMEM((rows, width), BF16),
        pltpu.VMEM((rows, width), BF16),
    ]


def fsdp_scatter_kernel(x_ref, o_ref, near_buf, far_out, far_in, send_sems, recv_sems):
    f, c, x, k, mate, across = fsdp_partners()
    greet([(mate, c), (across, c)])
    scatter = FsdpScatter(Pieces(send_sems, recv_sems), x_ref, near_buf, far_out, far_in)
    scatter.start()
    scatter.forward()

    def store(p, value):
        o_ref[p] = value

    scatter.finish(store)


def fsdp_scatter(values, ident, sizes):
    if sizes != (4, 8):
        return lax.psum_scatter(values, "fsdp", scatter_dimension=0, tiled=False).astype(F32)
    rows, width = values.shape[1:]
    return comm_call(
        fsdp_scatter_kernel,
        jax.ShapeDtypeStruct((rows, width), F32),
        scatter_buffers(rows, width)
        + [
            pltpu.SemaphoreType.DMA((2 * CHUNKS + 1,)),
            pltpu.SemaphoreType.DMA((2 * CHUNKS + 1,)),
        ],
        ident,
        (values,),
        any_space=False,
    )


class CtxExchange:
    def __init__(self, pieces, n, source, target, local_sem):
        f, c = lax.axis_index("fsdp"), lax.axis_index("ctx")
        self.copies = []
        for j in range(n - 1, 0, -1):
            there = (c + j) % n
            self.copies.append(pieces.copy(source(there), target(c), (f, there)))
        self.local = pltpu.make_async_copy(source(c), target(c), local_sem)

    def start(self):
        for copy in self.copies:
            copy.start()
        self.local.start()

    def finish(self):
        self.local.wait()
        for copy in self.copies:
            copy.wait()


def greet_ctx(n, others=()):
    f, c = lax.axis_index("fsdp"), lax.axis_index("ctx")
    greet([(f, (c + j) % n) for j in range(1, n)] + list(others))


def column_block(ref, block, lanes):
    return ref.at[:, pl.ds(pl.multiple_of(block * lanes, 128), lanes)]


def ctx_to_rows_kernel(n, x_ref, o_ref, local_sem, send_sems, recv_sems):
    lanes = x_ref.shape[-1]
    greet_ctx(n)
    move = CtxExchange(
        Pieces(send_sems, recv_sems),
        n,
        lambda j: x_ref.at[j],
        lambda j: column_block(o_ref, j, lanes),
        local_sem,
    )
    move.start()
    move.finish()


def ctx_to_heads_kernel(n, x_ref, o_ref, local_sem, send_sems, recv_sems):
    lanes = o_ref.shape[-1]
    greet_ctx(n)
    move = CtxExchange(
        Pieces(send_sems, recv_sems),
        n,
        lambda j: column_block(x_ref, j, lanes),
        lambda j: o_ref.at[j],
        local_sem,
    )
    move.start()
    move.finish()


def exchange_semaphores(n):
    return [
        pltpu.SemaphoreType.DMA,
        pltpu.SemaphoreType.DMA((n - 1,)),
        pltpu.SemaphoreType.DMA((n - 1,)),
    ]


def ctx_to_rows(values, ident, sizes):
    n, rows, lanes = values.shape
    if sizes != (4, 8):
        moved = lax.all_to_all(values, "ctx", split_axis=0, concat_axis=0, tiled=True)
        return moved.transpose(1, 0, 2).reshape(rows, n * lanes)
    return comm_call(
        functools.partial(ctx_to_rows_kernel, n),
        jax.ShapeDtypeStruct((rows, n * lanes), values.dtype),
        exchange_semaphores(n),
        ident,
        (values,),
    )


def ctx_to_heads(values, ident, sizes):
    n = sizes[1]
    rows, lanes = values.shape[0], values.shape[1] // n
    if sizes != (4, 8):
        return lax.all_to_all(
            values.reshape(rows, n, lanes).transpose(1, 0, 2),
            "ctx",
            split_axis=0,
            concat_axis=0,
            tiled=True,
        )
    return comm_call(
        functools.partial(ctx_to_heads_kernel, n),
        jax.ShapeDtypeStruct((n, rows, lanes), values.dtype),
        exchange_semaphores(n),
        ident,
        (values,),
    )


def last_kernel(
    n, attend_ref, mixing_ref, norms_ref, shrink_ref, expand_ref,
    attend_out, mixing_out, norms_out, shrink_out, expand_out,
    near_buf, far_out, far_in, mixing_in, norms_in, norms_own, block, blocks, expand_own,
    send_sems, recv_sems, local_sems, *gather_sems,
):
    f, c, x, k, mate, across = fsdp_partners()
    lanes = mixing_in.shape[-1]
    wide = attend_ref.shape[-1]
    own = attend_ref.shape[1]
    hidden = expand_ref.shape[-1]
    others = [(f + j) % 4 for j in (1, 2, 3)]
    greet_ctx(n, [(o, c) for o in others])
    pieces = Pieces(send_sems, recv_sems)
    sems = [gather_sems[3 * j : 3 * j + 3] for j in range(4)]

    def columns(j):
        return expand_own.at[:, pl.ds(pl.multiple_of(j * hidden, 128), hidden)]

    scatter = FsdpScatter(pieces, attend_ref, near_buf, far_out, far_in, 2)
    scatter.start()
    early = [pieces.copy(norms_ref.at[o], norms_in.at[f], (o, c)) for o in others]
    early += [pieces.copy(expand_ref.at[o], columns(f), (o, c)) for o in others]
    move = CtxExchange(
        pieces,
        n,
        lambda j: column_block(mixing_ref, j, lanes),
        lambda j: mixing_in.at[j],
        local_sems.at[0],
    )
    early += [
        pltpu.make_async_copy(norms_ref.at[f], norms_in.at[f], local_sems.at[1]),
        pltpu.make_async_copy(expand_ref.at[f], columns(f), local_sems.at[2]),
    ]
    for copy in early:
        copy.start()
    move.start()
    shrink = CtxGather(shrink_ref, shrink_out, gather_cut(shrink_ref.shape[0]), *sems[0])
    shrink.start()
    scatter.forward()
    for copy in early:
        copy.wait()
    norms_own[...] = norms_in[0] + norms_in[1] + norms_in[2] + norms_in[3]
    expand = CtxGather(expand_own, expand_out, gather_cut(expand_own.shape[0]), *sems[1])
    small = CtxGather(norms_own, norms_out, 4, *sems[2])
    expand.start()
    small.start()
    move.finish()
    total = mixing_in[0].astype(F32)
    for j in range(1, n):
        total += mixing_in[j].astype(F32)
    block[:, wide:] = total.astype(BF16)

    def store(p, value):
        block[p, :wide] = value.astype(BF16)

    scatter.finish(store)
    gather = CtxGather(block, blocks, gather_cut(own), *sems[3])
    gather.start()
    for each in (shrink, expand, small, gather):
        each.forward()
    for each in (shrink, expand, small, gather):
        each.finish()
    for j in range(n):
        for part in range(3):
            at = (part * n + j) * lanes
            attend_out[:, at : at + lanes] = blocks[j, :, part * lanes : (part + 1) * lanes]
        mixing_out[:, j * lanes : (j + 1) * lanes] = blocks[j, :, wide:]


def last_exchange(part_attend, own_mixing, grad_norms, shrink_piece, expand_piece, sizes):
    fsdp, n = sizes
    own, wide = part_attend.shape[1:]
    width = own_mixing.shape[1]
    lanes = width // n
    _, piece, hidden = expand_piece.shape
    if sizes != (4, 8):
        own_attend = lax.psum_scatter(part_attend, "fsdp", scatter_dimension=0, tiled=False)
        attend = (
            lax.all_gather(own_attend, "ctx", axis=0, tiled=False)
            .reshape(n, own, 3, lanes)
            .transpose(1, 2, 0, 3)
            .reshape(own, 3 * width)
        )
        norms = lax.psum_scatter(grad_norms, "fsdp", scatter_dimension=0, tiled=False)
        expand = lax.all_to_all(expand_piece, "fsdp", split_axis=0, concat_axis=0, tiled=True)
        expand = expand.transpose(1, 0, 2).reshape(piece, fsdp * hidden)
        return (
            attend,
            lax.psum(own_mixing, "ctx"),
            lax.all_gather(norms, "ctx", axis=0, tiled=False),
            lax.all_gather(shrink_piece, "ctx", axis=0, tiled=True),
            lax.all_gather(expand, "ctx", axis=0, tiled=True),
        )
    count = 2 * 2 + 1 + n - 1 + 6
    vmem, anywhere = pl.BlockSpec(memory_space=pltpu.VMEM), pl.BlockSpec(memory_space=pl.ANY)
    attend, mixing, norms, shrink, expand = pl.pallas_call(
        functools.partial(last_kernel, n),
        out_shape=(
            jax.ShapeDtypeStruct((own, 3 * width), BF16),
            jax.ShapeDtypeStruct((own, width), BF16),
            jax.ShapeDtypeStruct((n,) + grad_norms.shape[1:], F32),
            jax.ShapeDtypeStruct((n,) + shrink_piece.shape, BF16),
            jax.ShapeDtypeStruct((n, piece, fsdp * hidden), BF16),
        ),
        in_specs=[vmem, vmem, vmem, anywhere, anywhere],
        out_specs=(vmem, vmem, vmem, anywhere, anywhere),
        scratch_shapes=scatter_buffers(own, wide)
        + [
            pltpu.VMEM((n, own, lanes), BF16),
            pltpu.VMEM(grad_norms.shape, F32),
            pltpu.VMEM(grad_norms.shape[1:], F32),
            pltpu.VMEM((own, wide + lanes), BF16),
            pltpu.VMEM((n, own, wide + lanes), BF16),
            pltpu.VMEM((piece, fsdp * hidden), BF16),
            pltpu.SemaphoreType.DMA((count,)),
            pltpu.SemaphoreType.DMA((count,)),
            pltpu.SemaphoreType.DMA((3,)),
        ]
        + CtxGather.semaphores(n) * 4,
        compiler_params=pltpu.CompilerParams(collective_id=7, has_side_effects=True),
    )(part_attend, own_mixing, grad_norms, shrink_piece, expand_piece)
    return (
        attend,
        mixing,
        norms,
        shrink.reshape(n * shrink_piece.shape[0], width),
        expand.reshape(n * piece, fsdp * hidden),
    )


def head_rows(h):
    return slice(h * HD, (h + 1) * HD)


def attend_forward_kernel(
    heads, slot_ref, place_ref, qkv_ref, mixed_ref, out_t_ref, total_ref,
    q_pos, k_pos, v_pos, q_t, v_t, scores, o_pos,
):
    length, lanes = q_pos.shape
    blocks = slot_ref.shape[0]
    size = length // blocks
    tiles = length // TILE
    factor = LOG2E / math.sqrt(HD)
    for p in range(blocks):
        rows = qkv_ref[pl.ds(slot_ref[p] * size, size), :]
        here = slice(p * size, (p + 1) * size)
        q_pos[here, :] = rows[:, :lanes]
        k_pos[here, :] = rows[:, lanes : 2 * lanes]
        v_pos[here, :] = rows[:, 2 * lanes :]
    for t in range(tiles):
        here = slice(t * TILE, (t + 1) * TILE)
        q_t[:, here] = q_pos[here, :].T
        v_t[:, here] = v_pos[here, :].T
    head_of_row = lax.broadcasted_iota(jnp.int32, (lanes, TILE), 0) // HD
    allowed = lax.broadcasted_iota(jnp.int32, (TILE, TILE), 0) <= lax.broadcasted_iota(
        jnp.int32, (TILE, TILE), 1
    )

    def fold_max(values):
        return jnp.max(values.reshape(TILE // 8, 8, TILE), axis=0)

    def fold_sum(values):
        return jnp.sum(values.reshape(TILE // 8, 8, TILE), axis=0)

    @pl.loop(0, tiles)
    def _(i):
        here = pl.ds(pl.multiple_of(i * TILE, TILE), TILE)
        q_tile = q_t[:, here]
        q_heads = [
            jnp.where(head_of_row == h, q_tile, jnp.zeros_like(q_tile)) for h in range(heads)
        ]

        def first(j, tops):
            there = pl.ds(pl.multiple_of(j * TILE, TILE), TILE)
            keys = k_pos[there, :]
            result = []
            for h in range(heads):
                raw = dot(keys, q_heads[h])
                scores[h, there, :] = raw
                result.append(jnp.maximum(tops[h], fold_max(raw)))
            return tuple(result)

        tops = lax.fori_loop(
            0, i, first, tuple(jnp.full((8, TILE), NEG, F32) for _ in range(heads))
        )
        keys = k_pos[here, :]
        row_tops = []
        for h in range(heads):
            raw = jnp.where(allowed, dot(keys, q_heads[h]), NEG)
            scores[h, here, :] = raw
            row_tops.append(
                jnp.max(jnp.maximum(tops[h], fold_max(raw)), axis=0, keepdims=True) * factor
            )

        def second(j, state):
            there = pl.ds(pl.multiple_of(j * TILE, TILE), TILE)
            result = []
            for h in range(heads):
                sums, acc = state[h]
                probs = jnp.exp2(scores[h, there, :] * factor - row_tops[h])
                acc = acc + dot(v_t[head_rows(h), there], probs.astype(BF16))
                result.append((sums + fold_sum(probs), acc))
            return tuple(result)

        state = lax.fori_loop(
            0,
            i + 1,
            second,
            tuple(
                (jnp.zeros((8, TILE), F32), jnp.zeros((HD, TILE), F32)) for _ in range(heads)
            ),
        )
        outs = []
        for h in range(heads):
            sums, acc = state[h]
            row_sum = jnp.sum(sums, axis=0, keepdims=True)
            out = acc * (1.0 / row_sum)
            out_t_ref[head_rows(h), here] = out
            total_ref[pl.ds(h, 1), here] = row_tops[h] + jnp.log2(row_sum)
            outs.append(out)
        out = jnp.concatenate(outs, axis=0) if heads > 1 else outs[0]
        o_pos[here, :] = out.T.astype(BF16)

    for s in range(blocks):
        mixed_ref[s * size : (s + 1) * size, :] = o_pos[
            pl.ds(place_ref[s] * size, size), :
        ]


def attend_forward(slot_of, place_of, qkv, heads):
    length = qkv.shape[0]
    lanes = heads * HD
    vmem = pl.BlockSpec(memory_space=pltpu.VMEM)
    smem = pl.BlockSpec(memory_space=pltpu.SMEM)
    return pl.pallas_call(
        functools.partial(attend_forward_kernel, heads),
        out_shape=(
            jax.ShapeDtypeStruct((length, lanes), BF16),
            jax.ShapeDtypeStruct((lanes, length), F32),
            jax.ShapeDtypeStruct((8, length), F32),
        ),
        in_specs=[smem, smem, vmem],
        out_specs=(vmem, vmem, vmem),
        scratch_shapes=[pltpu.VMEM((length, lanes), BF16)] * 3
        + [pltpu.VMEM((lanes, length), BF16)] * 2
        + [pltpu.VMEM((heads, length, TILE), F32), pltpu.VMEM((length, lanes), BF16)],
        cost_estimate=pl.CostEstimate(
            flops=4 * length * length * lanes,
            bytes_accessed=10 * length * lanes,
            transcendentals=heads * length * length // 2,
        ),
    )(slot_of, place_of, qkv)


def attend_backward_kernel(
    heads, between, slot_ref, place_ref, qkv_ref, load_grad, out_t_ref, total_ref, result_ref,
    q_pos, k_pos, v_pos, g_pos, k_heads, v_heads, q_t, k_t, g_t, delta,
    dq_t, dk_acc, dv_acc, d_pos,
):
    length, lanes = q_pos.shape
    blocks = slot_ref.shape[0]
    size = length // blocks
    tiles = length // TILE
    scale = 1.0 / math.sqrt(HD)
    factor = LOG2E * scale
    for p in range(blocks):
        rows = qkv_ref[pl.ds(slot_ref[p] * size, size), :]
        here = slice(p * size, (p + 1) * size)
        q_pos[here, :] = rows[:, :lanes]
        k_pos[here, :] = rows[:, lanes : 2 * lanes]
        v_pos[here, :] = rows[:, 2 * lanes :]
    head_of_lane = lax.broadcasted_iota(jnp.int32, (TILE, lanes), 1) // HD
    allowed = lax.broadcasted_iota(jnp.int32, (TILE, TILE), 0) <= lax.broadcasted_iota(
        jnp.int32, (TILE, TILE), 1
    )
    for t in range(tiles):
        here = slice(t * TILE, (t + 1) * TILE)
        q_t[:, here] = q_pos[here, :].T
        k_t[:, here] = k_pos[here, :].T
        keys, values = k_pos[here, :], v_pos[here, :]
        for h in range(heads):
            k_heads[h, here, :] = jnp.where(head_of_lane == h, keys, jnp.zeros_like(keys))
            v_heads[h, here, :] = jnp.where(head_of_lane == h, values, jnp.zeros_like(values))
    dq_t[...] = jnp.zeros_like(dq_t)
    load = load_grad()
    for p in range(blocks):
        g_pos[p * size : (p + 1) * size, :] = load(slot_ref[p] * size, size)
    for t in range(tiles):
        here = slice(t * TILE, (t + 1) * TILE)
        g_tile = g_pos[here, :].T
        g_t[:, here] = g_tile
        product = g_tile.astype(F32) * out_t_ref[:, here]
        for h in range(heads):
            delta[h : h + 1, here] = jnp.sum(product[head_rows(h)], axis=0, keepdims=True)

    def pair(j, i, masked):
        there = pl.ds(pl.multiple_of(j * TILE, TILE), TILE)
        here = pl.ds(pl.multiple_of(i * TILE, TILE), TILE)
        for h in range(heads):
            raw = dot(k_heads[h, there, :], q_t[:, here])
            probs = jnp.exp2(raw * factor - total_ref[pl.ds(h, 1), here])
            if masked:
                probs = jnp.where(allowed, probs, 0.0)
            d_probs = dot(v_heads[h, there, :], g_t[:, here])
            d_scores = (probs * (d_probs - delta[pl.ds(h, 1), here])).astype(BF16)
            dv = dot(probs.astype(BF16), g_pos[here, :])
            dk = dot(d_scores, q_pos[here, :])
            if masked:
                dv_acc[h], dk_acc[h] = dv, dk
            else:
                dv_acc[h] += dv
                dk_acc[h] += dk
            dq_t[head_rows(h), here] += dot(k_t[head_rows(h), there], d_scores)

    @pl.loop(0, tiles)
    def _(j):
        pair(j, j, True)

        @pl.loop(j + 1, tiles)
        def _(i):
            pair(j, i, False)

        there = pl.ds(pl.multiple_of(j * TILE, TILE), TILE)
        for index, acc, weight in ((1, dk_acc, scale), (2, dv_acc, 1.0)):
            value = acc[0]
            for h in range(1, heads):
                value = jnp.where(head_of_lane == h, acc[h], value)
            d_pos[there, index * lanes : (index + 1) * lanes] = (value * weight).astype(BF16)
        between(j)

    for t in range(tiles):
        here = slice(t * TILE, (t + 1) * TILE)
        d_pos[here, :lanes] = (dq_t[:, here].T * scale).astype(BF16)
    for s in range(blocks):
        result_ref[s * size : (s + 1) * size, :] = d_pos[pl.ds(place_ref[s] * size, size), :]


def attend_backward_scratch(length, heads):
    lanes = heads * HD
    rows = pltpu.VMEM((length, lanes), BF16)
    columns = pltpu.VMEM((lanes, length), BF16)
    by_head = pltpu.VMEM((heads, length, lanes), BF16)
    return (
        [rows] * 4
        + [by_head] * 2
        + [columns] * 3
        + [
            pltpu.VMEM((8, length), F32),
            pltpu.VMEM((lanes, length), F32),
            pltpu.VMEM((heads, TILE, lanes), F32),
            pltpu.VMEM((heads, TILE, lanes), F32),
            pltpu.VMEM((length, 3 * lanes), BF16),
        ]
    )


ATTEND_SCRATCH = 14


def local_backward_kernel(
    heads, slot_ref, place_ref, qkv_ref, grad_ref, out_t_ref, total_ref, result_ref, *scratch
):
    attend_backward_kernel(
        heads, lambda j: None, slot_ref, place_ref, qkv_ref,
        lambda: lambda at, size: grad_ref[pl.ds(at, size), :],
        out_t_ref, total_ref, result_ref, *scratch,
    )


def attend_backward(slot_of, place_of, qkv, grad, out_t, total, heads):
    length = qkv.shape[0]
    lanes = heads * HD
    vmem = pl.BlockSpec(memory_space=pltpu.VMEM)
    smem = pl.BlockSpec(memory_space=pltpu.SMEM)
    return pl.pallas_call(
        functools.partial(local_backward_kernel, heads),
        out_shape=jax.ShapeDtypeStruct((length, 3 * lanes), BF16),
        in_specs=[smem, smem, vmem, vmem, vmem, vmem],
        out_specs=vmem,
        scratch_shapes=attend_backward_scratch(length, heads),
    )(slot_of, place_of, qkv, grad, out_t, total)


def backward_kernel(
    n, heads, slot_ref, place_ref, qkv_ref, out_t_ref, total_ref,
    mixed_ref, mixing_ref, out_ref, shrink_ref, expand_ref,
    result_ref, joint_ref, own_ref, branch_ref, piece_ref, *rest,
):
    scratch, rest = rest[:ATTEND_SCRATCH], rest[ATTEND_SCRATCH:]
    (
        grad_in, near_a, far_out_a, far_in_a, near_b, far_out_b, far_in_b,
        pair_in, pair_sum, line_in, local_sems, send_sems, recv_sems,
        pair_send, pair_recv, line_send, line_recv,
    ) = rest
    f, c, x, k, mate, across = fsdp_partners()
    depth = n // 2
    z, y = c // 2, c % 2
    lanes = heads * HD
    half = shrink_ref.shape[1]
    fsdp, _, small, hidden = expand_ref.shape
    length = qkv_ref.shape[0]
    rows = length // n
    greet_ctx(n, [(mate, c), (across, c)])
    pieces = Pieces(send_sems, recv_sems)
    to_heads = CtxExchange(
        pieces, n, lambda j: column_block(mixed_ref, j, lanes), lambda j: grad_in.at[j],
        local_sems.at[0],
    )
    to_rows = CtxExchange(
        pieces, n, lambda j: result_ref.at[pl.ds(pl.multiple_of(j * rows, 128), rows)],
        lambda j: column_block(joint_ref, j, 3 * lanes), local_sems.at[1],
    )
    mixing = FsdpScatter(pieces, mixing_ref, near_a, far_out_a, far_in_a)
    branch = FsdpScatter(pieces, out_ref, near_b, far_out_b, far_in_b)
    to_heads.start()

    def pair_copies(t):
        to = (z + 1 + t) % depth * 2 + 1 - y
        there = (f, z * 2 + 1 - y)
        return [
            remote(
                shrink_ref.at[to], pair_in.at[t, pl.ds(0, half)],
                pair_send.at[t, 0], pair_recv.at[t, 0], there,
            )
        ] + [
            remote(
                expand_ref.at[j, to], pair_in.at[t, pl.ds(half + j * small, small)],
                pair_send.at[t, 1 + j], pair_recv.at[t, 1 + j], there,
            )
            for j in range(fsdp)
        ]

    def pair_total(t):
        for copy in pair_copies(t):
            copy.wait_recv()
        to = (z + 1 + t) % depth * 2 + y
        yield 0, half, shrink_ref[to].astype(F32) + pair_in[t, :half].astype(F32)
        for j in range(fsdp):
            at = half + j * small
            yield at, small, (
                expand_ref[j, to].astype(F32) + pair_in[t, at : at + small].astype(F32)
            )

    def line_copy(t):
        return remote(
            pair_sum.at[t], line_in.at[t], line_send.at[t], line_recv.at[t],
            (f, (z + 1 + t) % depth * 2 + y),
        )

    for t in range(depth):
        for copy in pair_copies(t):
            copy.start()
    mixing.start()
    mixing.forward()
    branch.start()
    branch.forward()

    def load_grad():
        to_heads.finish()

        def load(at, size):
            return grad_in[at // rows, pl.ds(at % rows, size), :]

        return load

    def between(j):
        @pl.when((j % 2 == 0) & (j < 2 * (depth - 1)))
        def _():
            t = j // 2
            for at, count, value in pair_total(t):
                pair_sum[t, at : at + count] = value.astype(BF16)
            line_copy(t).start()

    attend_backward_kernel(
        heads, between, slot_ref, place_ref, qkv_ref, load_grad, out_t_ref, total_ref,
        result_ref, *scratch,
    )
    to_rows.start()

    def store_own(p, value):
        own_ref[p] = value.astype(BF16)

    def store_branch(p, value):
        branch_ref[p] = value

    mixing.finish(store_own)
    branch.finish(store_branch)
    for t in range(depth - 1):
        line_copy(t).wait_recv()
    for at, count, value in pair_total(depth - 1):
        for t in range(depth - 1):
            value += line_in[t, at : at + count].astype(F32)
        piece_ref[at : at + count] = value.astype(BF16)
    for t in range(depth):
        for copy in pair_copies(t):
            copy.wait_send()
    for t in range(depth - 1):
        line_copy(t).wait_send()
    to_rows.finish()


def backward_exchange(
    slot_of, place_of, qkv, out_t, total, grad_mixed, grad_mixing, part_out,
    grad_shrink, grad_expand, heads, sizes,
):
    fsdp, n = sizes
    length = qkv.shape[0]
    rows, lanes = length // n, heads * HD
    width = grad_mixed.shape[1]
    own = width // fsdp
    hidden = grad_expand.shape[1]
    small = own // n
    if sizes != (4, 8):
        grad_heads = ctx_to_heads(grad_mixed, None, sizes).reshape(length, lanes)
        d_qkv = attend_backward(slot_of, place_of, qkv, grad_heads, out_t, total, heads)
        shrink = lax.psum_scatter(grad_shrink, "ctx", scatter_dimension=0, tiled=True)
        expand = lax.psum_scatter(
            grad_expand.reshape(fsdp, n, small, hidden)
            .transpose(1, 0, 2, 3)
            .reshape(n * fsdp * small, hidden),
            "ctx",
            scatter_dimension=0,
            tiled=True,
        )
        return (
            d_qkv,
            ctx_to_rows(d_qkv.reshape(n, rows, 3 * lanes), None, sizes),
            lax.psum_scatter(grad_mixing, "fsdp", scatter_dimension=0, tiled=True),
            lax.psum_scatter(part_out, "fsdp", scatter_dimension=0, tiled=True).astype(F32),
            shrink,
            expand.reshape(fsdp, small, hidden),
        )
    half = hidden // n
    tall = half + fsdp * small
    depth = n // 2
    count = 2 * (n - 1) + 2 * (2 * CHUNKS + 1)
    vmem, anywhere = pl.BlockSpec(memory_space=pltpu.VMEM), pl.BlockSpec(memory_space=pl.ANY)
    smem = pl.BlockSpec(memory_space=pltpu.SMEM)
    d_qkv, joint, own_mixing, branch, piece = pl.pallas_call(
        functools.partial(backward_kernel, n, heads),
        out_shape=(
            jax.ShapeDtypeStruct((length, 3 * lanes), BF16),
            jax.ShapeDtypeStruct((rows, 3 * width), BF16),
            jax.ShapeDtypeStruct((own, width), BF16),
            jax.ShapeDtypeStruct((rows, width), F32),
            jax.ShapeDtypeStruct((tall, width), BF16),
        ),
        in_specs=[smem, smem] + [vmem] * 8,
        out_specs=(vmem, anywhere, vmem, vmem, vmem),
        scratch_shapes=attend_backward_scratch(length, heads)
        + [pltpu.VMEM((n, rows, lanes), BF16)]
        + scatter_buffers(own, width)
        + scatter_buffers(rows, width)
        + [
            pltpu.VMEM((depth, tall, width), BF16),
            pltpu.VMEM((depth - 1, tall, width), BF16),
            pltpu.VMEM((depth - 1, tall, width), BF16),
            pltpu.SemaphoreType.DMA((2,)),
            pltpu.SemaphoreType.DMA((count,)),
            pltpu.SemaphoreType.DMA((count,)),
            pltpu.SemaphoreType.DMA((depth, 1 + fsdp)),
            pltpu.SemaphoreType.DMA((depth, 1 + fsdp)),
            pltpu.SemaphoreType.DMA((depth - 1,)),
            pltpu.SemaphoreType.DMA((depth - 1,)),
        ],
        compiler_params=pltpu.CompilerParams(
            collective_id=6, has_side_effects=True, vmem_limit_bytes=58 * 2**20
        ),
    )(
        slot_of,
        place_of,
        qkv,
        out_t,
        total,
        grad_mixed,
        grad_mixing.reshape(fsdp, own, width),
        part_out.reshape(fsdp, rows, width),
        grad_shrink.reshape(n, half, width),
        grad_expand.reshape(fsdp, n, small, hidden),
    )
    return d_qkv, joint, own_mixing, branch, piece[:half], piece[half:].reshape(fsdp, small, width)


def shards(
    sizes,
    tokens,
    out_grad,
    slot_block,
    w_attend,
    w_mixing,
    w_expand,
    w_shrink,
    w_norms,
    first_attend,
    first_mixing,
    first_expand,
    first_shrink,
    first_norms,
    second_attend,
    second_mixing,
    second_expand,
    second_shrink,
    second_norms,
):
    fsdp, ctx = sizes
    f, c = lax.axis_index("fsdp"), lax.axis_index("ctx")
    rows, width = tokens.shape[1:]
    heads = width // HD // ctx
    lanes = heads * HD
    length = rows * ctx
    own = width // fsdp
    hidden = w_shrink.shape[0]

    place_of = slot_block[0]
    slot_of = jnp.sum(
        jnp.where(
            place_of[None, :] == jnp.arange(2 * ctx, dtype=jnp.int32)[:, None],
            jnp.arange(2 * ctx, dtype=jnp.int32)[None, :],
            0,
        ),
        axis=1,
    )

    start = tokens[0]
    incoming = out_grad[0]
    attend_grouped = (
        w_attend.reshape(own, 3, ctx, lanes).transpose(0, 2, 1, 3).reshape(own, 3 * width)
    )
    attend_here = lax.dynamic_slice_in_dim(
        w_attend.reshape(own, 3, width), c * lanes, lanes, 2
    ).reshape(own, 3 * lanes)
    padded_norms = jnp.concatenate([w_norms.astype(F32), jnp.zeros((4, own), F32)], axis=0)
    whole_tokens, whole_here, norms, expand_columns = start_exchange(
        start, attend_here, padded_norms, w_expand, hidden, sizes
    )
    norms = norms.transpose(1, 0, 2).reshape(8, width)
    whole_here = whole_here.reshape(width, 3 * lanes)
    whole_tokens, mixing_late, incoming_late, grouped_late = lax.optimization_barrier(
        (whole_tokens, w_mixing, incoming, attend_grouped)
    )
    whole_mixing = lax.all_gather(mixing_late, "fsdp", axis=0, tiled=True)
    grads_in = lax.all_gather(incoming_late, "fsdp", axis=0, tiled=True)
    whole_attend = lax.all_gather(grouped_late, "fsdp", axis=0, tiled=True)

    whole_tokens = whole_tokens.reshape(length, width)
    normed_all = (norm_parts(whole_tokens.astype(F32))[0] * norms[0] + norms[1]).astype(BF16)
    qkv = dot(normed_all, whole_here).astype(BF16)
    mixed_heads, out_t, total = attend_forward(slot_of, place_of, qkv, heads)
    mixed = ctx_to_rows(mixed_heads.reshape(ctx, rows, lanes), 1, sizes)

    middle = start.astype(F32) + dot(mixed, whole_mixing)
    normal_two, inverse_two = norm_parts(middle)
    normed_two = (normal_two * norms[2] + norms[3]).astype(BF16)
    normed_two_all = fsdp_gather(normed_two, 3, sizes).reshape(fsdp * rows, width)
    expanded = dot(normed_two_all, expand_columns)
    grad_activated = (
        lax.dot_general(
            grads_in, w_shrink, (((1,), (1,)), ((), ())), preferred_element_type=F32
        )
        .astype(BF16)
        .astype(F32)
    )
    activated, slope = gelu_and_slope(expanded)
    activated = activated.astype(BF16)
    grad_expanded = (grad_activated * slope).astype(BF16)
    part_normed_two = lax.dot_general(
        grad_expanded, expand_columns, (((1,), (1,)), ((), ())), preferred_element_type=F32
    ).astype(BF16)
    grad_normed_two = fsdp_scatter(part_normed_two.reshape(fsdp, rows, width), 4, sizes)
    part_out = dot(activated, w_shrink).astype(BF16)
    grad_shrink = lax.dot_general(
        activated, grads_in, (((0,), (0,)), ((), ())), preferred_element_type=F32
    ).astype(BF16)
    grad_expand = lax.dot_general(
        normed_two_all, grad_expanded, (((0,), (0,)), ((), ())), preferred_element_type=F32
    ).astype(BF16)
    grad_middle = incoming.astype(F32) + norm_back(
        grad_normed_two, norms[2], normal_two, inverse_two
    )
    grad_branch = grad_middle.astype(BF16)
    grad_mixed = lax.dot_general(
        grad_branch, whole_mixing, (((1,), (1,)), ((), ())), preferred_element_type=F32
    ).astype(BF16)
    grad_mixing = lax.dot_general(
        mixed, grad_branch, (((0,), (0,)), ((), ())), preferred_element_type=F32
    ).astype(BF16)
    grad_mixed, whole_attend = lax.optimization_barrier((grad_mixed, whole_attend))
    d_qkv, grad_joint, own_mixing, branch, shrink_piece, expand_piece = backward_exchange(
        slot_of, place_of, qkv, out_t, total, grad_mixed, grad_mixing, part_out,
        grad_shrink, grad_expand, heads, sizes,
    )
    layer_out = (middle + branch).astype(BF16)
    grad_normed = lax.dot_general(
        grad_joint, whole_attend, (((1,), (1,)), ((), ())), preferred_element_type=F32
    )
    normal_one, inverse_one = norm_parts(start.astype(F32))
    tokens_grad = (
        grad_middle + norm_back(grad_normed, norms[0], normal_one, inverse_one)
    )[None]
    zero = jnp.zeros((width,), F32)
    grad_norms = jnp.stack(
        [
            jnp.sum(grad_normed * normal_one, axis=0),
            jnp.sum(grad_normed, axis=0),
            jnp.sum(grad_normed_two * normal_two, axis=0),
            jnp.sum(grad_normed_two, axis=0),
        ]
        + [zero] * 4
    )
    part_attend = lax.dot_general(
        normed_all, d_qkv, (((0,), (0,)), ((), ())), preferred_element_type=F32
    ).astype(BF16)
    sum_attend, sum_mixing, parts_norms, sum_shrink, sum_expand = last_exchange(
        part_attend.reshape(fsdp, own, 3 * lanes),
        own_mixing,
        grad_norms.reshape(8, fsdp, own).transpose(1, 0, 2),
        shrink_piece,
        expand_piece,
        sizes,
    )
    sum_attend, sum_mixing = sum_attend.astype(F32), sum_mixing.astype(F32)
    sum_shrink, sum_expand = sum_shrink.astype(F32), sum_expand.astype(F32)
    sum_norms = jnp.sum(parts_norms, axis=0)[:4]

    result = [layer_out[None], tokens_grad]
    for weight, grad, first, second in (
        (w_attend, sum_attend, first_attend, second_attend),
        (w_mixing, sum_mixing, first_mixing, second_mixing),
        (w_expand, sum_expand, first_expand, second_expand),
        (w_shrink, sum_shrink, first_shrink, second_shrink),
        (w_norms, sum_norms, first_norms, second_norms),
    ):
        result.append(grad)
        result.extend(adam_step(weight, grad, first, second))
    return tuple(result)


def solution(mesh):
    rows = P("fsdp", None)
    columns = P(None, "fsdp")
    tokens = P("fsdp", "ctx", None)
    return jax.shard_map(
        functools.partial(shards, (mesh.shape["fsdp"], mesh.shape["ctx"])),
        mesh=mesh,
        in_specs=(tokens, tokens, rows)
        + (rows, rows, rows, rows, columns) * 3,
        out_specs=(tokens, tokens) + (rows,) * 16 + (columns,) * 4,
        check_vma=False,
    )
```

time: 621 us -> 474 us (0.76)
  waiting for transfers between devices: 98.1 us -> 1.42 us
  Pallas kernels: 279 us -> 341 us
  local copies, waits for them, and re-layouts: 59.3 us -> 10.1 us
  blocking collectives: 46.2 us -> 0 us
  other arithmetic: 59.1 us -> 50.9 us
  starting transfers between devices: 8.19 us -> 0.12 us
    pallas_call x1 -> x2, Pallas kernels: 26.5 us -> 202 us  [the longest x1 109 us: backward_exchange(): pl.pallas_call(functools.partial(backward_kernel, n, heads), out_shape=(j...]
    pallas_call x9 -> x4, Pallas kernels: 232 us -> 118 us  [comm_call(): pl.pallas_call(kernel, out_shape=out_shape, in_specs=[pl.BlockSpec(memory...]
    all_gather x5 -> x3, waiting for transfers between devices: 51.4 us -> 0.02 us  [the longest x1 0.02 us: shards(): whole_mixing = lax.all_gather(mixing_late, 'fsdp', axis=0, tiled=True)]
    psum x1 -> x0, blocking collectives: 41.1 us -> none  [shards(): lax.psum(grad_norms, ('fsdp', 'ctx'))]
    reduce_scatter x2 -> x0, waiting for transfers between devices: 40.1 us -> none  [the longest x1 23.2 us: shards(): stacked = lax.psum_scatter(stacked, 'ctx', scatter_dimension=0, tiled=False)]
    unnamed x73 -> x71, local copies, waits for them, and re-layouts: 33.9 us -> 4.98 us
    convert_element_type x4 -> x0, local copies, waits for them, and re-layouts: 8.78 us -> none  [the longest x1 5.67 us: shards(): sum_expand = stacked[:, shrink_piece:shrink_piece + expand_rows].reshape(...]
    all_to_all x2 -> x0, starting transfers between devices: 7.9 us -> none  [the longest x1 4.5 us: shards(): lax.all_to_all(w_expand.reshape(own, fsdp, hidden).transpose(1, 0, 2), 'f...]
  transfers between devices with their start and end apart: 9 -> 3, of which waited for: 5 -> 0; matrix products, arithmetic and copies ran while one was open for 18% -> 13% of each run, Pallas kernels for 42% -> 17%
where the time goes in v2:
time: 474 us; the launch traced here: 468 us
  Pallas kernels  341 us (72%)
  other arithmetic  50.9 us (11%)
  matrix products  49.8 us (11%)
  between operations  14.4 us (3%)
  local copies, waits for them, and re-layouts  10.1 us (2%)
    pallas_call x4, Pallas kernels, comm_call(): pl.pallas_call(kernel, out_shape=out_shape, in_specs=[pl.BlockSpec(memory...  118 us
    pallas_call x1, Pallas kernels, backward_exchange(): pl.pallas_call(functools.partial(backward_kernel, n, heads), out_shape=(j...  109 us
    pallas_call x1, Pallas kernels, last_exchange(): pl.pallas_call(functools.partial(last_kernel, n), out_shape=(jax.ShapeDty...  92.9 us
    mul x5, other arithmetic, adam_step(): -LEARN  27.3 us
    pallas_call x1, Pallas kernels, attend_forward(): pl.pallas_call(functools.partial(attend_forward_kernel, heads), out_shape...  20.3 us
    dot_general x4, matrix products, dot(): return jnp.dot(left, right, preferred_element_type=F32)  16.7 us
  transfers between devices with their start and end apart: 3, of which 0 were waited for; matrix products, arithmetic and copies ran while one was open for 13% of the time, Pallas kernels for 17%

profile of v2, /device:TPU:0, one launch (start us, length us, event | category | flops | bytes accessed | tf_op | source)
XLA Modules:
  0.0 467.8 jit_solution(14000812679425021771)
XLA Ops:
  7.3 1.7 copy.46
  9.0 0.8 copy.47.attend_ref
  9.8 1.2 copy.49
  11.1 0.6 concatenate.4.norms_ref
  11.7 61.2 %shard_map.345 = (bf16[8,256,1024]{2,1,0:T(8,128)(2,1)}, bf16[4,256,384]{2,1,0:T(8,128)(2,1)}, f32[4,8,256]{2,1,0:T(8,128)}, bf16[1024,1024]{1,0:T(8,128)(2,1)}) custom-call(bf16[256,1024]{1,0:T(8,128)(2,1)} %bitcast.85, bf16[256,384]{1,0:T(8,128)(2,1)} %copy.47.attend_ref, f32[8,256]{1,0:T(8,128)} %concatenate.4.norms_ref, bf16[256,4096]{1,0:T(8,128)(2,1)} %expand_ref.1), custom_call_target="tpu_custom_call" | custom-call | tf_op jit(solution)/shard_map/pallas_call | solution.py:72
  73.0 0.7 all-gather.6.cloned.1.call-update
  73.7 0.7 all-gather.8.cloned.1.call-update
  74.4 1.0 fusion.32
  75.4 3.8 convert_reduce_fusion
  79.3 1.4 multiply_reduce_fusion
  80.7 0.6 select_reduce_fusion.slot_ref
  81.4 1.7 add_convert_fusion
  83.1 3.6 convolution_convert_fusion.qkv_ref
  86.7 20.3 %shard_map.346 = (bf16[2048,128]{1,0:T(8,128)(2,1)}, f32[128,2048]{1,0:T(8,128)}, f32[8,2048]{1,0:T(8,128)}) custom-call(s32[16]{0:T(128)} %select_reduce_fusion.slot_ref, s32[16]{0:T(128)} %bitcast.120, bf16[2048,384]{1,0:T(8,128)(2,1)} %convolution_convert_fusion.qkv_ref), custom_call_target="tpu_custom_call" | custom-call | flops 2147483648 | bytes 2621440 | tf_op jit(solution)/shard_map/pallas_call | solution.py:790
  106.9 12.5 %shard_map.347 = bf16[256,1024]{1,0:T(8,128)(2,1)} custom-call(bf16[8,256,128]{2,1,0:T(8,128)(2,1)} %bitcast.101), custom_call_target="tpu_custom_call" | custom-call | tf_op jit(solution)/shard_map/pallas_call | solution.py:72
  119.7 0.3 fusion.18
  120.0 4.9 %fusion.3 = bf16[2048,1024]{1,0:T(8,128)(2,1)} fusion(bf16[8,256,1024]{2,1,0:T(8,128)(2,1)} %get-tuple-element.46, f32[1024]{0:T(1024)S(1)} %bitcast.111, f32[1024]{0:T(1024)S(1)} %bitcast.104, f32[2048]{0:T(1024)S(1)} %bitcast.113, f32[2048]{0:T(1024)S(1)} %bitcast.112), kind=kLoop, calls=%fused_computation.4 | loop fusion | flops 12582912 | bytes 8413184 | tf_op jit(solution)/shard_map/convert_element_type | solution.py:1201
  124.9 2.7 fusion.33
  127.8 1.1 add_convert_fusion.2.x_ref
  128.9 25.9 %shard_map.348 = bf16[4,256,1024]{2,1,0:T(8,128)(2,1)} custom-call(bf16[256,1024]{1,0:T(8,128)(2,1)} %add_convert_fusion.2.x_ref), custom_call_target="tpu_custom_call" | custom-call | tf_op jit(solution)/shard_map/pallas_call | solution.py:72
  154.8 6.6 %fusion.34 = f32[1024,1024]{1,0:T(8,128)} fusion(bf16[1024,1024]{1,0:T(8,128)(2,1)} %bitcast.91, bf16[1024,1024]{1,0:T(8,128)(2,1)} %get-tuple-element.54), kind=kOutput, calls=%fused_computation.87 | convolution fusion | flops 2147483648 | bytes 8388608 | tf_op jit(solution)/shard_map/dot_general | solution.py:30
  161.4 7.7 %multiply_convert_fusion.1 = bf16[1024,1024]{1,0:T(8,128)(2,1)S(1)} fusion(f32[1024,1024]{1,0:T(8,128)} %fusion.34, bf16[1024,1024]{1,0:T(8,128)(2,1)} %all-gather.6.cloned.1.call-done, bf16[1024,1024]{1,0:T(8,128)(2,1)} %param.24), kind=kOutput, calls=%fused_computation.18 | convolution fusion | flops 2168455168 | bytes 10485760 | tf_op jit(solution)/shard_map/dot_general | solution.py:1212
  169.1 3.7 convolution_convert_fusion.5
  172.8 18.7 %shard_map.349 = f32[256,1024]{1,0:T(8,128)} custom-call(bf16[4,256,1024]{2,1,0:T(8,128)(2,1)} %bitcast.94), custom_call_target="tpu_custom_call" | custom-call | tf_op jit(solution)/shard_map/pallas_call | solution.py:72
  191.5 1.7 multiply_reduce_fusion.1
  193.3 1.9 multiply_add_fusion.4
  195.2 2.1 convolution_convert_fusion.4
  197.3 1.6 convolution_convert_fusion.7.mixed_ref
  198.9 4.3 convolution_convert_fusion.1
  203.2 4.0 convolution_convert_fusion.3
  207.1 4.1 convolution_convert_fusion.2
  211.2 109.5 %shard_map.350 = (bf16[2048,384]{1,0:T(8,128)(2,1)}, bf16[256,3072]{1,0:T(8,128)(2,1)}, bf16[256,1024]{1,0:T(8,128)(2,1)}, f32[256,1024]{1,0:T(8,128)}, bf16[256,1024]{1,0:T(8,128)(2,1)}) custom-call(s32[16]{0:T(128)} %select_reduce_fusion.slot_ref, s32[16]{0:T(128)} %bitcast.121, bf16[2048,384]{1,0:T(8,128)(2,1)} %convolution_convert_fusion.qkv_ref, ...), custom_call_target="tpu_custom_call" | custom-call | tf_op jit(solution)/shard_map/pallas_call | solution.py:1094
  320.7 2.1 fusion.20
  322.8 6.4 %fusion.17 = (f32[1024]{0:T(1024)S(1)}, f32[256]{0:T(256)S(1)}, f32[256]{0:T(256)S(1)}, f32[1024]{0:T(1024)S(1)}, f32[256,1024]{1,0:T(8,128)}) fusion(f32[256]{0:T(256)S(1)} %add_rsqrt_fusion.1, f32[256]{0:T(256)S(1)} %broadcast_multiply_fusion.3, bf16[1,256,1024]{2,1,0:T(8,128)(2,1)S(1)} %copy-done.1, f32[1024]{0:T(1024)S(1)} %bitcast.105, ...), kind=kOutput, calls=%fused_computation.48 | convolution fusion | flops 1613231616 | bytes 9453568 | tf_op jit(solution)/shard_map/dot_general | solution.py:1248
  329.2 0.8 fusion.31
  330.0 3.3 convolution_convert_fusion.6
  333.3 0.7 stack.23
  334.0 92.9 %shard_map.351 = (bf16[256,3072]{1,0:T(8,128)(2,1)}, bf16[256,1024]{1,0:T(8,128)(2,1)}, f32[8,8,256]{2,1,0:T(8,128)}, bf16[8,128,1024]{2,1,0:T(8,128)(2,1)}, bf16[8,32,4096]{2,1,0:T(8,128)(2,1)}) custom-call(bf16[4,256,384]{2,1,0:T(8,128)(2,1)} %bitcast.99, bf16[256,1024]{1,0:T(8,128)(2,1)} %get-tuple-element.61.mixing_ref, f32[4,8,256]{2,1,0:T(8,128)} %bitcast.102, ...), custom_call_target="tpu_custom_call" | custom-call | tf_op jit(solution)/shard_map/pallas_call | solution.py:651
  426.9 0.9 reduce_sum.159
  427.8 2.7 fusion.16
  430.5 0.6 add_multiply_fusion.5
  431.2 3.7 add_multiply_fusion.4
  434.9 7.1 %add_multiply_fusion.3 = (f32[256,3072]{1,0:T(8,128)}, f32[256,3072]{1,0:T(8,128)}, f32[256,3072]{1,0:T(8,128)}, f32[256,3072]{1,0:T(8,128)}) fusion(bf16[256,3072]{1,0:T(8,128)(2,1)S(1)} %copy-done.4, f32[256,3072]{1,0:T(8,128)S(1)} %copy-done.11, f32[256,3072]{1,0:T(8,128)S(1)} %copy-done.12, bf16[256,3072]{1,0:T(8,128)(2,1)S(1)} %copy-done.19), kind=kLoop, calls=%fused_computation.22 | loop fusion | flops 12582912 | bytes 22020096 | tf_op jit(solution)/shard_map/mul | solution.py:63
  442.0 1.2 copy-done.7
  443.2 0.6 copy-done.16
  443.8 9.0 %add_multiply_fusion.1 = (f32[256,4096]{1,0:T(8,128)}, f32[256,4096]{1,0:T(8,128)}, f32[256,4096]{1,0:T(8,128)}, f32[256,4096]{1,0:T(8,128)}) fusion(bf16[256,4096]{1,0:T(8,128)(2,1)S(1)} %copy-done.2, f32[256,4096]{1,0:T(8,128)S(1)} %copy-done.6, f32[256,4096]{1,0:T(8,128)S(1)} %copy-done.7, bf16[8,32,4096]{2,1,0:T(8,128)(2,1)S(1)} %copy-done.16), kind=kLoop, calls=%fused_computation.15 | loop fusion | flops 16777216 | bytes 29360128 | tf_op jit(solution)/shard_map/mul | solution.py:63
  453.0 1.2 copy-done.15
  454.2 6.9 %add_multiply_fusion = (f32[1024,1024]{1,0:T(8,128)}, f32[1024,1024]{1,0:T(8,128)}, f32[1024,1024]{1,0:T(8,128)}, f32[1024,1024]{1,0:T(8,128)}) fusion(bf16[1024,1024]{1,0:T(8,128)(2,1)S(1)} %copy-done.14, f32[1024,1024]{1,0:T(8,128)S(1)} %copy-done.8, f32[1024,1024]{1,0:T(8,128)S(1)} %copy-done.9, bf16[8,128,1024]{2,1,0:T(8,128)(2,1)S(1)} %copy-done.15), kind=kLoop, calls=%fused_computation.13 | loop fusion | flops 16777216 | bytes 29360128 | tf_op jit(solution)/shard_map/mul | solution.py:63
  (87 shorter events, 0.9 us)
Async XLA Ops:
  7.2 3.9 copy-start.23
  7.2 117.7 %all-gather.4.cloned.1.call-start = ((), (), s32[]{:S(2)}) async-start(), calls=%async_computation | async-start | bytes 2621440 | tf_op jit(solution)/shard_map/all_gather | solution.py:1196
  72.9 88.4 %all-gather.6.cloned.1.call-start = ((), (), s32[]{:S(2)}) async-start(), calls=%async_computation.1 | async-start | bytes 2621440 | tf_op jit(solution)/shard_map/all_gather | solution.py:1197
  73.7 137.5 %all-gather.8.cloned.1.call-start = ((), (), s32[]{:S(2)}) async-start(), calls=%async_computation.2 | async-start | bytes 7864320 | tf_op jit(solution)/shard_map/all_gather | solution.py:1198
  74.4 4.9 %copy-start = (bf16[8,256,1024]{2,1,0:T(8,128)(2,1)S(1)}, bf16[8,256,1024]{2,1,0:T(8,128)(2,1)}, u32[]{:S(2)}) copy-start(bf16[8,256,1024]{2,1,0:T(8,128)(2,1)} %get-tuple-element.46) | copy-start | bytes 12582916
  75.4 5.3 %copy-start.26 = (s32[1,16]{1,0:T(1,128)S(1)}, s32[1,16]{1,0:T(1,128)}, u32[]{:S(2)}) copy-start(s32[1,16]{1,0:T(1,128)} %param.20) | copy-start | bytes 196
  81.4 1.7 copy-start.30
  86.7 32.8 %copy-start.1 = (bf16[1,256,1024]{2,1,0:T(8,128)(2,1)S(1)}, bf16[1,256,1024]{2,1,0:T(8,128)(2,1)}, u32[]{:S(2)}) copy-start(bf16[1,256,1024]{2,1,0:T(8,128)(2,1)} %param.18) | copy-start | bytes 1572868
  119.9 4.9 %copy-start.5 = (bf16[256,1024]{1,0:T(8,128)(2,1)S(1)}, bf16[256,1024]{1,0:T(8,128)(2,1)}, u32[]{:S(2)}) copy-start(bf16[256,1024]{1,0:T(8,128)(2,1)} %shard_map.347) | copy-start | bytes 1572868
  161.4 7.7 %copy-start.28 = (bf16[1024,1024]{1,0:T(8,128)(2,1)S(1)}, bf16[1024,1024]{1,0:T(8,128)(2,1)}, u32[]{:S(2)}) copy-start(bf16[1024,1024]{1,0:T(8,128)(2,1)} %get-tuple-element.54) | copy-start | bytes 6291460
  169.1 3.7 copy-start.32
  193.3 4.0 copy-start.3
  195.2 3.7 copy-start.18
  195.2 3.7 copy-start.33
  198.8 4.3 copy-start.13
  198.8 4.3 copy-start.31
  203.2 4.0 copy-start.27
  322.8 6.4 %copy-start.22 = (bf16[256,1024]{1,0:T(8,128)(2,1)S(1)}, bf16[256,1024]{1,0:T(8,128)(2,1)}, u32[]{:S(2)}) copy-start(bf16[256,1024]{1,0:T(8,128)(2,1)} %get-tuple-element.62) | copy-start | bytes 1572868
  322.8 7.2 %copy-start.10 = (bf16[2048,1024]{1,0:T(8,128)(2,1)S(1)}, bf16[2048,1024]{1,0:T(8,128)(2,1)}, u32[]{:S(2)}) copy-start(bf16[2048,1024]{1,0:T(8,128)(2,1)} %fusion.3) | copy-start | bytes 12582916
  322.8 7.2 %copy-start.29 = (bf16[2048,384]{1,0:T(8,128)(2,1)S(1)}, bf16[2048,384]{1,0:T(8,128)(2,1)}, u32[]{:S(2)}) copy-start(bf16[2048,384]{1,0:T(8,128)(2,1)} %get-tuple-element.60) | copy-start | bytes 4718596
  333.3 97.2 %copy-start.24 = (f32[4,256]{1,0:T(4,128)S(1)}, f32[4,256]{1,0:T(4,128)}, u32[]{:S(2)}) copy-start(f32[4,256]{1,0:T(4,128)} %param.30) | copy-start | bytes 12292
  333.3 97.2 %copy-start.25 = (f32[4,256]{1,0:T(4,128)S(1)}, f32[4,256]{1,0:T(4,128)}, u32[]{:S(2)}) copy-start(f32[4,256]{1,0:T(4,128)} %param.35) | copy-start | bytes 12292
  333.3 97.8 %copy-start.17 = (bf16[256,1024]{1,0:T(8,128)(2,1)S(1)}, bf16[256,1024]{1,0:T(8,128)(2,1)}, u32[]{:S(2)}) copy-start(bf16[256,1024]{1,0:T(8,128)(2,1)} %param.22) | copy-start | bytes 1572868
  333.3 97.8 %copy-start.20 = (f32[256,1024]{1,0:T(8,128)S(1)}, f32[256,1024]{1,0:T(8,128)}, u32[]{:S(2)}) copy-start(f32[256,1024]{1,0:T(8,128)} %param.27) | copy-start | bytes 3145732
  427.8 3.4 copy-start.21
  427.8 7.1 %copy-start.12 = (f32[256,3072]{1,0:T(8,128)S(1)}, f32[256,3072]{1,0:T(8,128)}, u32[]{:S(2)}) copy-start(f32[256,3072]{1,0:T(8,128)} %param.31) | copy-start | bytes 9437188
  430.5 4.3 copy-start.4
  430.5 4.3 copy-start.11
  430.5 4.3 copy-start.19
  434.9 7.2 %copy-start.2 = (bf16[256,4096]{1,0:T(8,128)(2,1)S(1)}, bf16[256,4096]{1,0:T(8,128)(2,1)}, u32[]{:S(2)}) copy-start(bf16[256,4096]{1,0:T(8,128)(2,1)} %expand_ref.1) | copy-start | bytes 6291460
  434.9 7.2 %copy-start.6 = (f32[256,4096]{1,0:T(8,128)S(1)}, f32[256,4096]{1,0:T(8,128)}, u32[]{:S(2)}) copy-start(f32[256,4096]{1,0:T(8,128)} %param.28) | copy-start | bytes 12582916
  434.9 8.3 %copy-start.7 = (f32[256,4096]{1,0:T(8,128)S(1)}, f32[256,4096]{1,0:T(8,128)}, u32[]{:S(2)}) copy-start(f32[256,4096]{1,0:T(8,128)} %param.33) | copy-start | bytes 12582916
  434.9 8.9 %copy-start.16 = (bf16[8,32,4096]{2,1,0:T(8,128)(2,1)S(1)}, bf16[8,32,4096]{2,1,0:T(8,128)(2,1)}, u32[]{:S(2)}) copy-start(bf16[8,32,4096]{2,1,0:T(8,128)(2,1)} %get-tuple-element.65) | copy-start | bytes 6291460
  443.8 9.0 %copy-start.8 = (f32[1024,1024]{1,0:T(8,128)S(1)}, f32[1024,1024]{1,0:T(8,128)}, u32[]{:S(2)}) copy-start(f32[1024,1024]{1,0:T(8,128)} %param.29) | copy-start | bytes 12582916
  443.8 9.0 %copy-start.9 = (f32[1024,1024]{1,0:T(8,128)S(1)}, f32[1024,1024]{1,0:T(8,128)}, u32[]{:S(2)}) copy-start(f32[1024,1024]{1,0:T(8,128)} %param.34) | copy-start | bytes 12582916
  443.8 9.2 %copy-start.14 = (bf16[1024,1024]{1,0:T(8,128)(2,1)S(1)}, bf16[1024,1024]{1,0:T(8,128)(2,1)}, u32[]{:S(2)}) copy-start(bf16[1024,1024]{1,0:T(8,128)(2,1)} %param.24) | copy-start | bytes 6291460
  443.8 10.4 %copy-start.15 = (bf16[8,128,1024]{2,1,0:T(8,128)(2,1)S(1)}, bf16[8,128,1024]{2,1,0:T(8,128)(2,1)}, u32[]{:S(2)}) copy-start(bf16[8,128,1024]{2,1,0:T(8,128)(2,1)} %get-tuple-element.66) | copy-start | bytes 6291460
Sparse Core Ops, SparseCore 0:
  73.1 19.0 all-gather.3
  93.7 22.6 all-gather.5
  118.6 57.5 all-gather.7

commit v3 on v2

v3 whole, which is shorter than its diff:
```python
import functools
import math

import jax
import jax.numpy as jnp
from jax import lax
from jax.experimental import pallas as pl
from jax.experimental.pallas import tpu as pltpu
from jax.sharding import PartitionSpec as P

HD = 64
STEP_COUNT = 10
EPS_NORM = 1e-05
NEG = -1e30
BETA_ONE = 0.9
BETA_TWO = 0.999
LEARN = 0.02
DECAY = 0.1
EPS_ADAM = 1e-08
CUBIC = 0.044715
ROOT_TWO_PI = math.sqrt(2.0 / math.pi)
LOG2E = math.log2(math.e)
TILE = 256
VMEM_LIMIT = 58 * 2**20
MESH = pl.DeviceIdType.MESH
F32 = jnp.float32
BF16 = jnp.bfloat16


def dot(left, right):
    return jnp.dot(left, right, preferred_element_type=F32)


def norm_parts(values):
    center = values - jnp.mean(values, axis=-1, keepdims=True)
    spread = jnp.mean(center * center, axis=-1, keepdims=True)
    inverse = lax.rsqrt(spread + EPS_NORM)
    return center * inverse, inverse


def norm_back(err, gain, normal, inverse):
    scaled = err * gain
    first = jnp.mean(scaled, axis=-1, keepdims=True)
    second = jnp.mean(scaled * normal, axis=-1, keepdims=True)
    return inverse * (scaled - first - normal * second)


def gelu_and_slope(values):
    square = values * values
    inner = ROOT_TWO_PI * values * (1.0 + CUBIC * square)
    tanh = jnp.tanh(inner)
    half = 0.5 * (1.0 + tanh)
    slope = half + 0.5 * values * (1.0 - tanh * tanh) * ROOT_TWO_PI * (
        1.0 + 3.0 * CUBIC * square
    )
    return values * half, slope


def adam_step(weight, grad, first, second):
    first_new = BETA_ONE * first + (1.0 - BETA_ONE) * grad
    second_new = BETA_TWO * second + (1.0 - BETA_TWO) * grad * grad
    mean_hat = first_new / (1.0 - BETA_ONE**STEP_COUNT)
    square_hat = second_new / (1.0 - BETA_TWO**STEP_COUNT)
    update = -LEARN * (
        mean_hat / (jnp.sqrt(square_hat) + EPS_ADAM) + DECAY * weight.astype(F32)
    )
    return (update, first_new, second_new)


def comm_call(kernel, out_shape, scratch, ident, operands, any_space=True):
    space = pl.ANY if any_space else pltpu.VMEM
    outs = jax.tree.map(lambda _: pl.BlockSpec(memory_space=space), out_shape)
    return pl.pallas_call(
        kernel,
        out_shape=out_shape,
        in_specs=[pl.BlockSpec(memory_space=space)] * len(operands),
        out_specs=outs,
        scratch_shapes=scratch,
        compiler_params=pltpu.CompilerParams(collective_id=ident, has_side_effects=True),
    )(*operands)


def remote(src, dst, send, recv, device):
    return pltpu.make_async_remote_copy(
        src_ref=src,
        dst_ref=dst,
        send_sem=send,
        recv_sem=recv,
        device_id=device,
        device_id_type=MESH,
    )


def fsdp_partners():
    f, c = lax.axis_index("fsdp"), lax.axis_index("ctx")
    x, k = f // 2, f % 2
    return f, c, x, k, x * 2 + 1 - k, (1 - x) * 2 + k


def greet(devices):
    barrier = pltpu.get_barrier_semaphore()
    for device in devices:
        pl.semaphore_signal(barrier, inc=1, device_id=device, device_id_type=MESH)
    pl.semaphore_wait(barrier, len(devices))


CHUNKS = 4


class Pieces:
    def __init__(self, send_sems, recv_sems):
        self.send_sems, self.recv_sems, self.used = send_sems, recv_sems, 0

    def copy(self, src, dst, device):
        n = self.used
        self.used += 1
        return remote(src, dst, self.send_sems.at[n], self.recv_sems.at[n], device)


def row_parts(rows, count):
    step = rows // count
    return [pl.ds(t * step, step) for t in range(count)]


class FsdpGather:
    def __init__(self, pieces, x_ref, o_ref, local_sem, chunks=CHUNKS):
        f, c, x, k, mate, across = fsdp_partners()
        self.parts = row_parts(x_ref.shape[0], chunks)
        self.local = pltpu.make_async_copy(x_ref, o_ref.at[f], local_sem)
        self.far = [
            pieces.copy(x_ref.at[p], o_ref.at[f, p], (across, c)) for p in self.parts
        ]
        self.near = pieces.copy(x_ref, o_ref.at[f], (mate, c))
        self.passed = [
            pieces.copy(o_ref.at[across, p], o_ref.at[across, p], (mate, c))
            for p in self.parts
        ]

    def start(self):
        for copy in self.far:
            copy.start()
        self.near.start()
        self.local.start()

    def forward(self):
        for copy, onward in zip(self.far, self.passed):
            copy.wait_recv()
            onward.start()

    def finish(self):
        self.local.wait()
        self.near.wait()
        for copy, onward in zip(self.far, self.passed):
            copy.wait_send()
            onward.wait()


class FsdpScatter:
    def __init__(self, pieces, x_ref, near_buf, far_out, far_in, chunks=CHUNKS):
        f, c, x, k, mate, across = fsdp_partners()
        self.parts = row_parts(x_ref.shape[1], chunks)
        self.x_ref, self.near_buf, self.far_out, self.far_in = x_ref, near_buf, far_out, far_in
        self.f, self.across = f, across
        away_mate = (1 - x) * 2 + 1 - k
        self.near_far = [
            pieces.copy(x_ref.at[away_mate, p], near_buf.at[0, p], (mate, c))
            for p in self.parts
        ]
        self.near_own = pieces.copy(x_ref.at[mate], near_buf.at[1], (mate, c))
        self.far = [pieces.copy(far_out.at[p], far_in.at[p], (across, c)) for p in self.parts]

    def start(self):
        for copy in self.near_far:
            copy.start()
        self.near_own.start()

    def forward(self):
        for p, near, far in zip(self.parts, self.near_far, self.far):
            near.wait_recv()
            self.far_out[p] = (
                self.x_ref[self.across, p].astype(F32) + self.near_buf[0, p].astype(F32)
            ).astype(BF16)
            far.start()

    def finish(self, store):
        self.near_own.wait_recv()
        for p, far in zip(self.parts, self.far):
            far.wait_recv()
            store(
                p,
                self.x_ref[self.f, p].astype(F32)
                + self.near_buf[1, p].astype(F32)
                + self.far_in[p].astype(F32),
            )
        self.near_own.wait_send()
        for near, far in zip(self.near_far, self.far):
            near.wait_send()
            far.wait_send()


class CtxGather:
    def __init__(self, x_ref, o_ref, local_sem, send_sem, recv_sem):
        f, c = lax.axis_index("fsdp"), lax.axis_index("ctx")
        self.f, self.c, self.z, self.y = f, c, c // 2, c % 2
        self.depth = o_ref.shape[0] // 2
        self.mate = self.z * 2 + 1 - self.y
        rows = x_ref.shape[0]
        some = rows * 7 // 16 // 8 * 8
        if some >= 32:
            self.parts = [pl.ds(0, some), pl.ds(some, some), pl.ds(2 * some, rows - 2 * some)]
            self.direct, self.turned = (0, 1), (2,)
        elif rows > 8:
            self.parts = [pl.ds(0, rows * 3 // 4), pl.ds(rows * 3 // 4, rows // 4)]
            self.direct, self.turned = (0,), (1,)
        else:
            self.parts = [pl.ds(0, rows)]
            self.direct, self.turned = (), (0,)
        self.x_ref, self.o_ref, self.send_sem, self.recv_sem = x_ref, o_ref, send_sem, recv_sem
        self.local = pltpu.make_async_copy(x_ref, o_ref.at[c], local_sem)

    @staticmethod
    def semaphores(n):
        return [
            pltpu.SemaphoreType.DMA,
            pltpu.SemaphoreType.DMA((n, 3, 3)),
            pltpu.SemaphoreType.DMA((n, 3)),
        ]

    def copy(self, zz, yy, part, way, own=False):
        block = zz * 2 + yy
        src = self.x_ref.at[self.parts[part]] if own else self.o_ref.at[block, self.parts[part]]
        there = (self.c - 2, self.c + 2, self.mate)[way]
        return remote(
            src,
            self.o_ref.at[block, self.parts[part]],
            self.send_sem.at[block, part, way],
            self.recv_sem.at[block, part],
            (self.f, there),
        )

    def both_ways(self, zz, yy, part, own=False):
        pl.when(self.z < self.depth - 1)(lambda: self.copy(zz, yy, part, 1, own).start())
        pl.when(self.z > 0)(lambda: self.copy(zz, yy, part, 0, own).start())

    def start(self):
        z, y = self.z, self.y
        for part in self.turned:
            self.copy(z, y, part, 2, True).start()
        for part in self.direct:
            self.both_ways(z, y, part, True)
            self.copy(z, y, part, 2, True).start()
        for part in self.turned:
            self.both_ways(z, y, part, True)
        self.local.start()

    def arrive(self, zz, yy, part, way):
        self.copy(zz, yy, part, way).wait_recv()
        if way == 1:
            pl.when(self.z < self.depth - 1)(lambda: self.copy(zz, yy, part, 1).start())
        else:
            pl.when(self.z > 0)(lambda: self.copy(zz, yy, part, 0).start())
        if part in self.direct:
            self.copy(zz, yy, part, 2).start()

    def along(self, step, yy, part):
        z = self.z
        pl.when(z - step >= 0)(lambda: self.arrive(z - step, yy, part, 1))
        pl.when(z + step < self.depth)(lambda: self.arrive(z + step, yy, part, 0))

    def step(self, step):
        z, y = self.z, self.y

        for part in self.direct:
            self.along(step, y, part)
        for part in self.turned:
            self.along(step, y, part)

            @pl.when(step == 1)
            def _():
                self.copy(z, 1 - y, part, 2).wait_recv()
                self.both_ways(z, 1 - y, part)

            self.along(step, 1 - y, part)

    def other(self, zz):
        for part in self.direct:
            self.copy(zz, 1 - self.y, part, 2).wait_recv()

    def others(self):
        z = self.z
        self.local.wait()
        self.other(z)
        for step in range(1, self.depth):
            pl.when(z - step >= 0)(lambda: self.other(z - step))
            pl.when(z + step < self.depth)(lambda: self.other(z + step))

    def sent(self):
        z, y, depth = self.z, self.y, self.depth
        blocks = [(y, part) for part in self.direct]
        for part in self.turned:
            blocks += [(y, part), (1 - y, part)]

        @pl.loop(0, depth)
        def _(step):
            for yy, part in blocks:

                def sent_right():
                    self.copy(z - step, yy, part, 1).wait_send()

                def sent_left():
                    self.copy(z + step, yy, part, 0).wait_send()

                pl.when((z - step >= 0) & (z < depth - 1))(sent_right)
                pl.when((z + step < depth) & (z > 0))(sent_left)

            for part in self.direct:
                pl.when((z - step >= 0) & (step > 0))(
                    lambda: self.copy(z - step, y, part, 2).wait_send()
                )
                pl.when(z + step < depth)(lambda: self.copy(z + step, y, part, 2).wait_send())

        for part in self.turned:
            self.copy(z, y, part, 2).wait_send()


def greet_lines(others, depth):
    f, c = lax.axis_index("fsdp"), lax.axis_index("ctx")
    z = c // 2
    barrier = pltpu.get_barrier_semaphore()

    def signal(device):
        pl.semaphore_signal(barrier, inc=1, device_id=device, device_id_type=MESH)

    for device in others:
        signal(device)
    pl.when(z > 0)(lambda: signal((f, c - 2)))
    pl.when(z < depth - 1)(lambda: signal((f, c + 2)))
    pl.semaphore_wait(
        barrier, len(others) + (z + depth - 1) // depth + (2 * depth - 2 - z) // depth
    )


def scatter_buffers(rows, width):
    return [
        pltpu.VMEM((2, rows, width), BF16),
        pltpu.VMEM((rows, width), BF16),
        pltpu.VMEM((rows, width), BF16),
    ]


class CtxExchange:
    def __init__(self, pieces, n, source, target, local_sems):
        f, c = lax.axis_index("fsdp"), lax.axis_index("ctx")
        self.copies = []
        for j in range(n - 1, 0, -1):
            there = (c + j) % n
            for src, dst in zip(source(there), target(c)):
                self.copies.append(pieces.copy(src, dst, (f, there)))
        self.local = [
            pltpu.make_async_copy(src, dst, sem)
            for src, dst, sem in zip(source(c), target(c), local_sems)
        ]

    def start(self):
        for copy in self.copies + self.local:
            copy.start()

    def finish(self):
        for copy in self.local + self.copies:
            copy.wait()


def greet_ctx(n, others=()):
    f, c = lax.axis_index("fsdp"), lax.axis_index("ctx")
    greet([(f, (c + j) % n) for j in range(1, n)] + list(others))


def column_block(ref, block, lanes):
    return ref.at[:, pl.ds(pl.multiple_of(block * lanes, 128), lanes)]


def ctx_to_rows(values):
    n, rows, lanes = values.shape
    moved = lax.all_to_all(values, "ctx", split_axis=0, concat_axis=0, tiled=True)
    return moved.transpose(1, 0, 2).reshape(rows, n * lanes)


def ctx_to_heads(values, n):
    rows, lanes = values.shape[0], values.shape[1] // n
    return lax.all_to_all(
        values.reshape(rows, n, lanes).transpose(1, 0, 2),
        "ctx",
        split_axis=0,
        concat_axis=0,
        tiled=True,
    )


def last_kernel(
    n, attend_ref, mixing_ref, sums_ref, shrink_ref, expand_ref, joint_ref, weight_ref,
    start_ref, gains_ref,
    attend_out, mixing_out, norms_out, shrink_out, expand_out, back_ref,
    mixing_in, norms_part, norms_in, norms_own, block, blocks, expand_own,
    joint, weight, err,
    send_sems, recv_sems, local_sems, *gather_sems,
):
    f, c, x, k, mate, across = fsdp_partners()
    lanes = mixing_in.shape[-1]
    own, wide = attend_ref.shape
    hidden = expand_ref.shape[-1]
    width = err.shape[1]
    others = [(f + j) % 4 for j in (1, 2, 3)]
    loads = [
        pltpu.make_async_copy(joint_ref, joint, local_sems.at[0]),
        pltpu.make_async_copy(weight_ref, weight, local_sems.at[1]),
    ]
    for copy in loads:
        copy.start()
    greet_ctx(n, [(o, c) for o in others])
    pieces = Pieces(send_sems, recv_sems)
    sems = [gather_sems[3 * j : 3 * j + 3] for j in range(4)]

    def columns(j):
        return expand_own.at[:, pl.ds(pl.multiple_of(j * hidden, 128), hidden)]

    early = [pieces.copy(expand_ref.at[o], columns(f), (o, c)) for o in others]
    early += [pltpu.make_async_copy(expand_ref.at[f], columns(f), local_sems.at[2])]
    move = CtxExchange(
        pieces,
        n,
        lambda j: [column_block(mixing_ref, j, lanes)],
        lambda j: [mixing_in.at[j]],
        [local_sems.at[3]],
    )
    for copy in early:
        copy.start()
    move.start()
    shrink = CtxGather(shrink_ref, shrink_out, *sems[0])
    expand = CtxGather(expand_own, expand_out, *sems[1])
    small = CtxGather(norms_own, norms_out, *sems[2])
    gather = CtxGather(block, blocks, *sems[3])
    shrink.start()
    for copy in early:
        copy.wait()
    expand.start()
    for copy in loads:
        copy.wait()
    shrink.step(1)

    def multiply(first, last):
        @pl.loop(first, last)
        def _(j):
            cols = pl.ds(pl.multiple_of(j * TILE, TILE), TILE)
            err[:, cols] = dot_last(joint[...], weight[cols, :])

    multiply(0, width // TILE // 2)
    expand.step(1)
    move.finish()
    total = mixing_in[0].astype(F32)
    for j in range(1, n):
        total += mixing_in[j].astype(F32)
    block[:, wide:] = total.astype(BF16)
    block[:, :wide] = attend_ref[...]
    gather.start()
    shrink.step(2)
    multiply(width // TILE // 2, width // TILE)
    expand.step(2)
    sums = [jnp.zeros((1, width), F32)] * 2
    for t in range(err.shape[0] // 64):
        part = slice(t * 64, (t + 1) * 64)
        one, scale = norm_parts(start_ref[part].astype(F32))
        value = err[part]
        sums[0] += jnp.sum(value * one, axis=0, keepdims=True)
        sums[1] += jnp.sum(value, axis=0, keepdims=True)
        back_ref[part] = norm_back(value, gains_ref[0:1, :], one, scale)
    for j in range(4):
        cols = slice(j * own, (j + 1) * own)
        norms_part[j] = sums_ref[:, cols]
        norms_part[j, 0:1] = sums[0][:, cols]
        norms_part[j, 1:2] = sums[1][:, cols]
    late = [pieces.copy(norms_part.at[o], norms_in.at[f], (o, c)) for o in others]
    for copy in late:
        copy.start()
    norms_in[f] = norms_part[f]
    gather.step(1)
    for copy in late:
        copy.wait()
    norms_own[...] = norms_in[0] + norms_in[1] + norms_in[2] + norms_in[3]
    small.start()
    shrink.step(3)
    expand.step(3)
    small.step(1)
    gather.step(2)
    small.step(2)
    gather.step(3)
    small.step(3)
    for each in (gather, small, shrink, expand):
        each.others()
    for j in range(n):
        for part in range(3):
            at = (part * n + j) * lanes
            attend_out[:, at : at + lanes] = blocks[j, :, part * lanes : (part + 1) * lanes]
        mixing_out[:, j * lanes : (j + 1) * lanes] = blocks[j, :, wide:]
    for each in (shrink, expand, small, gather):
        each.sent()


def last_exchange(
    own_attend, own_mixing, norm_sums, shrink_piece, expand_piece, joint, whole_attend, start,
    norms, sizes,
):
    fsdp, n = sizes
    own, wide = own_attend.shape
    rows, width = start.shape
    lanes = width // n
    _, piece, hidden = expand_piece.shape
    if sizes != (4, 8):
        attend = (
            lax.all_gather(own_attend, "ctx", axis=0, tiled=False)
            .reshape(n, own, 3, lanes)
            .transpose(1, 2, 0, 3)
            .reshape(own, 3 * width)
        )
        err = dot_last(joint, whole_attend)
        one, scale = norm_parts(start.astype(F32))
        sums = jnp.concatenate(
            [jnp.sum(err * one, axis=0)[None], jnp.sum(err, axis=0)[None], norm_sums[2:]], axis=0
        )
        parts = lax.psum_scatter(
            sums.reshape(8, fsdp, own).transpose(1, 0, 2),
            "fsdp",
            scatter_dimension=0,
            tiled=False,
        )
        expand = lax.all_to_all(expand_piece, "fsdp", split_axis=0, concat_axis=0, tiled=True)
        expand = expand.transpose(1, 0, 2).reshape(piece, fsdp * hidden)
        return (
            attend,
            lax.psum(own_mixing, "ctx"),
            lax.all_gather(parts, "ctx", axis=0, tiled=False),
            lax.all_gather(shrink_piece, "ctx", axis=0, tiled=True),
            lax.all_gather(expand, "ctx", axis=0, tiled=True),
            norm_back(err, norms[0], one, scale),
        )
    count = n - 1 + 6
    vmem, anywhere = pl.BlockSpec(memory_space=pltpu.VMEM), pl.BlockSpec(memory_space=pl.ANY)
    attend, mixing, parts, shrink, expand, back = pl.pallas_call(
        functools.partial(last_kernel, n),
        out_shape=(
            jax.ShapeDtypeStruct((own, 3 * width), BF16),
            jax.ShapeDtypeStruct((own, width), BF16),
            jax.ShapeDtypeStruct((n, 8, own), F32),
            jax.ShapeDtypeStruct((n,) + shrink_piece.shape, BF16),
            jax.ShapeDtypeStruct((n, piece, fsdp * hidden), BF16),
            jax.ShapeDtypeStruct((rows, width), F32),
        ),
        in_specs=[vmem, vmem, vmem] + [anywhere] * 4 + [vmem] * 2,
        out_specs=(vmem, vmem, vmem, anywhere, anywhere, vmem),
        scratch_shapes=[
            pltpu.VMEM((n, own, lanes), BF16),
            pltpu.VMEM((fsdp, 8, own), F32),
            pltpu.VMEM((fsdp, 8, own), F32),
            pltpu.VMEM((8, own), F32),
            pltpu.VMEM((own, wide + lanes), BF16),
            pltpu.VMEM((n, own, wide + lanes), BF16),
            pltpu.VMEM((piece, fsdp * hidden), BF16),
            pltpu.VMEM((rows, 3 * width), BF16),
            pltpu.VMEM((width, 3 * width), BF16),
            pltpu.VMEM((rows, width), F32),
            pltpu.SemaphoreType.DMA((count,)),
            pltpu.SemaphoreType.DMA((count,)),
            pltpu.SemaphoreType.DMA((4,)),
        ]
        + CtxGather.semaphores(n) * 4,
        compiler_params=pltpu.CompilerParams(
            collective_id=7, has_side_effects=True, vmem_limit_bytes=VMEM_LIMIT
        ),
    )(
        own_attend, own_mixing, norm_sums, shrink_piece, expand_piece, joint, whole_attend,
        start, norms,
    )
    return (
        attend,
        mixing,
        parts,
        shrink.reshape(n * shrink_piece.shape[0], width),
        expand.reshape(n * piece, fsdp * hidden),
        back,
    )


def head_rows(h):
    return slice(h * HD, (h + 1) * HD)


def attend_forward_kernel(
    heads, slot_ref, place_ref, qkv_ref, mixed_ref, out_t_ref, total_ref,
    q_pos, k_pos, v_pos, q_t, v_t, scores, o_pos,
):
    length, lanes = q_pos.shape
    blocks = slot_ref.shape[0]
    size = length // blocks
    tiles = length // TILE
    factor = LOG2E / math.sqrt(HD)
    for p in range(blocks):
        rows = qkv_ref[pl.ds(slot_ref[p] * size, size), :]
        here = slice(p * size, (p + 1) * size)
        q_pos[here, :] = rows[:, :lanes]
        k_pos[here, :] = rows[:, lanes : 2 * lanes]
        v_pos[here, :] = rows[:, 2 * lanes :]
    for t in range(tiles):
        here = slice(t * TILE, (t + 1) * TILE)
        q_t[:, here] = q_pos[here, :].T
        v_t[:, here] = v_pos[here, :].T
    head_of_row = lax.broadcasted_iota(jnp.int32, (lanes, TILE), 0) // HD
    allowed = lax.broadcasted_iota(jnp.int32, (TILE, TILE), 0) <= lax.broadcasted_iota(
        jnp.int32, (TILE, TILE), 1
    )

    def fold_max(values):
        return jnp.max(values.reshape(TILE // 8, 8, TILE), axis=0)

    def fold_sum(values):
        return jnp.sum(values.reshape(TILE // 8, 8, TILE), axis=0)

    @pl.loop(0, tiles)
    def _(i):
        here = pl.ds(pl.multiple_of(i * TILE, TILE), TILE)
        q_tile = q_t[:, here]
        q_heads = [
            jnp.where(head_of_row == h, q_tile, jnp.zeros_like(q_tile)) for h in range(heads)
        ]

        def first(j, tops):
            there = pl.ds(pl.multiple_of(j * TILE, TILE), TILE)
            keys = k_pos[there, :]
            result = []
            for h in range(heads):
                raw = dot(keys, q_heads[h])
                scores[h, there, :] = raw
                result.append(jnp.maximum(tops[h], fold_max(raw)))
            return tuple(result)

        tops = lax.fori_loop(
            0, i, first, tuple(jnp.full((8, TILE), NEG, F32) for _ in range(heads))
        )
        keys = k_pos[here, :]
        row_tops = []
        for h in range(heads):
            raw = jnp.where(allowed, dot(keys, q_heads[h]), NEG)
            scores[h, here, :] = raw
            row_tops.append(
                jnp.max(jnp.maximum(tops[h], fold_max(raw)), axis=0, keepdims=True) * factor
            )

        def second(j, state):
            there = pl.ds(pl.multiple_of(j * TILE, TILE), TILE)
            result = []
            for h in range(heads):
                sums, acc = state[h]
                probs = jnp.exp2(scores[h, there, :] * factor - row_tops[h])
                acc = acc + dot(v_t[head_rows(h), there], probs.astype(BF16))
                result.append((sums + fold_sum(probs), acc))
            return tuple(result)

        state = lax.fori_loop(
            0,
            i + 1,
            second,
            tuple(
                (jnp.zeros((8, TILE), F32), jnp.zeros((HD, TILE), F32)) for _ in range(heads)
            ),
        )
        outs = []
        for h in range(heads):
            sums, acc = state[h]
            row_sum = jnp.sum(sums, axis=0, keepdims=True)
            out = acc * (1.0 / row_sum)
            out_t_ref[head_rows(h), here] = out
            total_ref[pl.ds(h, 1), here] = row_tops[h] + jnp.log2(row_sum)
            outs.append(out)
        out = jnp.concatenate(outs, axis=0) if heads > 1 else outs[0]
        o_pos[here, :] = out.T.astype(BF16)

    for s in range(blocks):
        mixed_ref[s * size : (s + 1) * size, :] = o_pos[
            pl.ds(place_ref[s] * size, size), :
        ]


def attend_forward_scratch(length, heads):
    lanes = heads * HD
    return (
        [pltpu.VMEM((length, lanes), BF16)] * 3
        + [pltpu.VMEM((lanes, length), BF16)] * 2
        + [pltpu.VMEM((heads, length, TILE), F32), pltpu.VMEM((length, lanes), BF16)]
    )


def attend_forward(slot_of, place_of, qkv, heads):
    length = qkv.shape[0]
    lanes = heads * HD
    vmem = pl.BlockSpec(memory_space=pltpu.VMEM)
    smem = pl.BlockSpec(memory_space=pltpu.SMEM)
    return pl.pallas_call(
        functools.partial(attend_forward_kernel, heads),
        out_shape=(
            jax.ShapeDtypeStruct((length, lanes), BF16),
            jax.ShapeDtypeStruct((lanes, length), F32),
            jax.ShapeDtypeStruct((8, length), F32),
        ),
        in_specs=[smem, smem, vmem],
        out_specs=(vmem, vmem, vmem),
        scratch_shapes=attend_forward_scratch(length, heads),
        cost_estimate=pl.CostEstimate(
            flops=4 * length * length * lanes,
            bytes_accessed=10 * length * lanes,
            transcendentals=heads * length * length // 2,
        ),
    )(slot_of, place_of, qkv)


def forward_kernel(
    heads, slot_ref, place_ref, tokens_ref, attend_ref, norms_ref, expand_ref, mixing_ref, grad_ref,
    mixed_ref, out_t_ref, total_ref, qkv_ref, norms_out, normed_out, expand_out, mixing_out, grad_out,
    q_pos, k_pos, v_pos, q_t, v_t, scores, o_pos,
    tokens, attend_own, attend, normed, pick_sems, store_sem, local_sems, send_sems, recv_sems, ctx_local, ctx_send, ctx_recv,
):
    f, c, x, k, mate, across = fsdp_partners()
    n, rows, width = tokens.shape
    depth = n // 2
    z, y = c // 2, c % 2
    others = [(f + j) % 4 for j in (1, 2, 3)]
    greet_lines([(o, c) for o in others] + [(f, z * 2 + 1 - y)], depth)
    pieces = Pieces(send_sems, recv_sems)
    gather = CtxGather(tokens_ref, tokens, ctx_local, ctx_send, ctx_recv)
    gather.start()
    weights = FsdpGather(pieces, attend_own, attend, local_sems.at[0], 2)
    lanes = heads * HD
    picks = [
        pltpu.make_async_copy(
            column_block(attend_ref, part * n + c, lanes),
            attend_own.at[:, part * lanes : (part + 1) * lanes],
            pick_sems.at[part],
        )
        for part in range(3)
    ]
    for copy in picks:
        copy.start()
    for copy in picks:
        copy.wait()
    mixing = FsdpGather(pieces, mixing_ref, mixing_out, local_sems.at[1], 2)
    grads = FsdpGather(pieces, grad_ref, grad_out, local_sems.at[2], 2)
    weights.start()
    own, hidden = expand_ref.shape[0], expand_out.shape[1]
    norms = [pieces.copy(norms_ref, norms_out.at[f], (o, c)) for o in others]

    def columns(o):
        return (
            expand_ref.at[:, pl.ds(pl.multiple_of(o * hidden, 128), hidden)],
            expand_out.at[pl.ds(pl.multiple_of(f * own, 16), own)],
        )

    expands = [pieces.copy(*columns(o), (o, c)) for o in others]
    expands.append(pltpu.make_async_copy(*columns(f), local_sems.at[3]))
    for copy in norms + expands:
        copy.start()
    mixing.start()
    grads.start()
    norms_out[f] = norms_ref[...]
    for copy in norms:
        copy.wait()
    weights.forward()
    weights.finish()

    def process(block):
        @pl.loop(0, rows // 64)
        def _(t):
            part = pl.ds(pl.multiple_of(t * 64, 64), 64)
            value = norm_parts(tokens[block, part].astype(F32))[0]
            for j in range(4):
                cols = slice(j * own, (j + 1) * own)
                normed[block, part, cols] = (
                    value[:, cols] * norms_out[j, 0:1] + norms_out[j, 1:2]
                ).astype(BF16)

        at = pl.ds(pl.multiple_of(block * rows, 128), rows)
        qkv_ref[at] = dot(normed[block], attend[...].reshape(width, attend.shape[-1])).astype(BF16)

    @pl.loop(0, depth + 1)
    def _(step):
        @pl.when((step > 0) & (step < depth))
        def _():
            gather.step(step)

        @pl.loop(0, 4)
        def _(q):
            turn, down = q // 2, q % 2
            far = step - turn
            zz = z + (1 - 2 * down) * far
            yy = y * (1 - turn) + (1 - y) * turn
            valid = (far >= 0) & (far < depth) & (zz >= 0) & (zz < depth) & (far + 1 - down > 0)

            @pl.when(valid)
            def _():
                @pl.when(step == 0)
                def _():
                    gather.local.wait()

                @pl.when(turn == 1)
                def _():
                    gather.other(zz)

                process(zz * 2 + yy)

    store = pltpu.make_async_copy(normed, normed_out, store_sem)
    store.start()
    attend_forward_kernel(
        heads, slot_ref, place_ref, qkv_ref, mixed_ref, out_t_ref, total_ref,
        q_pos, k_pos, v_pos, q_t, v_t, scores, o_pos,
    )
    mixing.forward()
    grads.forward()
    mixing.finish()
    grads.finish()
    for copy in expands:
        copy.wait()
    gather.sent()
    store.wait()


def forward_stage(
    slot_of, place_of, tokens, w_attend, norms, w_expand, w_mixing, incoming, hidden, heads, sizes
):
    fsdp, n = sizes
    rows, width = tokens.shape
    length, lanes = n * rows, heads * HD
    own = w_mixing.shape[0]
    if sizes != (4, 8):
        columns = lax.all_to_all(
            w_expand.reshape(own, fsdp, hidden).transpose(1, 0, 2),
            "fsdp",
            split_axis=0,
            concat_axis=0,
            tiled=True,
        ).reshape(fsdp * own, hidden)
        everything = lax.all_gather(tokens, "ctx", axis=0, tiled=True)
        attend_here = lax.dynamic_slice_in_dim(
            w_attend.reshape(own, 3, width), lax.axis_index("ctx") * lanes, lanes, 2
        ).reshape(own, 3 * lanes)
        weights = lax.all_gather(attend_here, "fsdp", axis=0, tiled=True)
        gains = lax.all_gather(norms, "fsdp", axis=1, tiled=True)
        normed = (norm_parts(everything.astype(F32))[0] * gains[0] + gains[1]).astype(BF16)
        qkv = dot(normed, weights).astype(BF16)
        mixed, out_t, total = attend_forward(slot_of, place_of, qkv, heads)
        return (
            mixed,
            out_t,
            total,
            qkv,
            gains,
            normed,
            columns,
            lax.all_gather(w_mixing, "fsdp", axis=0, tiled=True),
            lax.all_gather(incoming, "fsdp", axis=0, tiled=True),
        )
    vmem, anywhere = pl.BlockSpec(memory_space=pltpu.VMEM), pl.BlockSpec(memory_space=pl.ANY)
    smem = pl.BlockSpec(memory_space=pltpu.SMEM)
    count = 3 * (2 * 2 + 1) + 6
    mixed, out_t, total, qkv, gains, normed, columns, mixing, grads = pl.pallas_call(
        functools.partial(forward_kernel, heads),
        out_shape=(
            jax.ShapeDtypeStruct((length, lanes), BF16),
            jax.ShapeDtypeStruct((lanes, length), F32),
            jax.ShapeDtypeStruct((8, length), F32),
            jax.ShapeDtypeStruct((length, 3 * lanes), BF16),
            jax.ShapeDtypeStruct((fsdp, 8, own), F32),
            jax.ShapeDtypeStruct((n, rows, width), BF16),
            jax.ShapeDtypeStruct((fsdp * own, hidden), BF16),
            jax.ShapeDtypeStruct((fsdp, own, width), BF16),
            jax.ShapeDtypeStruct((fsdp, rows, width), BF16),
        ),
        in_specs=[smem, smem, anywhere, anywhere, vmem] + [anywhere] * 3,
        out_specs=(vmem,) * 5 + (anywhere,) * 4,
        scratch_shapes=attend_forward_scratch(length, heads)
        + [
            pltpu.VMEM((n, rows, width), BF16),
            pltpu.VMEM((own, 3 * lanes), BF16),
            pltpu.VMEM((fsdp, own, 3 * lanes), BF16),
            pltpu.VMEM((n, rows, width), BF16),
            pltpu.SemaphoreType.DMA((3,)),
            pltpu.SemaphoreType.DMA,
            pltpu.SemaphoreType.DMA((4,)),
            pltpu.SemaphoreType.DMA((count,)),
            pltpu.SemaphoreType.DMA((count,)),
        ]
        + CtxGather.semaphores(n),
        compiler_params=pltpu.CompilerParams(
            collective_id=0, has_side_effects=True, vmem_limit_bytes=VMEM_LIMIT
        ),
    )(slot_of, place_of, tokens, w_attend, norms, w_expand, w_mixing, incoming)
    return (
        mixed,
        out_t,
        total,
        qkv,
        gains.transpose(1, 0, 2).reshape(8, width),
        normed.reshape(length, width),
        columns,
        mixing.reshape(width, width),
        grads.reshape(fsdp * rows, width),
    )


def attend_backward_kernel(
    heads, between, slot_ref, place_ref, qkv_ref, load_grad, out_t_ref, total_ref, result_ref,
    q_pos, k_pos, v_pos, g_pos, k_heads, v_heads, q_t, k_t, g_t, delta,
    dq_t, dk_acc, dv_acc, d_pos,
):
    length, lanes = q_pos.shape
    blocks = slot_ref.shape[0]
    size = length // blocks
    tiles = length // TILE
    scale = 1.0 / math.sqrt(HD)
    factor = LOG2E * scale
    for p in range(blocks):
        rows = qkv_ref[pl.ds(slot_ref[p] * size, size), :]
        here = slice(p * size, (p + 1) * size)
        q_pos[here, :] = rows[:, :lanes]
        k_pos[here, :] = rows[:, lanes : 2 * lanes]
        v_pos[here, :] = rows[:, 2 * lanes :]
    head_of_lane = lax.broadcasted_iota(jnp.int32, (TILE, lanes), 1) // HD
    allowed = lax.broadcasted_iota(jnp.int32, (TILE, TILE), 0) <= lax.broadcasted_iota(
        jnp.int32, (TILE, TILE), 1
    )
    for t in range(tiles):
        here = slice(t * TILE, (t + 1) * TILE)
        q_t[:, here] = q_pos[here, :].T
        k_t[:, here] = k_pos[here, :].T
        keys, values = k_pos[here, :], v_pos[here, :]
        for h in range(heads):
            k_heads[h, here, :] = jnp.where(head_of_lane == h, keys, jnp.zeros_like(keys))
            v_heads[h, here, :] = jnp.where(head_of_lane == h, values, jnp.zeros_like(values))
    dq_t[...] = jnp.zeros_like(dq_t)
    load = load_grad()
    for p in range(blocks):
        g_pos[p * size : (p + 1) * size, :] = load(slot_ref[p] * size, size)
    for t in range(tiles):
        here = slice(t * TILE, (t + 1) * TILE)
        g_tile = g_pos[here, :].T
        g_t[:, here] = g_tile
        product = g_tile.astype(F32) * out_t_ref[:, here]
        for h in range(heads):
            delta[h : h + 1, here] = jnp.sum(product[head_rows(h)], axis=0, keepdims=True)

    def pair(j, i, masked):
        there = pl.ds(pl.multiple_of(j * TILE, TILE), TILE)
        here = pl.ds(pl.multiple_of(i * TILE, TILE), TILE)
        for h in range(heads):
            raw = dot(k_heads[h, there, :], q_t[:, here])
            probs = jnp.exp2(raw * factor - total_ref[pl.ds(h, 1), here])
            if masked:
                probs = jnp.where(allowed, probs, 0.0)
            d_probs = dot(v_heads[h, there, :], g_t[:, here])
            d_scores = (probs * (d_probs - delta[pl.ds(h, 1), here])).astype(BF16)
            dv = dot(probs.astype(BF16), g_pos[here, :])
            dk = dot(d_scores, q_pos[here, :])
            if masked:
                dv_acc[h], dk_acc[h] = dv, dk
            else:
                dv_acc[h] += dv
                dk_acc[h] += dk
            dq_t[head_rows(h), here] += dot(k_t[head_rows(h), there], d_scores)

    @pl.loop(0, tiles)
    def _(j):
        pair(j, j, True)

        @pl.loop(j + 1, tiles)
        def _(i):
            pair(j, i, False)

        there = pl.ds(pl.multiple_of(j * TILE, TILE), TILE)
        for index, acc, weight in ((1, dk_acc, scale), (2, dv_acc, 1.0)):
            value = acc[0]
            for h in range(1, heads):
                value = jnp.where(head_of_lane == h, acc[h], value)
            d_pos[there, index * lanes : (index + 1) * lanes] = (value * weight).astype(BF16)
        between(j)

    for t in range(tiles):
        here = slice(t * TILE, (t + 1) * TILE)
        d_pos[here, :lanes] = (dq_t[:, here].T * scale).astype(BF16)
    for s in range(blocks):
        result_ref[s * size : (s + 1) * size, :] = d_pos[pl.ds(place_ref[s] * size, size), :]


def attend_backward_scratch(length, heads):
    lanes = heads * HD
    rows = pltpu.VMEM((length, lanes), BF16)
    columns = pltpu.VMEM((lanes, length), BF16)
    by_head = pltpu.VMEM((heads, length, lanes), BF16)
    return (
        [rows] * 4
        + [by_head] * 2
        + [columns] * 3
        + [
            pltpu.VMEM((8, length), F32),
            pltpu.VMEM((lanes, length), F32),
            pltpu.VMEM((heads, TILE, lanes), F32),
            pltpu.VMEM((heads, TILE, lanes), F32),
            pltpu.VMEM((length, 3 * lanes), BF16),
        ]
    )


ATTEND_SCRATCH = 14


def local_backward_kernel(
    heads, slot_ref, place_ref, qkv_ref, grad_ref, out_t_ref, total_ref, result_ref, *scratch
):
    attend_backward_kernel(
        heads, lambda j: None, slot_ref, place_ref, qkv_ref,
        lambda: lambda at, size: grad_ref[pl.ds(at, size), :],
        out_t_ref, total_ref, result_ref, *scratch,
    )


def attend_backward(slot_of, place_of, qkv, grad, out_t, total, heads):
    length = qkv.shape[0]
    lanes = heads * HD
    vmem = pl.BlockSpec(memory_space=pltpu.VMEM)
    smem = pl.BlockSpec(memory_space=pltpu.SMEM)
    return pl.pallas_call(
        functools.partial(local_backward_kernel, heads),
        out_shape=jax.ShapeDtypeStruct((length, 3 * lanes), BF16),
        in_specs=[smem, smem, vmem, vmem, vmem, vmem],
        out_specs=vmem,
        scratch_shapes=attend_backward_scratch(length, heads),
    )(slot_of, place_of, qkv, grad, out_t, total)


def backward_kernel(
    n, heads, slot_ref, place_ref, qkv_ref, out_t_ref, total_ref,
    mixed_ref, mixing_ref, out_ref, shrink_ref, expand_ref, normed_ref, weight_ref,
    joint_ref, own_mixing_ref, branch_ref, piece_ref, own_attend_ref, whole_ref, *rest,
):
    scratch, rest = rest[:ATTEND_SCRATCH], rest[ATTEND_SCRATCH:]
    (
        result, grad_in, normed, part_attend,
        near_a, far_out_a, far_in_a, near_b, far_out_b, far_in_b, near_c, far_out_c, far_in_c,
        pair_in, pair_sum, line_in, load_sem, local_sems, send_sems, recv_sems,
        pair_send, pair_recv, line_send, line_recv,
    ) = rest
    f, c, x, k, mate, across = fsdp_partners()
    depth = n // 2
    z, y = c // 2, c % 2
    lanes = heads * HD
    half = shrink_ref.shape[1]
    fsdp, _, small, hidden = expand_ref.shape
    length, width = normed.shape
    rows = length // n
    own = width // fsdp
    load = pltpu.make_async_copy(normed_ref, normed, load_sem)
    load.start()
    greet_ctx(n, [(mate, c), (across, c)])
    pieces = Pieces(send_sems, recv_sems)
    to_heads = CtxExchange(
        pieces, n, lambda j: [column_block(mixed_ref, j, lanes)], lambda j: [grad_in.at[j]],
        [local_sems.at[0]],
    )
    to_rows = CtxExchange(
        pieces,
        n,
        lambda j: [
            result.at[pl.ds(pl.multiple_of(j * rows, 128), rows), part * lanes : (part + 1) * lanes]
            for part in range(3)
        ],
        lambda j: [column_block(joint_ref, part * n + j, lanes) for part in range(3)],
        [local_sems.at[1 + part] for part in range(3)],
    )
    mixing = FsdpScatter(pieces, mixing_ref, near_a, far_out_a, far_in_a)
    branch = FsdpScatter(pieces, out_ref, near_b, far_out_b, far_in_b)
    attend = FsdpScatter(pieces, part_attend, near_c, far_out_c, far_in_c, 2)
    weights = FsdpGather(pieces, weight_ref, whole_ref, local_sems.at[4])
    to_heads.start()

    side = z // 2
    inner = z * (1 - side) + (depth - 1 - z) * side

    def owner(t):
        place = depth - 1 - t + inner * (t // 2) * (2 * (t % 2) - 1)
        return place * (1 - 2 * side) + (depth - 1) * side

    def pair_copies(t):
        to = owner(t) * 2 + 1 - y
        there = (f, z * 2 + 1 - y)
        return [
            remote(
                shrink_ref.at[to], pair_in.at[t, pl.ds(0, half)],
                pair_send.at[t, 0], pair_recv.at[t, 0], there,
            )
        ] + [
            remote(
                expand_ref.at[j, to], pair_in.at[t, pl.ds(half + j * small, small)],
                pair_send.at[t, 1 + j], pair_recv.at[t, 1 + j], there,
            )
            for j in range(fsdp)
        ]

    def pair_wait(t):
        for copy in pair_copies(t):
            copy.wait_recv()

    def pair_total(t, store):
        to = owner(t) * 2 + y

        @pl.loop(0, half // small)
        def _(j):
            at = pl.ds(pl.multiple_of(j * small, small), small)
            store(at, shrink_ref[to, at].astype(F32) + pair_in[t, at].astype(F32))

        @pl.loop(0, fsdp)
        def _(j):
            at = pl.ds(pl.multiple_of(half + j * small, small), small)
            store(at, expand_ref[j, to].astype(F32) + pair_in[t, at].astype(F32))

    def line_copy(t):
        zz = owner(t)
        up = (zz + depth - z) // depth
        last = (1 - up) * ((depth - 1 - (z - 1 - zz)) // (depth - 1))
        slot = zz + (depth - zz) * last
        return remote(
            pair_sum.at[t], line_in.at[slot], line_send.at[t], line_recv.at[slot],
            (f, c + 4 * up - 2),
        )

    def line_wait(slot):
        remote(
            pair_sum.at[0], line_in.at[slot], line_send.at[0], line_recv.at[slot],
            (f, z * 2 + 1 - y),
        ).wait_recv()

    def pass_on(t):
        pair_wait(t)
        zz = owner(t)

        @pl.when(inner == 0)
        def _():
            def store(at, value):
                pair_sum[t, at] = value.astype(BF16)

            pair_total(t, store)

        @pl.when(inner > 0)
        def _():
            line_wait(zz)

            def store(at, value):
                pair_sum[t, at] = (value + line_in[zz, at].astype(F32)).astype(BF16)

            pair_total(t, store)

        line_copy(t).start()

    for t in range(depth):
        for copy in pair_copies(t):
            copy.start()
    mixing.start()
    branch.start()
    mixing.forward()
    branch.forward()
    weights.start()

    def load_grad():
        to_heads.finish()

        def load_rows(at, size):
            return grad_in[at // rows, pl.ds(at % rows, size), :]

        return load_rows

    def between(j):
        @pl.when(((j == 0) & (inner == 0)) | (j == 3))
        def _():
            pass_on(j // 3 * (1 - inner))

    attend_backward_kernel(
        heads, between, slot_ref, place_ref, qkv_ref, load_grad, out_t_ref, total_ref,
        result, *scratch,
    )
    to_rows.start()
    pass_on(2 - inner)
    pl.when(inner > 0)(lambda: pass_on(2))
    load.wait()

    @pl.loop(0, fsdp)
    def _(j):
        cols = pl.ds(pl.multiple_of(j * own, own), own)
        part_attend[j] = dot_first(normed[:, cols], result[...]).astype(BF16)

    attend.start()
    attend.forward()

    def store_mixing(p, value):
        own_mixing_ref[p] = value.astype(BF16)

    def store_branch(p, value):
        branch_ref[p] = value

    def store_attend(p, value):
        own_attend_ref[p] = value.astype(BF16)

    mixing.finish(store_mixing)
    branch.finish(store_branch)
    weights.forward()
    attend.finish(store_attend)
    pair_wait(depth - 1)
    pl.when(z > 0)(lambda: line_wait(z))
    pl.when(z < depth - 1)(lambda: line_wait(depth))

    def store_piece(terms):
        def store(at, value):
            for slot in terms:
                value += line_in[slot, at].astype(F32)
            piece_ref[at] = value.astype(BF16)

        pair_total(depth - 1, store)

    pl.when(z == 0)(lambda: store_piece([depth]))
    pl.when(z == depth - 1)(lambda: store_piece([z]))
    pl.when(inner > 0)(lambda: store_piece([z, depth]))
    for t in range(depth):
        for copy in pair_copies(t):
            copy.wait_send()
    for t in range(depth - 1):
        line_copy(t).wait_send()
    weights.finish()
    to_rows.finish()


def backward_exchange(
    slot_of, place_of, qkv, out_t, total, grad_mixed, grad_mixing, part_out,
    grad_shrink, grad_expand, normed, w_attend, heads, sizes,
):
    fsdp, n = sizes
    length = qkv.shape[0]
    rows, lanes = length // n, heads * HD
    width = grad_mixed.shape[1]
    own = width // fsdp
    hidden = grad_expand.shape[1]
    small = own // n
    if sizes != (4, 8):
        grad_heads = ctx_to_heads(grad_mixed, n).reshape(length, lanes)
        d_qkv = attend_backward(slot_of, place_of, qkv, grad_heads, out_t, total, heads)
        shrink = lax.psum_scatter(grad_shrink, "ctx", scatter_dimension=0, tiled=True)
        expand = lax.psum_scatter(
            grad_expand.reshape(fsdp, n, small, hidden)
            .transpose(1, 0, 2, 3)
            .reshape(n * fsdp * small, hidden),
            "ctx",
            scatter_dimension=0,
            tiled=True,
        )
        joint = (
            ctx_to_rows(d_qkv.reshape(n, rows, 3 * lanes))
            .reshape(rows, n, 3, lanes)
            .transpose(0, 2, 1, 3)
            .reshape(rows, 3 * width)
        )
        return (
            joint,
            lax.psum_scatter(grad_mixing, "fsdp", scatter_dimension=0, tiled=True),
            lax.psum_scatter(part_out, "fsdp", scatter_dimension=0, tiled=True).astype(F32),
            shrink,
            expand.reshape(fsdp, small, hidden),
            lax.psum_scatter(
                dot_first(normed, d_qkv).astype(BF16), "fsdp", scatter_dimension=0, tiled=True
            ),
            lax.all_gather(w_attend, "fsdp", axis=0, tiled=True),
        )
    half = hidden // n
    tall = half + fsdp * small
    depth = n // 2
    count = 4 * (n - 1) + 3 * (2 * CHUNKS + 1) + 5
    vmem, anywhere = pl.BlockSpec(memory_space=pltpu.VMEM), pl.BlockSpec(memory_space=pl.ANY)
    smem = pl.BlockSpec(memory_space=pltpu.SMEM)
    joint, own_mixing, branch, piece, own_attend, whole_attend = pl.pallas_call(
        functools.partial(backward_kernel, n, heads),
        out_shape=(
            jax.ShapeDtypeStruct((rows, 3 * width), BF16),
            jax.ShapeDtypeStruct((own, width), BF16),
            jax.ShapeDtypeStruct((rows, width), F32),
            jax.ShapeDtypeStruct((tall, width), BF16),
            jax.ShapeDtypeStruct((own, 3 * lanes), BF16),
            jax.ShapeDtypeStruct((fsdp,) + w_attend.shape, BF16),
        ),
        in_specs=[smem, smem] + [vmem] * 8 + [anywhere] * 2,
        out_specs=(anywhere, vmem, vmem, vmem, vmem, anywhere),
        scratch_shapes=attend_backward_scratch(length, heads)
        + [
            pltpu.VMEM((length, 3 * lanes), BF16),
            pltpu.VMEM((n, rows, lanes), BF16),
            pltpu.VMEM((length, width), BF16),
            pltpu.VMEM((fsdp, own, 3 * lanes), BF16),
        ]
        + scatter_buffers(own, width)
        + scatter_buffers(rows, width)
        + scatter_buffers(own, 3 * lanes)
        + [
            pltpu.VMEM((depth, tall, width), BF16),
            pltpu.VMEM((depth - 1, tall, width), BF16),
            pltpu.VMEM((depth + 1, tall, width), BF16),
            pltpu.SemaphoreType.DMA,
            pltpu.SemaphoreType.DMA((5,)),
            pltpu.SemaphoreType.DMA((count,)),
            pltpu.SemaphoreType.DMA((count,)),
            pltpu.SemaphoreType.DMA((depth, 1 + fsdp)),
            pltpu.SemaphoreType.DMA((depth, 1 + fsdp)),
            pltpu.SemaphoreType.DMA((depth - 1,)),
            pltpu.SemaphoreType.DMA((depth + 1,)),
        ],
        compiler_params=pltpu.CompilerParams(
            collective_id=6, has_side_effects=True, vmem_limit_bytes=VMEM_LIMIT
        ),
    )(
        slot_of,
        place_of,
        qkv,
        out_t,
        total,
        grad_mixed,
        grad_mixing.reshape(fsdp, own, width),
        part_out.reshape(fsdp, rows, width),
        grad_shrink.reshape(n, half, width),
        grad_expand.reshape(fsdp, n, small, hidden),
        normed,
        w_attend,
    )
    return (
        joint,
        own_mixing,
        branch,
        piece[:half],
        piece[half:].reshape(fsdp, small, width),
        own_attend,
        whole_attend.reshape(width, 3 * width),
    )


def dot_last(left, right):
    return lax.dot_general(left, right, (((1,), (1,)), ((), ())), preferred_element_type=F32)


def dot_first(left, right):
    return lax.dot_general(left, right, (((0,), (0,)), ((), ())), preferred_element_type=F32)


def middle_kernel(
    n, heads_ref, start_ref, norms_ref, mixing_ref, expand_ref, shrink_ref, grads_ref,
    middle_ref, grad_middle_ref, grad_mixed_ref, sums_ref,
    grad_mixing_ref, part_out_ref, grad_shrink_ref, grad_expand_ref,
    w_mixing, w_expand, w_shrink, grads, mixed, normal, inverse, own_two, normed,
    activated, grad_expanded, part_two, part_out, grad_mixing, grad_shrink, grad_expand,
    branch, near_buf, far_out, far_in,
    load_sems, store_sems, local_sems, send_sems, recv_sems,
):
    f, c, x, k, mate, across = fsdp_partners()
    rows, width = start_ref.shape
    lanes = heads_ref.shape[-1]
    hidden = w_expand.shape[1]
    everything = normed.shape[0] * rows
    loads = [
        pltpu.make_async_copy(src, dst, load_sems.at[j])
        for j, (src, dst) in enumerate(
            (
                (mixing_ref, w_mixing),
                (expand_ref, w_expand),
                (shrink_ref, w_shrink),
                (grads_ref, grads),
            )
        )
    ]
    stores = [
        pltpu.make_async_copy(src, dst, store_sems.at[j])
        for j, (src, dst) in enumerate(
            (
                (part_out, part_out_ref),
                (grad_shrink, grad_shrink_ref),
                (grad_expand, grad_expand_ref),
                (grad_mixing, grad_mixing_ref),
            )
        )
    ]
    for copy in loads:
        copy.start()
    greet_ctx(n, [(mate, c), (across, c)])
    pieces = Pieces(send_sems, recv_sems)
    to_rows = CtxExchange(
        pieces, n, lambda j: [heads_ref.at[j]], lambda j: [column_block(mixed, j, lanes)],
        [local_sems.at[0]],
    )
    gather = FsdpGather(pieces, own_two, normed, local_sems.at[1])
    scatter = FsdpScatter(pieces, part_two, near_buf, far_out, far_in)
    to_rows.start()
    loads[0].wait()
    to_rows.finish()

    gain, shift = norms_ref[2:3, :], norms_ref[3:4, :]
    middle_ref[...] = start_ref[...].astype(F32) + dot(mixed[...], w_mixing[...])

    @pl.loop(0, rows // 64)
    def _(t):
        part = pl.ds(pl.multiple_of(t * 64, 64), 64)
        one, scale = norm_parts(middle_ref[part])
        normal[part] = one
        inverse[part] = jnp.broadcast_to(scale, (64, 128))
        own_two[part] = (one * gain + shift).astype(BF16)

    gather.start()
    for copy in loads[1:]:
        copy.wait()

    @pl.loop(0, 4)
    def _(t):
        b = (x + t // 2) % 2 * 2 + (k + t) % 2

        @pl.when(t == 0)
        def _():
            gather.local.wait()

        @pl.when(t == 1)
        def _():
            gather.near.wait_recv()

        @pl.when(t == 2)
        def _():
            gather.forward()

        @pl.when(t == 3)
        def _():
            for copy in gather.passed:
                copy.wait_recv()

        @pl.loop(0, hidden // TILE)
        def _(j):
            cols = pl.ds(pl.multiple_of(j * TILE, TILE), TILE)
            value, slope = gelu_and_slope(dot(normed[b], w_expand[:, cols]))
            grad = dot_last(grads[b], w_shrink[cols, :]).astype(BF16).astype(F32)
            activated[b, :, cols] = value.astype(BF16)
            grad_expanded[b, :, cols] = (grad * slope).astype(BF16)

        @pl.loop(0, width // TILE)
        def _(j):
            cols = pl.ds(pl.multiple_of(j * TILE, TILE), TILE)
            part_two[b, :, cols] = dot_last(grad_expanded[b], w_expand[cols, :]).astype(BF16)

    scatter.start()
    scatter.forward()

    @pl.loop(0, 4)
    def _(b):
        @pl.loop(0, width // TILE)
        def _(j):
            cols = pl.ds(pl.multiple_of(j * TILE, TILE), TILE)
            part_out[b, :, cols] = dot(activated[b], w_shrink[:, cols]).astype(BF16)

    stores[0].start()

    @pl.loop(0, hidden // TILE)
    def _(j):
        cols = pl.ds(pl.multiple_of(j * TILE, TILE), TILE)
        grad_shrink[cols, :] = dot_first(
            activated[:, :, cols].reshape(everything, TILE), grads[...].reshape(everything, width)
        ).astype(BF16)

    stores[1].start()

    @pl.loop(0, width // TILE)
    def _(j):
        cols = pl.ds(pl.multiple_of(j * TILE, TILE), TILE)
        grad_expand[cols, :] = dot_first(
            normed[:, :, cols].reshape(everything, TILE),
            grad_expanded[...].reshape(everything, hidden),
        ).astype(BF16)

    stores[2].start()
    sums_ref[...] = jnp.zeros_like(sums_ref)

    def store(p, err):
        one = normal[p]
        sums_ref[2:3, :] += jnp.sum(err * one, axis=0, keepdims=True)
        sums_ref[3:4, :] += jnp.sum(err, axis=0, keepdims=True)
        total = grads[f, p].astype(F32) + norm_back(err, gain, one, inverse[p, :1])
        grad_middle_ref[p] = total
        branch[p] = total.astype(BF16)

    scatter.finish(store)
    grad_mixed_ref[...] = dot_last(branch[...], w_mixing[...]).astype(BF16)

    @pl.loop(0, width // TILE)
    def _(j):
        cols = pl.ds(pl.multiple_of(j * TILE, TILE), TILE)
        grad_mixing[cols, :] = dot_first(mixed[:, cols], branch[...]).astype(BF16)

    stores[3].start()
    gather.near.wait_send()
    for copy, onward in zip(gather.far, gather.passed):
        copy.wait_send()
        onward.wait_send()
    for copy in stores:
        copy.wait()


def middle_stage(mixed_heads, start, norms, whole_mixing, expand_columns, w_shrink, grads_in, sizes):
    fsdp, n = sizes
    rows, width = start.shape
    lanes = width // n
    hidden = w_shrink.shape[0]
    if sizes != (4, 8):
        mixed = ctx_to_rows(mixed_heads.reshape(n, rows, lanes))
        middle = start.astype(F32) + dot(mixed, whole_mixing)
        normal, inverse = norm_parts(middle)
        own_two = (normal * norms[2] + norms[3]).astype(BF16)
        normed = lax.all_gather(own_two, "fsdp", axis=0, tiled=True)
        activated, slope = gelu_and_slope(dot(normed, expand_columns))
        activated = activated.astype(BF16)
        grad = dot_last(grads_in, w_shrink).astype(BF16).astype(F32)
        grad_expanded = (grad * slope).astype(BF16)
        part_two = dot_last(grad_expanded, expand_columns).astype(BF16)
        err = lax.psum_scatter(part_two, "fsdp", scatter_dimension=0, tiled=True).astype(F32)
        f = lax.axis_index("fsdp")
        incoming = lax.dynamic_slice_in_dim(grads_in, f * rows, rows, 0)
        grad_middle = incoming.astype(F32) + norm_back(err, norms[2], normal, inverse)
        branch = grad_middle.astype(BF16)
        zero = jnp.zeros((width,), F32)
        sums = jnp.stack(
            [zero, zero, jnp.sum(err * normal, axis=0), jnp.sum(err, axis=0)] + [zero] * 4
        )
        return (
            middle,
            grad_middle,
            dot_last(branch, whole_mixing).astype(BF16),
            sums,
            dot_first(mixed, branch).astype(BF16),
            dot(activated, w_shrink).astype(BF16),
            dot_first(activated, grads_in).astype(BF16),
            dot_first(normed, grad_expanded).astype(BF16),
        )
    vmem, anywhere = pl.BlockSpec(memory_space=pltpu.VMEM), pl.BlockSpec(memory_space=pl.ANY)
    count = n - 1 + 2 * (2 * CHUNKS + 1)
    blocks = pltpu.VMEM((fsdp, rows, width), BF16)
    hidden_blocks = pltpu.VMEM((fsdp, rows, hidden), BF16)
    result = pl.pallas_call(
        functools.partial(middle_kernel, n),
        out_shape=(
            jax.ShapeDtypeStruct((rows, width), F32),
            jax.ShapeDtypeStruct((rows, width), F32),
            jax.ShapeDtypeStruct((rows, width), BF16),
            jax.ShapeDtypeStruct((8, width), F32),
            jax.ShapeDtypeStruct((width, width), BF16),
            jax.ShapeDtypeStruct((fsdp, rows, width), BF16),
            jax.ShapeDtypeStruct((hidden, width), BF16),
            jax.ShapeDtypeStruct((width, hidden), BF16),
        ),
        in_specs=[vmem] * 3 + [anywhere] * 4,
        out_specs=(vmem,) * 4 + (anywhere,) * 4,
        scratch_shapes=[
            pltpu.VMEM((width, width), BF16),
            pltpu.VMEM((width, hidden), BF16),
            pltpu.VMEM((hidden, width), BF16),
            blocks,
            pltpu.VMEM((rows, width), BF16),
            pltpu.VMEM((rows, width), F32),
            pltpu.VMEM((rows, 128), F32),
            pltpu.VMEM((rows, width), BF16),
            blocks,
            hidden_blocks,
            hidden_blocks,
            blocks,
            blocks,
            pltpu.VMEM((width, width), BF16),
            pltpu.VMEM((hidden, width), BF16),
            pltpu.VMEM((width, hidden), BF16),
            pltpu.VMEM((rows, width), BF16),
        ]
        + scatter_buffers(rows, width)
        + [
            pltpu.SemaphoreType.DMA((4,)),
            pltpu.SemaphoreType.DMA((4,)),
            pltpu.SemaphoreType.DMA((2,)),
            pltpu.SemaphoreType.DMA((count,)),
            pltpu.SemaphoreType.DMA((count,)),
        ],
        compiler_params=pltpu.CompilerParams(
            collective_id=4, has_side_effects=True, vmem_limit_bytes=VMEM_LIMIT
        ),
    )(
        mixed_heads.reshape(n, rows, lanes),
        start,
        norms,
        whole_mixing,
        expand_columns,
        w_shrink,
        grads_in.reshape(fsdp, rows, width),
    )
    middle, grad_middle, grad_mixed, sums, grad_mixing, part_out, grad_shrink, grad_expand = result
    return (
        middle,
        grad_middle,
        grad_mixed,
        sums,
        grad_mixing,
        part_out.reshape(fsdp * rows, width),
        grad_shrink,
        grad_expand,
    )


def shards(
    sizes,
    tokens,
    out_grad,
    slot_block,
    w_attend,
    w_mixing,
    w_expand,
    w_shrink,
    w_norms,
    first_attend,
    first_mixing,
    first_expand,
    first_shrink,
    first_norms,
    second_attend,
    second_mixing,
    second_expand,
    second_shrink,
    second_norms,
):
    fsdp, ctx = sizes
    f, c = lax.axis_index("fsdp"), lax.axis_index("ctx")
    rows, width = tokens.shape[1:]
    heads = width // HD // ctx
    lanes = heads * HD
    length = rows * ctx
    own = width // fsdp
    hidden = w_shrink.shape[0]

    place_of = slot_block[0]
    slot_of = jnp.sum(
        jnp.where(
            place_of[None, :] == jnp.arange(2 * ctx, dtype=jnp.int32)[:, None],
            jnp.arange(2 * ctx, dtype=jnp.int32)[None, :],
            0,
        ),
        axis=1,
    )

    start = tokens[0]
    incoming = out_grad[0]
    padded_norms = jnp.concatenate([w_norms.astype(F32), jnp.zeros((4, own), F32)], axis=0)
    mixed_heads, out_t, total, qkv, norms, normed_all, expand_columns, whole_mixing, grads_in = (
        forward_stage(
            slot_of, place_of, start, w_attend, padded_norms, w_expand, w_mixing, incoming,
            hidden, heads, sizes,
        )
    )
    (
        middle,
        grad_middle,
        grad_mixed,
        norm_sums,
        grad_mixing,
        part_out,
        grad_shrink,
        grad_expand,
    ) = middle_stage(
        mixed_heads, start, norms, whole_mixing, expand_columns, w_shrink, grads_in, sizes
    )
    joint, own_mixing, branch, shrink_piece, expand_piece, own_attend, whole_attend = (
        backward_exchange(
            slot_of, place_of, qkv, out_t, total, grad_mixed, grad_mixing, part_out,
            grad_shrink, grad_expand, normed_all, w_attend, heads, sizes,
        )
    )
    layer_out = (middle + branch).astype(BF16)
    sum_attend, sum_mixing, parts_norms, sum_shrink, sum_expand, back = last_exchange(
        own_attend, own_mixing, norm_sums, shrink_piece, expand_piece, joint, whole_attend,
        start, norms, sizes,
    )
    tokens_grad = (grad_middle + back)[None]
    sum_attend, sum_mixing = sum_attend.astype(F32), sum_mixing.astype(F32)
    sum_shrink, sum_expand = sum_shrink.astype(F32), sum_expand.astype(F32)
    sum_norms = jnp.sum(parts_norms, axis=0)[:4]

    result = [layer_out[None], tokens_grad]
    for weight, grad, first, second in (
        (w_attend, sum_attend, first_attend, second_attend),
        (w_mixing, sum_mixing, first_mixing, second_mixing),
        (w_expand, sum_expand, first_expand, second_expand),
        (w_shrink, sum_shrink, first_shrink, second_shrink),
        (w_norms, sum_norms, first_norms, second_norms),
    ):
        result.append(grad)
        result.extend(adam_step(weight, grad, first, second))
    return tuple(result)


def solution(mesh):
    rows = P("fsdp", None)
    columns = P(None, "fsdp")
    tokens = P("fsdp", "ctx", None)
    return jax.shard_map(
        functools.partial(shards, (mesh.shape["fsdp"], mesh.shape["ctx"])),
        mesh=mesh,
        in_specs=(tokens, tokens, rows)
        + (rows, rows, rows, rows, columns) * 3,
        out_specs=(tokens, tokens) + (rows,) * 16 + (columns,) * 4,
        check_vma=False,
    )
```

time: 474 us -> 374 us (0.79); the launches traced: 468 us -> 374 us
  matrix products: 49.8 us -> 0 us
  other arithmetic: 50.9 us -> 33.7 us
  between operations: 14.4 us -> 0.87 us
  local copies, waits for them, and re-layouts: 10.1 us -> 3.9 us
  Pallas kernels: 341 us -> 336 us
    dot_general x12 -> x0, matrix products: 49.8 us -> none  [the longest x4 16.7 us: dot(): return jnp.dot(left, right, preferred_element_type=F32)]
    pallas_call x1, Pallas kernels: 109 us -> 90.5 us  [backward_exchange(): pl.pallas_call(functools.partial(backward_kernel, n, heads), out_shape=(j...]
    pallas_call x1, Pallas kernels: 92.9 us -> 107 us  [last_exchange(): pl.pallas_call(functools.partial(last_kernel, n), out_shape=(jax.ShapeDty...]
    reduce_sum x6 -> x0, other arithmetic: 7.65 us -> none  [the longest x2 3.98 us: norm_parts(): center = values - jnp.mean(values, axis=-1, keepdims=True)]
    convert_element_type x3 -> x0, other arithmetic: 7.64 us -> none  [the longest x2 6.59 us: shards(): (norm_parts(whole_tokens.astype(F32))[0] * norms[0] + norms[1]).astype(BF16)]
    pallas_call x5 -> x2, Pallas kernels: 139 us -> 138 us  [the longest x1 79.9 us: forward_stage(): pl.pallas_call(functools.partial(forward_kernel, heads), out_shape=(jax.S...]
  transfers between devices with their start and end apart: 3 -> 0, of which waited for: 0 -> 0; matrix products, arithmetic and copies ran while one was open for 13% -> 0% of each run, Pallas kernels for 17% -> 0%
where the time goes in v3:
time: 374 us
  Pallas kernels  336 us (90%)
  other arithmetic  33.7 us (9%)
  local copies, waits for them, and re-layouts  3.9 us (1%)
    pallas_call x1, Pallas kernels, last_exchange(): pl.pallas_call(functools.partial(last_kernel, n), out_shape=(jax.ShapeDty...  107 us
    pallas_call x1, Pallas kernels, backward_exchange(): pl.pallas_call(functools.partial(backward_kernel, n, heads), out_shape=(j...  90.5 us
    pallas_call x1, Pallas kernels, forward_stage(): pl.pallas_call(functools.partial(forward_kernel, heads), out_shape=(jax.S...  79.9 us
    pallas_call x1, Pallas kernels, middle_stage(): pl.pallas_call(functools.partial(middle_kernel, n), out_shape=(jax.ShapeD...  57.8 us
    mul x5, other arithmetic, adam_step(): -LEARN  29.6 us

profile of v3, /device:TPU:0, one launch (start us, length us, event | category | flops | bytes accessed | tf_op | source)
XLA Modules:
  0.0 374.1 jit_solution(17873967253964397738)
XLA Ops:
  0.7 1.3 select_reduce_fusion.slot_ref
  1.9 1.3 concatenate.3.norms_ref
  3.2 79.9 %shard_map.345 = (bf16[2048,128]{1,0:T(8,128)(2,1)}, f32[128,2048]{1,0:T(8,128)}, f32[8,2048]{1,0:T(8,128)}, bf16[2048,384]{1,0:T(8,128)(2,1)}, f32[4,8,256]{2,1...) custom-call(s32[16]{0:T(128)} %select_reduce_fusion.slot_ref, ...), custom_call_target="tpu_custom_call" | custom-call | tf_op jit(solution)/shard_map/pallas_call | solution.py:870
  83.1 57.8 %shard_map.346 = (f32[256,1024]{1,0:T(8,128)}, f32[256,1024]{1,0:T(8,128)}, bf16[256,1024]{1,0:T(8,128)(2,1)}, f32[8,1024]{1,0:T(8,128)}, bf16[1024,1024]{1,0:T(...) custom-call(bf16[8,256,128]{2,1,0:T(8,128)(2,1)} %bitcast.37, ...), custom_call_target="tpu_custom_call" | custom-call | tf_op jit(solution)/shard_map/pallas_call | solution.py:1555
  140.9 90.5 %shard_map.347 = (bf16[256,3072]{1,0:T(8,128)(2,1)}, bf16[256,1024]{1,0:T(8,128)(2,1)}, f32[256,1024]{1,0:T(8,128)}, bf16[256,1024]{1,0:T(8,128)(2,1)}, bf16[256...) custom-call(s32[16]{0:T(128)} %select_reduce_fusion.slot_ref, s32[16]{0:T(128)} %bitcast.42, ...), custom_call_target="tpu_custom_call" | custom-call | tf_op jit(solution)/shard_map/pallas_call | solution.py:1289
  231.4 1.9 fusion.11
  233.2 0.0 copy-start.12
  233.2 0.0 copy-start.13
  233.2 0.0 copy-start.14
  233.2 107.5 %shard_map.348 = (bf16[256,3072]{1,0:T(8,128)(2,1)}, bf16[256,1024]{1,0:T(8,128)(2,1)}, f32[8,8,256]{2,1,0:T(8,128)}, bf16[8,128,1024]{2,1,0:T(8,128)(2,1)}, bf1...) custom-call(bf16[256,384]{1,0:T(8,128)(2,1)} %get-tuple-element.68.attend_ref, ...), custom_call_target="tpu_custom_call" | custom-call | tf_op jit(solution)/shard_map/pallas_call | solution.py:547
  340.7 0.0 copy-start.15
  340.7 0.0 copy-start.16
  340.7 0.0 copy-start.17
  340.7 0.0 copy-start.18
  340.7 0.0 copy-start.9
  340.8 0.0 copy-start.11
  340.8 0.0 copy-done.12
  340.8 0.0 copy-done.13
  340.8 0.0 copy-done.14
  340.8 2.8 add_bitcast_fusion
  343.6 0.0 copy-start
  343.6 0.0 copy-done.15
  343.6 0.0 copy-done.16
  343.7 0.0 copy-done.17
  343.7 0.0 copy-done.18
  343.7 0.0 copy-start.7
  343.7 0.0 copy-start.10
  343.7 0.6 add_multiply_fusion.4
  344.3 0.0 copy-done.9
  344.3 0.0 copy-done.11
  344.3 4.0 %add_multiply_fusion.3 = (f32[256,1024]{1,0:T(8,128)}, f32[256,1024]{1,0:T(8,128)}, f32[256,1024]{1,0:T(8,128)}, f32[256,1024]{1,0:T(8,128)}) fusion(bf16[256,1024]{1,0:T(8,128)(2,1)S(1)} %copy-done.9, f32[256,1024]{1,0:T(8,128)S(1)} %copy-done.11, f32[256,1024]{1,0:T(8,128)} %param.32, bf16[256,1024]{1,0:T(8,128)(2,1)} %get-tuple-element.76), kind=kLoop, calls=%fused_computation.16 | loop fusion | flops 4194304 | bytes 7340032 | tf_op jit(solution)/shard_map/mul | solution.py:64
  348.4 0.0 copy-done
  348.4 0.0 copy-done.7
  348.4 0.0 copy-done.10
  348.4 0.0 copy-start.1
  348.4 0.0 copy-start.3
  348.4 0.0 copy-start.4
  348.4 8.2 %add_multiply_fusion.2 = (f32[256,3072]{1,0:T(8,128)}, f32[256,3072]{1,0:T(8,128)}, f32[256,3072]{1,0:T(8,128)}, f32[256,3072]{1,0:T(8,128)}) fusion(bf16[256,3072]{1,0:T(8,128)(2,1)S(1)} %copy-done, f32[256,3072]{1,0:T(8,128)S(1)} %copy-done.7, f32[256,3072]{1,0:T(8,128)} %param.31, bf16[256,3072]{1,0:T(8,128)(2,1)S(1)} %copy-done.10), kind=kLoop, calls=%fused_computation.10 | loop fusion | flops 12582912 | bytes 22020096 | tf_op jit(solution)/shard_map/mul | solution.py:64
  356.6 0.0 copy-done.1
  356.6 0.0 copy-done.3
  356.6 0.7 copy-done.4
  357.3 0.0 copy-start.2
  357.3 9.8 %add_multiply_fusion.1 = (f32[256,4096]{1,0:T(8,128)}, f32[256,4096]{1,0:T(8,128)}, f32[256,4096]{1,0:T(8,128)}, f32[256,4096]{1,0:T(8,128)}) fusion(bf16[256,4096]{1,0:T(8,128)(2,1)S(1)} %copy-done.1, f32[256,4096]{1,0:T(8,128)S(1)} %copy-done.3, f32[256,4096]{1,0:T(8,128)S(1)} %copy-done.4, bf16[8,32,4096]{2,1,0:T(8,128)(2,1)} %get-tuple-element.77), kind=kLoop, calls=%fused_computation.7 | loop fusion | flops 16777216 | bytes 29360128 | tf_op jit(solution)/shard_map/mul | solution.py:64
  367.2 0.0 copy-done.2
  367.2 0.0 copy-done.5
  367.2 0.0 copy-done.6
  367.2 0.0 copy-done.8
  367.2 6.9 %add_multiply_fusion = (f32[1024,1024]{1,0:T(8,128)}, f32[1024,1024]{1,0:T(8,128)}, f32[1024,1024]{1,0:T(8,128)}, f32[1024,1024]{1,0:T(8,128)}) fusion(bf16[1024,1024]{1,0:T(8,128)(2,1)S(1)} %copy-done.2, f32[1024,1024]{1,0:T(8,128)S(1)} %copy-done.5, f32[1024,1024]{1,0:T(8,128)S(1)} %copy-done.6, bf16[8,128,1024]{2,1,0:T(8,128)(2,1)S(1)} %copy-done.8), kind=kLoop, calls=%fused_computation.5 | loop fusion | flops 16777216 | bytes 29360128 | tf_op jit(solution)/shard_map/mul | solution.py:64
  (4 shorter events, 0.0 us)
Async XLA Ops:
  233.2 107.6 %copy-start.12 = (f32[256,1024]{1,0:T(8,128)S(1)}, f32[256,1024]{1,0:T(8,128)}, u32[]{:S(2)}) copy-start(f32[256,1024]{1,0:T(8,128)} %get-tuple-element.56) | copy-start | bytes 3145732
  233.2 107.6 %copy-start.13 = (f32[256,1024]{1,0:T(8,128)S(1)}, f32[256,1024]{1,0:T(8,128)}, u32[]{:S(2)}) copy-start(f32[256,1024]{1,0:T(8,128)} %get-tuple-element.67) | copy-start | bytes 3145732
  233.2 107.6 %copy-start.14 = (f32[256,1024]{1,0:T(8,128)S(1)}, f32[256,1024]{1,0:T(8,128)}, u32[]{:S(2)}) copy-start(f32[256,1024]{1,0:T(8,128)} %get-tuple-element.66) | copy-start | bytes 3145732
  340.7 2.9 copy-start.15
  340.7 2.9 copy-start.16
  340.7 2.9 copy-start.17
  340.7 2.9 copy-start.18
  340.7 3.6 copy-start.9
  340.8 3.6 copy-start.11
  343.6 4.7 %copy-start = (bf16[256,3072]{1,0:T(8,128)(2,1)S(1)}, bf16[256,3072]{1,0:T(8,128)(2,1)}, u32[]{:S(2)}) copy-start(bf16[256,3072]{1,0:T(8,128)(2,1)} %weight_ref.1) | copy-start | bytes 4718596
  343.7 4.7 %copy-start.7 = (f32[256,3072]{1,0:T(8,128)S(1)}, f32[256,3072]{1,0:T(8,128)}, u32[]{:S(2)}) copy-start(f32[256,3072]{1,0:T(8,128)} %param.26) | copy-start | bytes 9437188
  343.7 4.7 %copy-start.10 = (bf16[256,3072]{1,0:T(8,128)(2,1)S(1)}, bf16[256,3072]{1,0:T(8,128)(2,1)}, u32[]{:S(2)}) copy-start(bf16[256,3072]{1,0:T(8,128)(2,1)} %get-tuple-element.75) | copy-start | bytes 4718596
  348.4 8.3 %copy-start.1 = (bf16[256,4096]{1,0:T(8,128)(2,1)S(1)}, bf16[256,4096]{1,0:T(8,128)(2,1)}, u32[]{:S(2)}) copy-start(bf16[256,4096]{1,0:T(8,128)(2,1)} %expand_ref.1) | copy-start | bytes 6291460
  348.4 8.3 %copy-start.3 = (f32[256,4096]{1,0:T(8,128)S(1)}, f32[256,4096]{1,0:T(8,128)}, u32[]{:S(2)}) copy-start(f32[256,4096]{1,0:T(8,128)} %param.28) | copy-start | bytes 12582916
  348.4 8.9 %copy-start.4 = (f32[256,4096]{1,0:T(8,128)S(1)}, f32[256,4096]{1,0:T(8,128)}, u32[]{:S(2)}) copy-start(f32[256,4096]{1,0:T(8,128)} %param.33) | copy-start | bytes 12582916
  357.3 9.8 %copy-start.2 = (bf16[1024,1024]{1,0:T(8,128)(2,1)S(1)}, bf16[1024,1024]{1,0:T(8,128)(2,1)}, u32[]{:S(2)}) copy-start(bf16[1024,1024]{1,0:T(8,128)(2,1)} %shrink_ref.1) | copy-start | bytes 6291460
  357.3 9.8 %copy-start.5 = (f32[1024,1024]{1,0:T(8,128)S(1)}, f32[1024,1024]{1,0:T(8,128)}, u32[]{:S(2)}) copy-start(f32[1024,1024]{1,0:T(8,128)} %param.29) | copy-start | bytes 12582916
  357.3 9.9 %copy-start.6 = (f32[1024,1024]{1,0:T(8,128)S(1)}, f32[1024,1024]{1,0:T(8,128)}, u32[]{:S(2)}) copy-start(f32[1024,1024]{1,0:T(8,128)} %param.34) | copy-start | bytes 12582916
  357.3 9.9 %copy-start.8 = (bf16[8,128,1024]{2,1,0:T(8,128)(2,1)S(1)}, bf16[8,128,1024]{2,1,0:T(8,128)(2,1)}, u32[]{:S(2)}) copy-start(bf16[8,128,1024]{2,1,0:T(8,128)(2,1)} %get-tuple-element.78) | copy-start | bytes 6291460
